TPU v7x, 32 devices: a whole 2x2x4 slice. The times are simulated.
32 devices in a mesh: seq: 2 (over x), head: 4 (over z), pool: 4 (over y, core).
Axes of the slice: x: 2, y: 2, z: 4, core: 2. Of those that a mesh axis runs over, the one named last changes fastest.
Arguments:
- tokens: bfloat16 [32, 4096], P(('seq', 'head'), 'pool'), may hold values from -6 to 6
- routes: int32 [32, 8], P(('seq', 'head')), may hold values from 0 to 15, all different within a row; in each aligned block of 4 rows (0 to 3, 4 to 7, ...) at most 2 rows name the same one
- gate_fixed: int32 [32, 8], P(('seq', 'head')), may hold values from 1 to 65535
- gate_weight: bfloat16 [16, 4096, 3072], P('seq', 'pool', 'head'), may hold values from -0.09375 to 0.09375
- up_weight: bfloat16 [16, 4096, 3072], P('seq', 'pool', 'head'), may hold values from -0.09375 to 0.09375
- down_weight: bfloat16 [16, 3072, 4096], P('seq', 'head', 'pool'), may hold values from -0.109375 to 0.109375
- gate_scale: bfloat16 [16, 32, 24], P('seq', 'pool', 'head'), may hold values from 0.5 to 2
- up_scale: bfloat16 [16, 32, 24], P('seq', 'pool', 'head'), may hold values from 0.5 to 2
- down_scale: bfloat16 [16, 24, 32], P('seq', 'head', 'pool'), may hold values from 0.5 to 2
Outputs:
- combined: bfloat16 [32, 4096], P(('seq', 'head'), 'pool')
Inputs may be any that keep to these rules, and one draw needn't show every extreme that they name: `routes`: each row names 8 different experts. Within the rows of one device (aligned blocks of 4 rows) no expert is named by more than 2 rows, and in some blocks one expert is named by exactly 2 rows.
All inputs are finite; a program needn't handle non-finite values.
Results may differ from a plain program's by a relative error of at most 0.02.
Values may be sent and summed in bfloat16 or wider, within the bound.
No kernel may reach another device: no remote copies, remote signals or barrier semaphores. Data moves between devices by JAX's collectives and lax.ppermute only.
A program may use at most 128 MiB of HBM per device.

v0:
```python
import jax
import jax.numpy as jnp
from jax import lax
from jax.sharding import PartitionSpec as P

QB = 128
CAP = 2


largest_choice = lax.Precision.HIGHEST


def expand_scale(route_weight, scale):
    grown = jnp.repeat(jnp.repeat(scale, QB, axis=1), QB, axis=2)
    return route_weight * grown


def slot_positions(block_routes, expert_total):
    flattened = block_routes.reshape(-1)
    expert_ids = lax.broadcasted_iota(jnp.int32, (1, expert_total), 1)
    onehot = (flattened[:, None] == expert_ids).astype(jnp.int32)
    before = jnp.cumsum(onehot, axis=0) - onehot
    slot_index = jnp.sum(before * onehot, axis=1)
    return (flattened * CAP + slot_index).reshape(block_routes.shape)


def local_buffer(tokens, positions, slot_total):
    targets = lax.broadcasted_iota(jnp.int32, (slot_total, 1, 1), 0)
    selector = jnp.any(positions[None, :, :] == targets, axis=2).astype(jnp.bfloat16)
    return jnp.dot(selector, tokens, preferred_element_type=jnp.float32).astype(jnp.bfloat16)


def per_device(
    tokens,
    routes,
    gate_fixed,
    gate_weight,
    up_weight,
    down_weight,
    gate_scale,
    up_scale,
    down_scale,
):
    seq_count = lax.axis_size("seq")
    head_count = lax.axis_size("head")
    local_experts = gate_weight.shape[0]
    expert_total = local_experts * seq_count
    feature_width = tokens.shape[1]
    slot_total = expert_total * CAP
    block_total = seq_count * head_count
    gate_dense = expand_scale(gate_weight, gate_scale)
    up_dense = expand_scale(up_weight, up_scale)
    down_dense = expand_scale(down_weight, down_scale)
    positions = slot_positions(routes, expert_total)
    outgoing = local_buffer(tokens, positions, slot_total)
    outgoing = outgoing.reshape(seq_count, 1, local_experts, 1, CAP, feature_width)
    outgoing = jnp.broadcast_to(
        outgoing, (seq_count, head_count, local_experts, 1, CAP, feature_width)
    )
    outgoing = outgoing.reshape(block_total, local_experts, 1, CAP, feature_width)
    arrived = lax.all_to_all(outgoing, ("seq", "head"), split_axis=0, concat_axis=2, tiled=True)
    slot_rows = arrived.reshape(local_experts, seq_count, head_count, CAP, feature_width)
    gate_sum = jnp.einsum(
        "jshcd,jdf->jshcf", slot_rows, gate_dense, preferred_element_type=jnp.float32
    )
    up_sum = jnp.einsum("jshcd,jdf->jshcf", slot_rows, up_dense, preferred_element_type=jnp.float32)
    gate_sum, up_sum = (
        lax.psum(gate_sum.astype(jnp.bfloat16), "pool").astype(jnp.float32),
        lax.psum(up_sum.astype(jnp.bfloat16), "pool").astype(jnp.float32),
    )
    hidden = (jax.nn.silu(gate_sum) * up_sum).astype(jnp.bfloat16)
    partial_out = jnp.einsum(
        "jshcf,jfd->jshcd", hidden, down_dense, preferred_element_type=jnp.float32
    )
    sending = partial_out.astype(jnp.bfloat16).reshape(
        local_experts, block_total, CAP, feature_width
    )
    gathered_back = lax.all_to_all(
        sending, ("seq", "head"), split_axis=1, concat_axis=0, tiled=True
    )
    gathered_back = gathered_back.reshape(seq_count, head_count, local_experts, CAP, feature_width)
    results = jnp.sum(gathered_back.astype(jnp.float32), axis=1).astype(jnp.bfloat16)
    results = results.reshape(slot_total, feature_width)
    fixed = gate_fixed.astype(jnp.float32)
    weights = fixed / jnp.sum(fixed, axis=1, keepdims=True)
    slot_ids = lax.broadcasted_iota(jnp.int32, (1, 1, slot_total), 2)
    combine_weight = jnp.sum(
        jnp.where(positions[:, :, None] == slot_ids, weights[:, :, None], 0.0), axis=1
    )
    combined = jnp.dot(
        combine_weight,
        results.astype(jnp.float32),
        precision=largest_choice,
        preferred_element_type=jnp.float32,
    )
    return combined.astype(jnp.bfloat16)


def solution(mesh):
    return jax.shard_map(
        per_device,
        mesh=mesh,
        in_specs=(
            P(("seq", "head"), "pool"),
            P(("seq", "head"), None),
            P(("seq", "head"), None),
            P("seq", "pool", "head"),
            P("seq", "pool", "head"),
            P("seq", "head", "pool"),
            P("seq", "pool", "head"),
            P("seq", "pool", "head"),
            P("seq", "head", "pool"),
        ),
        out_specs=P(("seq", "head"), "pool"),
        check_vma=False,
    )
```

profile of v0, /device:TPU:0, one launch (start us, length us, event | category | flops | bytes accessed | tf_op | source)
XLA Modules:
  0.0 150.8 jit_solution(4185804847729853960)
XLA Ops:
  6.5 0.0 copy-start
  6.5 0.8 eq.20
  7.3 0.1 fusion.24
  7.4 0.1 reduce_window_sum.11
  7.4 0.2 select_reduce_fusion.1
  7.6 0.1 reduce_sum.42
  7.7 0.7 multiply_add_fusion
  8.4 0.1 fusion.25
  8.5 0.0 copy-done
  8.5 0.2 convolution_convert_fusion
  8.8 0.7 broadcast_in_dim.44
  9.5 7.3 %all-to-all-start = ((bf16[8,8,1,2,1024]{4,1,3,2,0:T(8,128)(2,1)}), bf16[8,8,1,2,1024]{4,1,3,2,0:T(8,128)(2,1)S(1)}, u32[]{:S(2)}, u32[]{:S(2)}) async-start(bf16[8,8,1,2,1024]{4,1,3,2,0:T(8,128)(2,1)} %bitcast), calls=%async_computation | async-start | bytes 524288 | tf_op jit(solution)/shard_map/all_to_all | solution.py:61
  16.8 0.0 copy-start.4
  16.8 0.0 all-reduce.3.cloned.1.call-start
  16.9 16.6 %copy.58 = bf16[8,1024,768]{1,2,0:T(8,128)(2,1)} copy(bf16[8,1024,768]{2,1,0:T(8,128)(2,1)} %param.12) | data formatting | bytes 25165824 | tf_op args[3]
  33.5 0.0 copy-done.4
  33.5 0.1 broadcast_in_dim.46
  33.7 0.1 copy.57
  33.7 0.0 copy-start.5
  33.8 16.6 %copy.62 = bf16[8,1024,768]{1,2,0:T(8,128)(2,1)} copy(bf16[8,1024,768]{2,1,0:T(8,128)(2,1)} %param.13) | data formatting | bytes 25165824 | tf_op args[4]
  50.4 0.0 copy-done.5
  50.4 0.1 broadcast_in_dim.48
  50.6 0.1 copy.61
  50.6 0.0 copy-start.3
  50.6 11.1 %bitcast_multiply_fusion.1 = bf16[8,1024,768]{1,2,0:T(8,128)(2,1)} fusion(bf16[8,1024,768]{1,2,0:T(8,128)(2,1)} %copy.58, bf16[8,1024,6]{1,2,0:T(8,128)(2,1)S(1)} %copy.57), kind=kLoop, calls=%fused_computation.7 | loop fusion | flops 6291456 | bytes 25264128 | tf_op jit(solution)/shard_map/mul | solution.py:15
  61.8 1.8 %copy-done.3 = bf16[8,1024,768]{1,2,0:T(8,128)(2,1)S(1)} copy-done((bf16[8,1024,768]{1,2,0:T(8,128)(2,1)S(1)}, bf16[8,1024,768]{1,2,0:T(8,128)(2,1)}, u32[]{:S(2)}) %copy-start.3) | copy-done | bytes 12582936
  63.5 5.2 %bitcast_multiply_fusion = bf16[8,1024,768]{1,2,0:T(8,128)(2,1)} fusion(bf16[8,1024,768]{1,2,0:T(8,128)(2,1)S(1)} %copy-done.3, bf16[8,1024,6]{1,2,0:T(8,128)(2,1)S(1)} %copy.61), kind=kLoop, calls=%fused_computation.6 | loop fusion | flops 6291456 | bytes 25264128 | tf_op jit(solution)/shard_map/mul | solution.py:15
  68.8 0.0 all-to-all-done
  68.8 0.0 copy-start.2
  68.8 0.0 copy-start.6
  68.8 8.9 %fusion.10 = bf16[8,2,4,2,768]{4,2,3,1,0:T(4,128)(2,1)} fusion(bf16[8,1024,768]{1,2,0:T(8,128)(2,1)} %bitcast_multiply_fusion.1, bf16[8,2,4,2,1024]{4,0,3,2,1:T(8,128)(2,1)S(1)} %bitcast.54), kind=kOutput, calls=%fused_computation.10 | convolution fusion | flops 201424896 | bytes 13041664 | tf_op jit(solution)/shard_map/jshcd,jdf->jshcf/dot_general | solution.py:63
  77.7 0.0 copy-done.2
  77.7 4.2 %fusion.13 = bf16[8,2,4,2,768]{4,2,3,1,0:T(4,128)(2,1)} fusion(bf16[8,1024,768]{1,2,0:T(8,128)(2,1)S(1)} %copy-done.2, bf16[8,2,4,2,1024]{4,0,3,2,1:T(8,128)(2,1)S(1)} %bitcast.55), kind=kOutput, calls=%fused_computation.11 | convolution fusion | flops 201424896 | bytes 13041664 | tf_op jit(solution)/shard_map/jshcd,jdf->jshcf/dot_general | solution.py:66
  81.9 0.0 all-reduce.3.cloned.1.call-update
  81.9 0.0 copy-done.6
  81.9 0.2 broadcast_in_dim.50
  82.1 8.9 %broadcast_in_dim.51 = bf16[8,768,8,128]{3,2,1,0:T(8,128)(2,1)} broadcast(bf16[8,768,8]{2,1,0:T(8,128)(2,1)S(1)} %bitcast.53), dimensions={0,1,2} | broadcast | bytes 12681216 | tf_op jit(solution)/shard_map/broadcast_in_dim | solution.py:14
  91.0 19.4 %reshape.62 = bf16[8,768,1024]{2,1,0:T(8,128)(2,1)} reshape(bf16[8,768,8,128]{3,2,1,0:T(8,128)(2,1)} %broadcast_in_dim.51) | data formatting | bytes 25165824 | tf_op jit(solution)/shard_map/reshape | solution.py:14
  110.4 6.0 %all-reduce.3.cloned.1.call-done = (bf16[8,2,4,2,768]{4,2,3,1,0:T(4,128)(2,1)}, bf16[8,2,4,2,768]{4,2,3,1,0:T(4,128)(2,1)}) async-done(((bf16[8,2,4,2,768]{4,2,3,1,0:T(4,128)(2,1)}, bf16[8,2,4,2,768]{4,2,3,1,0:T(4,128)(2,1)}), (bf16[8,2,4,2,768]{4,2,3,1,0:T(4,128)(2,1)}, bf16[8,2,4,2,768]{4,2,3,1,0:T(4,128)(2,1)})) %all-reduce.3.cloned.1.call-update) | async-done | bytes 393232 | tf_op jit(solution)/shard_map/psum | solution.py:69
  116.4 0.0 copy-start.1
  116.4 0.0 copy-start.7
  116.4 11.4 %fusion.7 = bf16[8,2,4,2,1024]{4,2,3,1,0:T(4,128)(2,1)S(1)} fusion(bf16[8,768,1024]{2,1,0:T(8,128)(2,1)} %param.14, bf16[8,768,1024]{2,1,0:T(8,128)(2,1)} %reshape.62, bf16[8,2,4,2,768]{4,2,3,1,0:T(4,128)(2,1)} %get-tuple-element.5, bf16[8,2,4,2,768]{4,2,3,1,0:T(4,128)(2,1)} %get-tuple-element.6), kind=kOutput, calls=%fused_computation.9 | convolution fusion | flops 208535552 | bytes 25821184 | tf_op jit(solution)/shard_map/jshcf,jfd->jshcd/dot_general | solution.py:72
  127.8 0.8 copy.66
  128.6 5.5 %all-to-all-start.1 = ((bf16[8,8,2,1024]{3,0,2,1:T(8,128)(2,1)}), bf16[8,8,2,1024]{3,0,2,1:T(8,128)(2,1)S(1)}, u32[]{:S(2)}, u32[]{:S(2)}) async-start(bf16[8,8,2,1024]{3,0,2,1:T(8,128)(2,1)} %bitcast.13), calls=%async_computation.1 | async-start | bytes 524288 | tf_op jit(solution)/shard_map/all_to_all | solution.py:78
  134.1 0.0 copy-done.7
  134.1 0.1 convert_reduce_fusion
  134.3 0.1 convert_divide_fusion
  134.3 0.1 select_reduce_fusion
  134.4 8.6 %all-to-all-done.1 = bf16[8,8,2,1024]{3,0,2,1:T(8,128)(2,1)S(1)} async-done(((bf16[8,8,2,1024]{3,0,2,1:T(8,128)(2,1)}), bf16[8,8,2,1024]{3,0,2,1:T(8,128)(2,1)S(1)}, u32[]{:S(2)}, u32[]{:S(2)}) %all-to-all-start.1) | async-done | bytes 262176 | tf_op jit(solution)/shard_map/all_to_all | solution.py:78
  143.1 0.1 copy.67
  143.2 0.8 convolution_convert_fusion.1
  143.9 0.0 copy-done.1
  (7 shorter events, 0.2 us)
Async XLA Ops:
  6.5 2.0 %copy-start = (bf16[4,1024]{1,0:T(4,128)(2,1)S(1)}, bf16[4,1024]{1,0:T(4,128)(2,1)}, u32[]{:S(2)}) copy-start(bf16[4,1024]{1,0:T(4,128)(2,1)} %param.9) | copy-start | bytes 24580
  9.5 59.3 %all-to-all-start = ((bf16[8,8,1,2,1024]{4,1,3,2,0:T(8,128)(2,1)}), bf16[8,8,1,2,1024]{4,1,3,2,0:T(8,128)(2,1)S(1)}, u32[]{:S(2)}, u32[]{:S(2)}) async-start(bf16[8,8,1,2,1024]{4,1,3,2,0:T(8,128)(2,1)} %bitcast), calls=%async_computation | async-start | bytes 524288 | tf_op jit(solution)/shard_map/all_to_all | solution.py:61
  16.8 16.7 %copy-start.4 = (bf16[8,8,6]{1,0,2:T(8,128)(2,1)S(1)}, bf16[8,8,6]{1,0,2:T(8,128)(2,1)}, u32[]{:S(2)}) copy-start(bf16[8,8,6]{1,0,2:T(8,128)(2,1)} %param.15) | copy-start | bytes 2308
  16.8 99.6 %all-reduce.3.cloned.1.call-start = ((), (), s32[]{:S(2)}) async-start(), calls=%async_computation.2 | async-start | bytes 786432 | tf_op jit(solution)/shard_map/psum | solution.py:69
  33.7 16.6 %copy-start.5 = (bf16[8,8,6]{1,0,2:T(8,128)(2,1)S(1)}, bf16[8,8,6]{1,0,2:T(8,128)(2,1)}, u32[]{:S(2)}) copy-start(bf16[8,8,6]{1,0,2:T(8,128)(2,1)} %param.16) | copy-start | bytes 2308
  50.6 12.9 %copy-start.3 = (bf16[8,1024,768]{1,2,0:T(8,128)(2,1)S(1)}, bf16[8,1024,768]{1,2,0:T(8,128)(2,1)}, u32[]{:S(2)}) copy-start(bf16[8,1024,768]{1,2,0:T(8,128)(2,1)} %copy.62) | copy-start | bytes 37748740
  68.8 8.9 %copy-start.2 = (bf16[8,1024,768]{1,2,0:T(8,128)(2,1)S(1)}, bf16[8,1024,768]{1,2,0:T(8,128)(2,1)}, u32[]{:S(2)}) copy-start(bf16[8,1024,768]{1,2,0:T(8,128)(2,1)} %bitcast_multiply_fusion) | copy-start | bytes 37748740
  68.8 13.1 %copy-start.6 = (bf16[8,6,8]{2,0,1:T(8,128)(2,1)S(1)}, bf16[8,6,8]{2,0,1:T(8,128)(2,1)}, u32[]{:S(2)}) copy-start(bf16[8,6,8]{2,0,1:T(8,128)(2,1)} %param.17) | copy-start | bytes 2308
  116.4 27.5 %copy-start.1 = (bf16[4,1024]{1,0:T(4,128)(2,1)S(1)}, bf16[4,1024]{1,0:T(4,128)(2,1)}, u32[]{:S(2)}) copy-start(bf16[4,1024]{1,0:T(4,128)(2,1)} %param.9) | copy-start | bytes 24580
  116.4 17.8 %copy-start.7 = (s32[4,8]{1,0:T(4,128)S(1)}, s32[4,8]{1,0:T(4,128)}, u32[]{:S(2)}) copy-start(s32[4,8]{1,0:T(4,128)} %param.11) | copy-start | bytes 388
  128.6 14.4 %all-to-all-start.1 = ((bf16[8,8,2,1024]{3,0,2,1:T(8,128)(2,1)}), bf16[8,8,2,1024]{3,0,2,1:T(8,128)(2,1)S(1)}, u32[]{:S(2)}, u32[]{:S(2)}) async-start(bf16[8,8,2,1024]{3,0,2,1:T(8,128)(2,1)} %bitcast.13), calls=%async_computation.1 | async-start | bytes 524288 | tf_op jit(solution)/shard_map/all_to_all | solution.py:78
Sparse Core Ops, SparseCore 0:
  82.0 34.2 all-reduce.2
where the time goes:
time: 152 us; the launch traced here: 151 us
  local copies, waits for them, and re-layouts  66.6 us (44%)
  matrix products  25.5 us (17%)
  other arithmetic  17.8 us (12%)
  waiting for transfers between devices  14.6 us (10%)
  between operations  13.5 us (9%)
  starting transfers between devices  12.8 us (8%)
    unnamed x19, local copies, waits for them, and re-layouts  35.1 us
    reshape x5, local copies, waits for them, and re-layouts, expand_scale(): grown = jnp.repeat(jnp.repeat(scale, QB, axis=1), QB, axis=2)  19.6 us
    mul x2, other arithmetic, expand_scale(): return route_weight * grown  16.4 us
    dot_general x1, matrix products, per_device(): jnp.einsum('jshcf,jfd->jshcd', hidden, down_dense, preferred_element_type...  11.4 us
    broadcast_in_dim x4, local copies, waits for them, and re-layouts, expand_scale(): grown = jnp.repeat(jnp.repeat(scale, QB, axis=1), QB, axis=2)  9.3 us
    dot_general x1, matrix products, per_device(): jnp.einsum('jshcd,jdf->jshcf', slot_rows, gate_dense, preferred_element_t...  8.89 us
    all_to_all x1, waiting for transfers between devices, per_device(): lax.all_to_all(sending, ('seq', 'head'), split_axis=1, concat_axis=0, til...  8.59 us
    all_to_all x1, starting transfers between devices, per_device(): lax.all_to_all(outgoing, ('seq', 'head'), split_axis=0, concat_axis=2, ti...  7.28 us
  transfers between devices with their start and end apart: 3, of which 2 were waited for; matrix products, arithmetic and copies ran while one was open for 52% of the time, Pallas kernels for 0%

commit v1 on v0

v1 whole, which is shorter than its diff:
```python
import functools

import jax
import jax.numpy as jnp
from jax import lax
from jax.experimental import pallas as pl
from jax.experimental.pallas import tpu as pltpu
from jax.sharding import PartitionSpec as P

QB = 128
CAP = 2
LANES = 128
BF = jnp.bfloat16
F32 = jnp.float32
I32 = jnp.int32

VM = pl.BlockSpec(memory_space=pltpu.VMEM)
SM = pl.BlockSpec(memory_space=pltpu.SMEM)
HB = pl.BlockSpec(memory_space=pltpu.HBM)


def sds(shape, dtype):
    return jax.ShapeDtypeStruct(shape, dtype)


def run(kernel, out_shape, in_specs, args, name, limit=2 << 20, flops=0, bytes_=0, **more):
    outs = out_shape if isinstance(out_shape, (list, tuple)) else [out_shape]
    specs = [VM] * len(outs)
    return pl.pallas_call(
        kernel,
        out_shape=out_shape,
        in_specs=in_specs,
        out_specs=specs if isinstance(out_shape, (list, tuple)) else VM,
        compiler_params=pltpu.CompilerParams(vmem_limit_bytes=limit),
        cost_estimate=pl.CostEstimate(flops=flops, bytes_accessed=bytes_, transcendentals=0),
        name=name,
        **more,
    )(*args)


def iota(shape, dim):
    return lax.broadcasted_iota(I32, shape, dim)


def placed(values, start):
    n = values.shape[1]
    spot = (iota((n, LANES), 1) == iota((n, LANES), 0) + start).astype(BF)
    return jnp.dot(values.astype(F32).astype(BF), spot, preferred_element_type=F32)


def pack(tokens, routes, gates, scales):
    rows, width = tokens.shape
    top = routes.shape[1]

    def kernel(t_in, r_in, g_in, *rest):
        s_in, (x_out, *s_out) = rest[:3], rest[3:7]
        t_v, r_v, g_v, *s_v = rest[7:13]
        sems = rest[13]
        copies = [
            pltpu.make_async_copy(src, dst, sems.at[i])
            for i, (src, dst) in enumerate(
                zip((r_in, g_in, t_in, *s_in), (r_v, g_v, t_v, *s_v))
            )
        ]
        for copy in copies:
            copy.start()
        for copy in copies:
            copy.wait()
        x_out[:, :width] = t_v[...]
        gate = g_v[...]
        meta = (
            placed(r_v[...], 0)
            + placed(lax.shift_right_logical(gate, 8), top)
            + placed(gate & 255, 2 * top)
        )
        x_out[:, width:] = meta.astype(BF)
        for src, dst in zip(s_v, s_out):
            dst[...] = src[...].astype(F32)

    arrays = (tokens, routes, gates, *scales)
    return run(
        kernel,
        [sds((rows, width + LANES), BF)] + [sds(s.shape, F32) for s in scales],
        [HB] * len(arrays),
        arrays,
        "pack",
        scratch_shapes=[pltpu.VMEM(a.shape, a.dtype) for a in arrays]
        + [pltpu.SemaphoreType.DMA((len(arrays),))],
    )


def cat(a, b):
    rows = a.shape[0]

    def kernel(a_ref, b_ref, o_ref):
        o_ref[:rows] = a_ref[...]
        o_ref[rows:] = b_ref[...]

    return run(kernel, sds((2 * rows,) + a.shape[1:], a.dtype), [VM] * 2, (a, b), "cat")


def dispatch(x, width, top, rows_dev, experts, slots):
    rows = x.shape[0]
    per = slots // experts
    meta = x[:, width:].astype(F32)
    base = (lax.axis_index("seq") * experts).astype(F32)
    lane = iota((rows, LANES), 1)
    named = jnp.where(lane < experts, lane, -LANES).astype(F32) + base
    hits = jnp.zeros((rows, LANES), F32)
    gates = jnp.zeros((rows, LANES), F32)
    total = jnp.zeros((rows, 1), F32)
    for k in range(top):
        gate = meta[:, top + k : top + k + 1] * 256.0 + meta[:, 2 * top + k : 2 * top + k + 1]
        equal = meta[:, k : k + 1] == named
        hits = hits + jnp.where(equal, 1.0, 0.0)
        gates = gates + jnp.where(equal, gate, 0.0)
        total = total + gate
    weights = gates / total
    r0, r1 = iota((rows, rows), 0), iota((rows, rows), 1)
    earlier = ((r0 // rows_dev == r1 // rows_dev) & (r1 < r0)).astype(BF)
    rank = jnp.dot(earlier, hits.astype(BF), preferred_element_type=F32)
    grow = (iota((LANES, slots), 1) // per == iota((LANES, slots), 0)).astype(BF)
    wide_hits = jnp.dot(hits.astype(BF), grow, preferred_element_type=F32)
    wide_rank = jnp.dot(rank.astype(BF), grow, preferred_element_type=F32)
    spot = (iota((rows, slots), 1) % per - (iota((rows, slots), 0) // rows_dev) * CAP).astype(F32)
    sel = jnp.where((wide_hits > 0.5) & (wide_rank == spot), 1.0, 0.0).astype(BF)
    slot_rows = lax.dot_general(
        sel, x[:, :width], (((0,), (0,)), ((), ())), preferred_element_type=F32
    ).astype(BF)
    return sel, weights, slot_rows


def scaled(w, scale, e, d, f, d_blk, f_blk):
    block = w[e, pl.ds(d, QB), pl.ds(f, QB)]
    return block * scale[e, d_blk, f_blk].astype(BF)


def half_products(xs_ref, gw, uw, gs, us, o_ref, half):
    experts, width, hidden = gw.shape
    n = hidden // 2 // QB
    per = xs_ref.shape[0] // experts
    columns = [(gw, gs, j) for j in range(n)] + [(uw, us, j) for j in range(n)]
    starts = [pl.multiple_of((half * n + j) * QB, QB) for j in range(n)]
    group, deep = (2 if n % 1 == 0 else 1), 2 * QB
    for e in range(experts):
        xs = xs_ref[e * per : (e + 1) * per, :]
        for at in range(0, len(columns), group):
            acc = jnp.zeros((per, group * QB), F32)
            for d in range(0, width, deep):
                rhs = jnp.concatenate(
                    [
                        jnp.concatenate(
                            [
                                scaled(w, s, e, d + q, starts[j], (d + q) // QB, half * n + j)
                                for w, s, j in columns[at : at + group]
                            ],
                            axis=1,
                        )
                        for q in range(0, deep, QB)
                    ],
                    axis=0,
                )
                acc = acc + jnp.dot(xs[:, d : d + deep], rhs, preferred_element_type=F32)
            o_ref[e * per : (e + 1) * per, at * QB : (at + group) * QB] = acc.astype(o_ref.dtype)


def other_half(x, gw, uw, gs, us, top, rows_dev, blocks):
    experts, width, hidden = gw.shape
    rows = x.shape[0]
    slots = experts * blocks * CAP

    def kernel(x_ref, gw_ref, uw_ref, gs_ref, us_ref, o_ref, xs_ref, sel_ref, wt_ref):
        sel, weights, slot_rows = dispatch(x_ref[...], width, top, rows_dev, experts, slots)
        sel_ref[...] = sel
        wt_ref[...] = weights
        xs_ref[...] = slot_rows
        half = 1 - lax.rem(lax.axis_index("pool"), 2)
        half_products(xs_ref, gw_ref, uw_ref, gs_ref, us_ref, o_ref, half)

    return run(
        kernel,
        [sds((slots, hidden), BF), sds((slots, width), BF), sds((rows, slots), BF), sds((rows, LANES), F32)],
        [VM] * 3 + [SM] * 2,
        (x, gw, uw, gs, us),
        "other_half",
        limit=8 << 20,
        flops=2 * slots * width * hidden,
        bytes_=2 * experts * width * hidden,
    )


def own_half(xs, gw, uw, gs, us):
    experts, width, hidden = gw.shape
    slots = xs.shape[0]

    def kernel(xs_ref, gw_ref, uw_ref, gs_ref, us_ref, o_ref):
        half = lax.rem(lax.axis_index("pool"), 2)
        half_products(xs_ref, gw_ref, uw_ref, gs_ref, us_ref, o_ref, half)

    return run(
        kernel,
        sds((slots, hidden), F32),
        [VM] * 3 + [SM] * 2,
        (xs, gw, uw, gs, us),
        "own_half",
        limit=8 << 20,
        flops=2 * slots * width * hidden,
        bytes_=2 * experts * width * hidden,
    )


def add_round(own, got):
    def kernel(a_ref, b_ref, o_ref, r_ref):
        total = a_ref[...] + b_ref[...].astype(F32)
        o_ref[...] = total
        r_ref[...] = total.astype(BF)

    return run(kernel, [sds(own.shape, F32), sds(own.shape, BF)], [VM] * 2, (own, got), "add_round")


def activate(own, got):
    slots, hidden = own.shape
    n = hidden // 2

    def kernel(a_ref, b_ref, o_ref):
        gate = a_ref[:, :n] + b_ref[:, :n].astype(F32)
        up = a_ref[:, n:] + b_ref[:, n:].astype(F32)
        o_ref[...] = (jax.nn.silu(gate) * up).astype(BF)

    return run(kernel, sds((slots, n), BF), [VM] * 2, (own, got), "activate")


def down_products(h_ref, sel_ref, wt_ref, dw, ds, half):
    experts, hidden, width = dw.shape
    rows, slots = sel_ref.shape
    per = slots // experts
    n = hidden // 2 // QB
    sel = sel_ref[...].astype(F32)
    owner = iota((rows, slots), 1) // per
    stack = jnp.concatenate([jnp.where(owner == e, sel, 0.0) for e in range(experts)], axis=0)
    spread = jnp.dot(stack.astype(BF), h_ref[...], preferred_element_type=F32)
    weights = wt_ref[...]
    pieces = []
    for e in range(experts):
        part = spread[e * rows : (e + 1) * rows] * weights[:, e : e + 1]
        part = part.astype(BF)
        pieces += [(e, j, part[:, j * QB : (j + 1) * QB]) for j in range(n)]
    starts = [pl.multiple_of((half * n + j) * QB, QB) for j in range(n)]
    deep = 2 if len(pieces) % 2 == 0 else 1
    group = 2
    outs = []
    for c in range(0, width // QB, group):
        acc = jnp.zeros((rows, group * QB), F32)
        for at in range(0, len(pieces), deep):
            use = pieces[at : at + deep]
            lhs = jnp.concatenate([p for _, _, p in use], axis=1)
            rhs = jnp.concatenate(
                [
                    jnp.concatenate(
                        [
                            scaled(dw, ds, e, starts[j], (c + q) * QB, half * n + j, c + q)
                            for q in range(group)
                        ],
                        axis=1,
                    )
                    for e, j, _ in use
                ],
                axis=0,
            )
            acc = acc + jnp.dot(lhs, rhs, preferred_element_type=F32)
        outs.append(acc)
    return outs


def down_own(hid, sel, wt, dw, ds):
    experts, hidden, width = dw.shape
    rows = sel.shape[0]

    def kernel(h_ref, sel_ref, wt_ref, dw_ref, ds_ref, o_ref):
        half = lax.rem(lax.axis_index("pool"), 2)
        for i, acc in enumerate(down_products(h_ref, sel_ref, wt_ref, dw_ref, ds_ref, half)):
            o_ref[:, i * 2 * QB : (i + 1) * 2 * QB] = acc

    return run(
        kernel,
        sds((rows, width), F32),
        [VM] * 4 + [SM],
        (hid, sel, wt, dw, ds),
        "down_own",
        limit=8 << 20,
        flops=experts * rows * width * hidden,
        bytes_=experts * width * hidden,
    )


def down_other(hid, sel, wt, dw, ds, own):
    experts, hidden, width = dw.shape
    rows = sel.shape[0]
    keep = rows // 2

    def kernel(h_ref, sel_ref, wt_ref, dw_ref, ds_ref, a_ref, o_ref, s_ref):
        half = 1 - lax.rem(lax.axis_index("pool"), 2)
        for i, acc in enumerate(down_products(h_ref, sel_ref, wt_ref, dw_ref, ds_ref, half)):
            at = slice(i * 2 * QB, (i + 1) * 2 * QB)
            total = acc + a_ref[:, at]
            o_ref[:, at] = total[:keep]
            s_ref[:, at] = total[keep:].astype(BF)

    return run(
        kernel,
        [sds((keep, width), F32), sds((rows - keep, width), BF)],
        [VM] * 4 + [SM, VM],
        (hid, sel, wt, dw, ds, own),
        "down_other",
        limit=8 << 20,
        flops=experts * rows * width * hidden,
        bytes_=experts * width * hidden,
    )


def fold(own, got):
    rows, width = own.shape
    keep = rows // 2

    def kernel(a_ref, b_ref, o_ref, s_ref):
        o_ref[...] = a_ref[:keep] + b_ref[:keep].astype(F32)
        s_ref[...] = (a_ref[keep:] + b_ref[keep:].astype(F32)).astype(BF)

    return run(
        kernel, [sds((keep, width), F32), sds((keep, width), BF)], [VM] * 2, (own, got), "fold"
    )


def finish(own, got):
    def kernel(a_ref, b_ref, o_ref):
        o_ref[...] = (a_ref[...] + b_ref[...].astype(F32)).astype(BF)

    return run(kernel, sds(own.shape, BF), [VM] * 2, (own, got), "finish")


def swap(x, axis, bit):
    return lax.ppermute(x, axis, [(j, j ^ bit) for j in range(lax.axis_size(axis))])


def bits(count):
    return [1 << i for i in range(count.bit_length() - 1)]


def per_device(tokens, routes, gate_fixed, gw, uw, dw, gs, us, ds):
    n_seq, n_head, n_pool = (lax.axis_size(a) for a in ("seq", "head", "pool"))
    rows_dev, width = tokens.shape
    top = routes.shape[1]
    hops = [("head", b) for b in reversed(bits(n_head))] + [("seq", b) for b in bits(n_seq)]

    gw, uw, dw = (pltpu.with_memory_space_constraint(w, pltpu.VMEM) for w in (gw, uw, dw))
    x, gs, us, ds = pack(tokens, routes, gate_fixed, (gs, us, ds))
    for axis, bit in hops:
        x = cat(x, swap(x, axis, bit))

    send, xs, sel, wt = other_half(x, gw, uw, gs, us, top, rows_dev, n_seq * n_head)
    got = swap(send, "pool", 1)
    own = own_half(xs, gw, uw, gs, us)
    for bit in bits(n_pool)[1:]:
        own, send = add_round(own, got)
        got = swap(send, "pool", bit)
    hid = activate(own, got)
    other = swap(hid, "pool", 1)
    acc = down_own(hid, sel, wt, dw, ds)
    acc, send = down_other(other, sel, wt, dw, ds, acc)
    for axis, bit in reversed(hops[1:]):
        acc, send = fold(acc, swap(send, axis, bit))
    axis, bit = hops[0]
    return finish(acc, swap(send, axis, bit))


def solution(mesh):
    return jax.shard_map(
        per_device,
        mesh=mesh,
        in_specs=(
            P(("seq", "head"), "pool"),
            P(("seq", "head"), None),
            P(("seq", "head"), None),
            P("seq", "pool", "head"),
            P("seq", "pool", "head"),
            P("seq", "head", "pool"),
            P("seq", "pool", "head"),
            P("seq", "pool", "head"),
            P("seq", "head", "pool"),
        ),
        out_specs=P(("seq", "head"), "pool"),
        check_vma=False,
    )
```

time: 152 us -> 63.4 us (0.42)
  local copies, waits for them, and re-layouts: 66.6 us -> 17.8 us
  matrix products: 25.5 us -> 0 us
  other arithmetic: 17.8 us -> 0.01 us
  between operations: 13.5 us -> 0.11 us
  Pallas kernels: 0 us -> 13.3 us
  starting transfers between devices: 12.8 us -> 16.7 us
    dot_general x5 -> x0, matrix products: 25.5 us -> none  [the longest x1 11.4 us: per_device(): jnp.einsum('jshcf,jfd->jshcd', hidden, down_dense, preferred_element_type...]
    reshape x6 -> x0, local copies, waits for them, and re-layouts: 19.6 us -> none  [the longest x5 19.6 us: expand_scale(): grown = jnp.repeat(jnp.repeat(scale, QB, axis=1), QB, axis=2)]
    unnamed x19 -> x25, local copies, waits for them, and re-layouts: 35.1 us -> 17.8 us
    ppermute x0 -> x9, starting transfers between devices: none -> 16.7 us  [swap(): lax.ppermute(x, axis, [(j, j ^ bit) for j in range(lax.axis_size(axis))])]
    mul x2 -> x0, other arithmetic: 16.4 us -> none  [expand_scale(): return route_weight * grown]
    ppermute x0 -> x9, waiting for transfers between devices: none -> 15 us  [swap(): lax.ppermute(x, axis, [(j, j ^ bit) for j in range(lax.axis_size(axis))])]
    pallas_call x0 -> x13, Pallas kernels: none -> 13.3 us  [run(): pl.pallas_call(kernel, out_shape=out_shape, in_specs=in_specs, out_specs=...]
    all_to_all x2 -> x0, starting transfers between devices: 12.8 us -> none  [the longest x1 7.28 us: per_device(): lax.all_to_all(outgoing, ('seq', 'head'), split_axis=0, concat_axis=2, ti...]
  transfers between devices with their start and end apart: 3 -> 9, of which waited for: 2 -> 7; matrix products, arithmetic and copies ran while one was open for 52% -> 0% of each run, Pallas kernels for 0% -> 9%
where the time goes in v1:
time: 63.4 us; the launch traced here: 62.9 us
  local copies, waits for them, and re-layouts  17.8 us (28%)
  starting transfers between devices  16.7 us (26%)
  waiting for transfers between devices  15 us (24%)
  Pallas kernels  13.3 us (21%)
    unnamed x25, local copies, waits for them, and re-layouts  17.8 us
    ppermute x9, starting transfers between devices, swap(): lax.ppermute(x, axis, [(j, j ^ bit) for j in range(lax.axis_size(axis))])  16.7 us
    ppermute x9, waiting for transfers between devices, swap(): lax.ppermute(x, axis, [(j, j ^ bit) for j in range(lax.axis_size(axis))])  15 us
    pallas_call x13, Pallas kernels, run(): pl.pallas_call(kernel, out_shape=out_shape, in_specs=in_specs, out_specs=...  13.3 us
  transfers between devices with their start and end apart: 9, of which 7 were waited for; matrix products, arithmetic and copies ran while one was open for 0% of the time, Pallas kernels for 9%

profile of v1, /device:TPU:0, one launch (start us, length us, event | category | flops | bytes accessed | tf_op | source)
XLA Modules:
  0.0 62.9 jit_solution(184636212303487677)
XLA Ops:
  0.0 0.8 %copy.10.rest_0_ = bf16[8,8,6]{2,1,0:T(8,128)(2,1)S(1)} copy(bf16[8,8,6]{1,0,2:T(8,128)(2,1)} %param.15) | data formatting | bytes 1536 | tf_op args[6]
  0.8 0.8 %copy.11.rest_1_ = bf16[8,8,6]{2,1,0:T(8,128)(2,1)S(1)} copy(bf16[8,8,6]{1,0,2:T(8,128)(2,1)} %param.16) | data formatting | bytes 1536 | tf_op args[7]
  1.7 0.7 %copy.12.rest_2_ = bf16[8,6,8]{2,1,0:T(8,128)(2,1)S(1)} copy(bf16[8,6,8]{2,0,1:T(8,128)(2,1)} %param.17) | data formatting | bytes 1536 | tf_op args[8]
  2.4 0.0 copy-start.5
  2.4 0.7 %copy-done.5 = bf16[4,1024]{1,0:T(4,128)(2,1)S(1)} copy-done((bf16[4,1024]{1,0:T(4,128)(2,1)S(1)}, bf16[4,1024]{1,0:T(4,128)(2,1)}, u32[]{:S(2)}) %copy-start.5) | copy-done | bytes 8216
  3.1 0.0 copy-start.6
  3.1 0.7 %copy-done.6 = s32[4,8]{1,0:T(4,128)S(1)} copy-done((s32[4,8]{1,0:T(4,128)S(1)}, s32[4,8]{1,0:T(4,128)}, u32[]{:S(2)}) %copy-start.6) | copy-done | bytes 152
  3.8 0.0 copy-start.7
  3.8 0.7 %copy-done.7 = s32[4,8]{1,0:T(4,128)S(1)} copy-done((s32[4,8]{1,0:T(4,128)S(1)}, s32[4,8]{1,0:T(4,128)}, u32[]{:S(2)}) %copy-start.7) | copy-done | bytes 152
  4.5 0.2 pack.1
  4.7 4.1 %collective-permute-start = (bf16[4,1152]{1,0:T(4,128)(2,1)S(1)}, bf16[4,1152]{1,0:T(4,128)(2,1)S(1)}, u32[]{:S(2)}, u32[]{:S(2)}) collective-permute-start(bf16[4,1152]{1,0:T(4,128)(2,1)S(1)} %get-tuple-element.21.a_ref), channel_id=1, source_target_pairs={{0,8},{4,12},{8,0},{12,4},{1,9},{5,13},{9,1},{13,5},{2,10},{6,14},... | collective-permute-start | bytes 27656 | tf_op jit(solution)/shard_map/ppermute | solution.py:342
  8.8 1.6 %collective-permute-done.b_ref = bf16[4,1152]{1,0:T(4,128)(2,1)S(1)} collective-permute-done((bf16[4,1152]{1,0:T(4,128)(2,1)S(1)}, bf16[4,1152]{1,0:T(4,128)(2,1)S(1)}, u32[]{:S(2)}, u32[]{:S(2)}) %collective-permute-start) | collective-permute-done | bytes 9248 | tf_op jit(solution)/shard_map/ppermute | solution.py:342
  10.5 1.9 %collective-permute-start.1 = (bf16[8,1152]{1,0:T(8,128)(2,1)S(1)}, bf16[8,1152]{1,0:T(8,128)(2,1)S(1)}, u32[]{:S(2)}, u32[]{:S(2)}) collective-permute-start(bf16[8,1152]{1,0:T(8,128)(2,1)S(1)} %cat.3.a_ref), channel_id=1, source_target_pairs={{0,4},{4,0},{8,12},{12,8},{1,5},{5,1},{9,13},{13,9},{2,6},{6,2},{1... | collective-permute-start | bytes 55304 | tf_op jit(solution)/shard_map/ppermute | solution.py:342
  12.4 1.9 %collective-permute-done.1.b_ref = bf16[8,1152]{1,0:T(8,128)(2,1)S(1)} collective-permute-done((bf16[8,1152]{1,0:T(8,128)(2,1)S(1)}, bf16[8,1152]{1,0:T(8,128)(2,1)S(1)}, u32[]{:S(2)}, u32[]{:S(2)}) %collective-permute-start.1) | collective-permute-done | bytes 18464 | tf_op jit(solution)/shard_map/ppermute | solution.py:342
  14.3 1.8 %collective-permute-start.2 = (bf16[16,1152]{1,0:T(8,128)(2,1)S(1)}, bf16[16,1152]{1,0:T(8,128)(2,1)S(1)}, u32[]{:S(2)}, u32[]{:S(2)}) collective-permute-start(bf16[16,1152]{1,0:T(8,128)(2,1)S(1)} %cat.4.a_ref), channel_id=1, source_target_pairs={{0,16},{16,0},{1,17},{17,1},{2,18},{18,2},{3,19},{19,3},{4,20},{20... | collective-permute-start | bytes 110600 | tf_op jit(solution)/shard_map/ppermute | solution.py:342
  16.1 2.1 %collective-permute-done.2.b_ref = bf16[16,1152]{1,0:T(8,128)(2,1)S(1)} collective-permute-done((bf16[16,1152]{1,0:T(8,128)(2,1)S(1)}, bf16[16,1152]{1,0:T(8,128)(2,1)S(1)}, u32[]{:S(2)}, u32[]{:S(2)}) %collective-permute-start.2) | collective-permute-done | bytes 36896 | tf_op jit(solution)/shard_map/ppermute | solution.py:342
  18.2 0.0 copy-start
  18.2 4.6 %copy-done = bf16[8,1024,768]{2,1,0:T(8,128)(2,1)S(1)} copy-done((bf16[8,1024,768]{2,1,0:T(8,128)(2,1)S(1)}, bf16[8,1024,768]{2,1,0:T(8,128)(2,1)}, u32[]{:S(2)}) %copy-start) | copy-done | bytes 12582936
  22.8 0.0 copy-start.2
  22.8 4.6 %copy-done.2 = bf16[8,1024,768]{2,1,0:T(8,128)(2,1)S(1)} copy-done((bf16[8,1024,768]{2,1,0:T(8,128)(2,1)S(1)}, bf16[8,1024,768]{2,1,0:T(8,128)(2,1)}, u32[]{:S(2)}) %copy-start.2) | copy-done | bytes 12582936
  27.4 0.0 copy-start.1
  27.4 0.0 copy-start.3
  27.4 4.0 %other_half.1 = (bf16[128,768]{1,0:T(8,128)(2,1)S(1)}, bf16[128,1024]{1,0:T(8,128)(2,1)S(1)}, bf16[32,128]{1,0:T(8,128)(2,1)S(1)}, f32[32,128]{1,0:T(8,128)S(1)}) custom-call(bf16[32,1152]{1,0:T(8,128)(2,1)S(1)} %cat.5.x_ref, bf16[8,1024,768]{2,1,0:T(8,128)(2,1)S(1)} %copy-done, bf16[8,1024,768]{2,1,0:T(8,128)(2,1)S(1)} %copy-done.2, ...), custom_call_target="tpu_custom_call" | custom-call | flops 201326592 | bytes 12582912 | tf_op jit(solution)/shard_map/other_half/pallas_call | solution.py:29
  31.3 0.0 collective-permute-start.3
  31.3 0.6 copy-done.1
  31.9 3.6 %copy-done.3 = bf16[8,1024,768]{2,1,0:T(8,128)(2,1)S(1)} copy-done((bf16[8,1024,768]{2,1,0:T(8,128)(2,1)S(1)}, bf16[8,1024,768]{2,1,0:T(8,128)(2,1)}, u32[]{:S(2)}) %copy-start.3) | copy-done | bytes 12582936
  35.5 0.0 copy-start.4
  35.5 0.0 slice-start
  35.5 0.0 slice-start.1
  35.5 3.5 %own_half.1.a_ref = f32[128,768]{1,0:T(8,128)S(1)} custom-call(bf16[128,1024]{1,0:T(8,128)(2,1)S(1)} %get-tuple-element.24.xs_ref, bf16[8,1024,768]{2,1,0:T(8,128)(2,1)S(1)} %copy-done.1, bf16[8,1024,768]{2,1,0:T(8,128)(2,1)S(1)} %copy-done.3, f32[8,8,6]{2,1,0:T(8,128)S(1)} %get-tuple-element.22.gs_ref, f32[8,8,6]{2,1,0:T(8,128)S(1)} %get-tuple-element.23.us_ref), custom_call_target="tpu_custom_call" | custom-call | flops 201326592 | bytes 12582912 | tf_op jit(solution)/shard_map/own_half/pallas_call | solution.py:29
  39.0 0.0 collective-permute-done.3.b_ref
  39.0 0.1 add_round.1
  39.1 1.9 %collective-permute-start.4 = (bf16[128,768]{1,0:T(8,128)(2,1)S(1)}, bf16[128,768]{1,0:T(8,128)(2,1)S(1)}, u32[]{:S(2)}, u32[]{:S(2)}) collective-permute-start(bf16[128,768]{1,0:T(8,128)(2,1)S(1)} %get-tuple-element.27), channel_id=1, source_target_pairs={{0,2},{1,3},{2,0},{3,1},{4,6},{5,7},{6,4},{7,5},{8,10},{9,11},{10,... | collective-permute-start | bytes 589832 | tf_op jit(solution)/shard_map/ppermute | solution.py:342
  41.0 3.8 %collective-permute-done.4.b_ref = bf16[128,768]{1,0:T(8,128)(2,1)S(1)} collective-permute-done((bf16[128,768]{1,0:T(8,128)(2,1)S(1)}, bf16[128,768]{1,0:T(8,128)(2,1)S(1)}, u32[]{:S(2)}, u32[]{:S(2)}) %collective-permute-start.4) | collective-permute-done | bytes 196640 | tf_op jit(solution)/shard_map/ppermute | solution.py:342
  44.8 0.0 slice-start.2
  44.8 0.1 activate.1.h_ref
  44.9 0.1 collective-permute-start.5
  45.0 0.0 copy-done.4
  45.0 2.4 %down_own.1.a_ref = f32[32,1024]{1,0:T(8,128)S(1)} custom-call(bf16[128,384]{1,0:T(8,128)(2,1)S(1)} %activate.1.h_ref, bf16[32,128]{1,0:T(8,128)(2,1)S(1)} %get-tuple-element.28.sel_ref, f32[32,128]{1,0:T(8,128)S(1)} %get-tuple-element.29.wt_ref, bf16[8,768,1024]{2,1,0:T(8,128)(2,1)S(1)} %copy-done.4, f32[8,6,8]{2,1,0:T(8,128)S(1)} %get-tuple-element.30.ds_ref), custom_call_target="tpu_custom_call" | custom-call | flops 201326592 | bytes 6291456 | tf_op jit(solution)/shard_map/down_own/pallas_call | solution.py:29
  47.4 0.0 collective-permute-done.5.h_ref
  47.4 0.0 slice-done
  47.4 0.0 slice-done.1
  47.4 0.0 slice-done.2
  47.5 2.4 %down_other.1 = (f32[16,1024]{1,0:T(8,128)S(1)}, bf16[16,1024]{1,0:T(8,128)(2,1)S(1)}) custom-call(bf16[128,384]{1,0:T(8,128)(2,1)S(1)} %collective-permute-done.5.h_ref, bf16[32,128]{1,0:T(8,128)(2,1)S(1)} %get-tuple-element.28.sel_ref, f32[32,128]{1,0:T(8,128)S(1)} %get-tuple-element.29.wt_ref, bf16[8,768,1024]{2,1,0:T(8,128)(2,1)S(1)} %bitcast.1, ...), custom_call_target="tpu_custom_call" | custom-call | flops 201326592 | bytes 6291456 | tf_op jit(solution)/shard_map/down_other/pallas_call | solution.py:29
  49.9 1.9 %collective-permute-start.6 = (bf16[16,1024]{1,0:T(8,128)(2,1)S(1)}, bf16[16,1024]{1,0:T(8,128)(2,1)S(1)}, u32[]{:S(2)}, u32[]{:S(2)}) collective-permute-start(bf16[16,1024]{1,0:T(8,128)(2,1)S(1)} %get-tuple-element.32), channel_id=1, source_target_pairs={{0,16},{16,0},{1,17},{17,1},{2,18},{18,2},{3,19},{19,3},{4,20},{20... | collective-permute-start | bytes 98312 | tf_op jit(solution)/shard_map/ppermute | solution.py:342
  51.7 2.1 %collective-permute-done.6.b_ref = bf16[16,1024]{1,0:T(8,128)(2,1)S(1)} collective-permute-done((bf16[16,1024]{1,0:T(8,128)(2,1)S(1)}, bf16[16,1024]{1,0:T(8,128)(2,1)S(1)}, u32[]{:S(2)}, u32[]{:S(2)}) %collective-permute-start.6) | collective-permute-done | bytes 32800 | tf_op jit(solution)/shard_map/ppermute | solution.py:342
  53.9 2.0 %collective-permute-start.7 = (bf16[8,1024]{1,0:T(8,128)(2,1)S(1)}, bf16[8,1024]{1,0:T(8,128)(2,1)S(1)}, u32[]{:S(2)}, u32[]{:S(2)}) collective-permute-start(bf16[8,1024]{1,0:T(8,128)(2,1)S(1)} %get-tuple-element.34), channel_id=1, source_target_pairs={{0,4},{4,0},{8,12},{12,8},{1,5},{5,1},{9,13},{13,9},{2,6},{6,2},{1... | collective-permute-start | bytes 49160 | tf_op jit(solution)/shard_map/ppermute | solution.py:342
  55.8 1.8 %collective-permute-done.7.b_ref = bf16[8,1024]{1,0:T(8,128)(2,1)S(1)} collective-permute-done((bf16[8,1024]{1,0:T(8,128)(2,1)S(1)}, bf16[8,1024]{1,0:T(8,128)(2,1)S(1)}, u32[]{:S(2)}, u32[]{:S(2)}) %collective-permute-start.7) | collective-permute-done | bytes 16416 | tf_op jit(solution)/shard_map/ppermute | solution.py:342
  57.7 3.0 %collective-permute-start.8 = (bf16[4,1024]{1,0:T(4,128)(2,1)S(1)}, bf16[4,1024]{1,0:T(4,128)(2,1)S(1)}, u32[]{:S(2)}, u32[]{:S(2)}) collective-permute-start(bf16[4,1024]{1,0:T(4,128)(2,1)S(1)} %get-tuple-element.36), channel_id=1, source_target_pairs={{0,8},{4,12},{8,0},{12,4},{1,9},{5,13},{9,1},{13,5},{2,10},{6,14},... | collective-permute-start | bytes 24584 | tf_op jit(solution)/shard_map/ppermute | solution.py:342
  60.7 1.6 %collective-permute-done.8.b_ref = bf16[4,1024]{1,0:T(4,128)(2,1)S(1)} collective-permute-done((bf16[4,1024]{1,0:T(4,128)(2,1)S(1)}, bf16[4,1024]{1,0:T(4,128)(2,1)S(1)}, u32[]{:S(2)}, u32[]{:S(2)}) %collective-permute-start.8) | collective-permute-done | bytes 8224 | tf_op jit(solution)/shard_map/ppermute | solution.py:342
  62.3 0.6 finish.1
  (6 shorter events, 0.0 us)
Async XLA Ops:
  2.4 0.7 %copy-start.5 = (bf16[4,1024]{1,0:T(4,128)(2,1)S(1)}, bf16[4,1024]{1,0:T(4,128)(2,1)}, u32[]{:S(2)}) copy-start(bf16[4,1024]{1,0:T(4,128)(2,1)} %t_in.1) | copy-start | bytes 24580
  3.1 0.7 %copy-start.6 = (s32[4,8]{1,0:T(4,128)S(1)}, s32[4,8]{1,0:T(4,128)}, u32[]{:S(2)}) copy-start(s32[4,8]{1,0:T(4,128)} %r_in.1) | copy-start | bytes 388
  3.8 0.7 %copy-start.7 = (s32[4,8]{1,0:T(4,128)S(1)}, s32[4,8]{1,0:T(4,128)}, u32[]{:S(2)}) copy-start(s32[4,8]{1,0:T(4,128)} %g_in.1) | copy-start | bytes 388
  4.7 5.8 %collective-permute-start = (bf16[4,1152]{1,0:T(4,128)(2,1)S(1)}, bf16[4,1152]{1,0:T(4,128)(2,1)S(1)}, u32[]{:S(2)}, u32[]{:S(2)}) collective-permute-start(bf16[4,1152]{1,0:T(4,128)(2,1)S(1)} %get-tuple-element.21.a_ref), channel_id=1, source_target_pairs={{0,8},{4,12},{8,0},{12,4},{1,9},{5,13},{9,1},{13,5},{2,10},{6,14},... | collective-permute-start | bytes 27656 | tf_op jit(solution)/shard_map/ppermute | solution.py:342
  10.5 3.8 %collective-permute-start.1 = (bf16[8,1152]{1,0:T(8,128)(2,1)S(1)}, bf16[8,1152]{1,0:T(8,128)(2,1)S(1)}, u32[]{:S(2)}, u32[]{:S(2)}) collective-permute-start(bf16[8,1152]{1,0:T(8,128)(2,1)S(1)} %cat.3.a_ref), channel_id=1, source_target_pairs={{0,4},{4,0},{8,12},{12,8},{1,5},{5,1},{9,13},{13,9},{2,6},{6,2},{1... | collective-permute-start | bytes 55304 | tf_op jit(solution)/shard_map/ppermute | solution.py:342
  14.3 4.0 %collective-permute-start.2 = (bf16[16,1152]{1,0:T(8,128)(2,1)S(1)}, bf16[16,1152]{1,0:T(8,128)(2,1)S(1)}, u32[]{:S(2)}, u32[]{:S(2)}) collective-permute-start(bf16[16,1152]{1,0:T(8,128)(2,1)S(1)} %cat.4.a_ref), channel_id=1, source_target_pairs={{0,16},{16,0},{1,17},{17,1},{2,18},{18,2},{3,19},{19,3},{4,20},{20... | collective-permute-start | bytes 110600 | tf_op jit(solution)/shard_map/ppermute | solution.py:342
  18.2 4.6 %copy-start = (bf16[8,1024,768]{2,1,0:T(8,128)(2,1)S(1)}, bf16[8,1024,768]{2,1,0:T(8,128)(2,1)}, u32[]{:S(2)}) copy-start(bf16[8,1024,768]{2,1,0:T(8,128)(2,1)} %gw_ref.3) | copy-start | bytes 37748740
  22.8 4.6 %copy-start.2 = (bf16[8,1024,768]{2,1,0:T(8,128)(2,1)S(1)}, bf16[8,1024,768]{2,1,0:T(8,128)(2,1)}, u32[]{:S(2)}) copy-start(bf16[8,1024,768]{2,1,0:T(8,128)(2,1)} %uw_ref.3) | copy-start | bytes 37748740
  27.4 4.6 %copy-start.1 = (bf16[8,1024,768]{2,1,0:T(8,128)(2,1)S(1)}, bf16[8,1024,768]{2,1,0:T(8,128)(2,1)}, u32[]{:S(2)}) copy-start(bf16[8,1024,768]{2,1,0:T(8,128)(2,1)} %gw_ref.3) | copy-start | bytes 37748740
  27.4 8.2 %copy-start.3 = (bf16[8,1024,768]{2,1,0:T(8,128)(2,1)S(1)}, bf16[8,1024,768]{2,1,0:T(8,128)(2,1)}, u32[]{:S(2)}) copy-start(bf16[8,1024,768]{2,1,0:T(8,128)(2,1)} %uw_ref.3) | copy-start | bytes 37748740
  31.3 7.7 %collective-permute-start.3 = (bf16[128,768]{1,0:T(8,128)(2,1)S(1)}, bf16[128,768]{1,0:T(8,128)(2,1)S(1)}, u32[]{:S(2)}, u32[]{:S(2)}) collective-permute-start(bf16[128,768]{1,0:T(8,128)(2,1)S(1)} %get-tuple-element.25), channel_id=1, source_target_pairs={{0,1},{1,0},{2,3},{3,2},{4,5},{5,4},{6,7},{7,6},{8,9},{9,8},{10,11... | collective-permute-start | bytes 589832 | tf_op jit(solution)/shard_map/ppermute | solution.py:342
  35.5 9.5 %copy-start.4 = (bf16[8,768,1024]{2,1,0:T(8,128)(2,1)S(1)}, bf16[8,768,1024]{2,1,0:T(8,128)(2,1)}, u32[]{:S(2)}) copy-start(bf16[8,768,1024]{2,1,0:T(8,128)(2,1)} %dw_ref.3) | copy-start | bytes 37748740
  35.5 11.9 %slice-start = ((s8[12582912]{0:T(1024)(128)(4,1)}), s8[4194304]{0:T(1024)(128)(4,1)S(1)}, s32[]{:S(2)}) async-start(s8[12582912]{0:T(1024)(128)(4,1)} %bitcast), calls=%async_computation | async-start | bytes 8388608
  35.5 11.9 %slice-start.1 = ((s8[12582912]{0:T(1024)(128)(4,1)}), s8[4194304]{0:T(1024)(128)(4,1)S(1)}, s32[]{:S(2)}) async-start(s8[12582912]{0:T(1024)(128)(4,1)} %bitcast), calls=%async_computation.1 | async-start | bytes 8388608
  39.1 5.7 %collective-permute-start.4 = (bf16[128,768]{1,0:T(8,128)(2,1)S(1)}, bf16[128,768]{1,0:T(8,128)(2,1)S(1)}, u32[]{:S(2)}, u32[]{:S(2)}) collective-permute-start(bf16[128,768]{1,0:T(8,128)(2,1)S(1)} %get-tuple-element.27), channel_id=1, source_target_pairs={{0,2},{1,3},{2,0},{3,1},{4,6},{5,7},{6,4},{7,5},{8,10},{9,11},{10,... | collective-permute-start | bytes 589832 | tf_op jit(solution)/shard_map/ppermute | solution.py:342
  44.8 2.6 %slice-start.2 = ((s8[12582912]{0:T(1024)(128)(4,1)}), s8[4194304]{0:T(1024)(128)(4,1)S(1)}, s32[]{:S(2)}) async-start(s8[12582912]{0:T(1024)(128)(4,1)} %bitcast), calls=%async_computation.2 | async-start | bytes 8388608
  44.9 2.5 %collective-permute-start.5 = (bf16[128,384]{1,0:T(8,128)(2,1)S(1)}, bf16[128,384]{1,0:T(8,128)(2,1)S(1)}, u32[]{:S(2)}, u32[]{:S(2)}) collective-permute-start(bf16[128,384]{1,0:T(8,128)(2,1)S(1)} %activate.1.h_ref), channel_id=1, source_target_pairs={{0,1},{1,0},{2,3},{3,2},{4,5},{5,4},{6,7},{7,6},{8,9},{9,8},{10,11... | collective-permute-start | bytes 294920 | tf_op jit(solution)/shard_map/ppermute | solution.py:342
  49.9 4.0 %collective-permute-start.6 = (bf16[16,1024]{1,0:T(8,128)(2,1)S(1)}, bf16[16,1024]{1,0:T(8,128)(2,1)S(1)}, u32[]{:S(2)}, u32[]{:S(2)}) collective-permute-start(bf16[16,1024]{1,0:T(8,128)(2,1)S(1)} %get-tuple-element.32), channel_id=1, source_target_pairs={{0,16},{16,0},{1,17},{17,1},{2,18},{18,2},{3,19},{19,3},{4,20},{20... | collective-permute-start | bytes 98312 | tf_op jit(solution)/shard_map/ppermute | solution.py:342
  53.9 3.8 %collective-permute-start.7 = (bf16[8,1024]{1,0:T(8,128)(2,1)S(1)}, bf16[8,1024]{1,0:T(8,128)(2,1)S(1)}, u32[]{:S(2)}, u32[]{:S(2)}) collective-permute-start(bf16[8,1024]{1,0:T(8,128)(2,1)S(1)} %get-tuple-element.34), channel_id=1, source_target_pairs={{0,4},{4,0},{8,12},{12,8},{1,5},{5,1},{9,13},{13,9},{2,6},{6,2},{1... | collective-permute-start | bytes 49160 | tf_op jit(solution)/shard_map/ppermute | solution.py:342
  57.7 4.6 %collective-permute-start.8 = (bf16[4,1024]{1,0:T(4,128)(2,1)S(1)}, bf16[4,1024]{1,0:T(4,128)(2,1)S(1)}, u32[]{:S(2)}, u32[]{:S(2)}) collective-permute-start(bf16[4,1024]{1,0:T(4,128)(2,1)S(1)} %get-tuple-element.36), channel_id=1, source_target_pairs={{0,8},{4,12},{8,0},{12,4},{1,9},{5,13},{9,1},{13,5},{2,10},{6,14},... | collective-permute-start | bytes 24584 | tf_op jit(solution)/shard_map/ppermute | solution.py:342

commit v2 on v1

v2 whole, which is shorter than its diff:
```python
import functools

import jax
import jax.numpy as jnp
from jax import lax
from jax.experimental import pallas as pl
from jax.experimental.pallas import tpu as pltpu
from jax.sharding import PartitionSpec as P

QB = 128
CAP = 2
LANES = 128
BF = jnp.bfloat16
F32 = jnp.float32
I32 = jnp.int32

VM = pl.BlockSpec(memory_space=pltpu.VMEM)
SM = pl.BlockSpec(memory_space=pltpu.SMEM)
HB = pl.BlockSpec(memory_space=pltpu.HBM)


def sds(shape, dtype):
    return jax.ShapeDtypeStruct(shape, dtype)


def run(kernel, out_shape, in_specs, args, name, limit=2 << 20, flops=0, bytes_=0, **more):
    outs = out_shape if isinstance(out_shape, (list, tuple)) else [out_shape]
    specs = [VM] * len(outs)
    return pl.pallas_call(
        kernel,
        out_shape=out_shape,
        in_specs=in_specs,
        out_specs=specs if isinstance(out_shape, (list, tuple)) else VM,
        compiler_params=pltpu.CompilerParams(vmem_limit_bytes=limit),
        cost_estimate=pl.CostEstimate(flops=flops, bytes_accessed=bytes_, transcendentals=0),
        name=name,
        **more,
    )(*args)


def in_hbm(a):
    return pltpu.with_memory_space_constraint(a, pltpu.HBM)


def in_vmem(a):
    return pltpu.with_memory_space_constraint(a, pltpu.VMEM)


def iota(shape, dim):
    return lax.broadcasted_iota(I32, shape, dim)


def placed(values, start):
    n = values.shape[1]
    spot = (iota((n, LANES), 1) == iota((n, LANES), 0) + start).astype(BF)
    return jnp.dot(values.astype(F32).astype(BF), spot, preferred_element_type=F32)


def pack(tokens, routes, gates, scales):
    rows, width = tokens.shape
    top = routes.shape[1]

    def kernel(t_in, r_in, g_in, *rest):
        s_in, (x_out, *s_out) = rest[:3], rest[3:7]
        t_v, r_v, g_v, *s_v = rest[7:13]
        sems = rest[13]
        copies = [
            pltpu.make_async_copy(src, dst, sems.at[i])
            for i, (src, dst) in enumerate(
                zip((r_in, g_in, t_in, *s_in), (r_v, g_v, t_v, *s_v))
            )
        ]
        for copy in copies:
            copy.start()
        for copy in copies:
            copy.wait()
        x_out[:, :width] = t_v[...]
        gate = g_v[...]
        meta = (
            placed(r_v[...], 0)
            + placed(lax.shift_right_logical(gate, 8), top)
            + placed(gate & 255, 2 * top)
        )
        x_out[:, width:] = meta.astype(BF)
        for src, dst in zip(s_v, s_out):
            dst[...] = src[...].astype(F32)

    arrays = (tokens, routes, gates, *scales)
    arrays = [in_hbm(a) for a in arrays]
    return run(
        kernel,
        [sds((rows, width + LANES), BF)] + [sds(s.shape, F32) for s in scales],
        [HB] * len(arrays),
        arrays,
        "pack",
        scratch_shapes=[pltpu.VMEM(a.shape, a.dtype) for a in arrays]
        + [pltpu.SemaphoreType.DMA((len(arrays),))],
    )


def cat(a, b, after):
    rows = a.shape[0]

    def kernel(a_ref, b_ref, *rest):
        o_ref = rest[-1]
        o_ref[:rows] = a_ref[...]
        o_ref[rows:] = b_ref[...]

    return run(
        kernel,
        sds((2 * rows,) + a.shape[1:], a.dtype),
        [VM] * (2 + len(after)),
        (a, b, *after),
        "cat",
    )


def load(sources, after):
    shape = sources[0][0].shape[1:]
    count = len(sources)
    arrays = []
    for w, _ in sources:
        if not any(w is a for a in arrays):
            arrays.append(w)
    where = [([w is a for a in arrays].index(True), e) for w, e in sources]

    def kernel(*refs):
        w_refs, (o_ref, t_ref, sems) = refs[: len(arrays)], refs[len(arrays) + 1 :]
        copies = [
            pltpu.make_async_copy(w_refs[k].at[e], o_ref.at[i], sems.at[i])
            for i, (k, e) in enumerate(where)
        ]
        for copy in copies:
            copy.start()
        t_ref[...] = jnp.zeros_like(t_ref)
        for copy in copies:
            copy.wait()

    moved = 2 * count * shape[0] * shape[1]
    return pl.pallas_call(
        kernel,
        out_shape=[pltpu.VMEM((count,) + shape, BF), sds((8, LANES), F32)],
        in_specs=[HB] * len(arrays) + [VM],
        out_specs=[VM, VM],
        scratch_shapes=[pltpu.SemaphoreType.DMA((count,))],
        compiler_params=pltpu.CompilerParams(vmem_limit_bytes=1 << 20),
        cost_estimate=pl.CostEstimate(flops=0, bytes_accessed=2 * moved, transcendentals=0),
        name="load",
    )(*[in_hbm(a) for a in arrays], after)


def dispatch(x, width, top, rows_dev, experts, slots):
    rows = x.shape[0]
    per = slots // experts
    meta = x[:, width:].astype(F32)
    base = (lax.axis_index("seq") * experts).astype(F32)
    lane = iota((rows, LANES), 1)
    named = jnp.where(lane < experts, lane, -LANES).astype(F32) + base
    hits = jnp.zeros((rows, LANES), F32)
    gates = jnp.zeros((rows, LANES), F32)
    total = jnp.zeros((rows, 1), F32)
    for k in range(top):
        gate = meta[:, top + k : top + k + 1] * 256.0 + meta[:, 2 * top + k : 2 * top + k + 1]
        equal = meta[:, k : k + 1] == named
        hits = hits + jnp.where(equal, 1.0, 0.0)
        gates = gates + jnp.where(equal, gate, 0.0)
        total = total + gate
    weights = gates / total
    r0, r1 = iota((rows, rows), 0), iota((rows, rows), 1)
    earlier = ((r0 // rows_dev == r1 // rows_dev) & (r1 < r0)).astype(BF)
    rank = jnp.dot(earlier, hits.astype(BF), preferred_element_type=F32)
    grow = (iota((LANES, slots), 1) // per == iota((LANES, slots), 0)).astype(BF)
    wide_hits = jnp.dot(hits.astype(BF), grow, preferred_element_type=F32)
    wide_rank = jnp.dot(rank.astype(BF), grow, preferred_element_type=F32)
    spot = (iota((rows, slots), 1) % per - (iota((rows, slots), 0) // rows_dev) * CAP).astype(F32)
    sel = jnp.where((wide_hits > 0.5) & (wide_rank == spot), 1.0, 0.0).astype(BF)
    slot_rows = lax.dot_general(
        sel, x[:, :width], (((0,), (0,)), ((), ())), preferred_element_type=F32
    ).astype(BF)
    return sel, weights, slot_rows


class Blocks:
    def __init__(self, held_refs, held_at, streams, rows_cut, half, n):
        self.held_refs, self.held_at, self.streams = held_refs, held_at, streams
        self.rows_cut, self.half, self.n = rows_cut, half, n
        self.starts = [pl.multiple_of((half * n + j) * QB, QB) for j in range(n)]

    def start(self):
        for copy in self.streams.values():
            copy[0].start()

    def arrive(self, key):
        if key in self.streams:
            self.streams[key][0].wait()

    def get(self, key, j, k):
        far = pl.ds(k * QB, QB)
        if key in self.held_at:
            ref, at = self.held_at[key]
            near = pl.ds(self.starts[j], QB)
            ref = self.held_refs[ref]
        else:
            ref, at = self.streams[key][1:]
            near = pl.ds(j * QB, QB)
        return ref[at, near, far] if self.rows_cut else ref[at, far, near]


def blocks_of(held_refs, held_at, sources, buf, sems, rows_cut, half, n):
    streams = {}
    for i, (key, ref, e) in enumerate(sources):
        cut = pl.ds(pl.multiple_of(half * (n * QB), QB), n * QB)
        src = ref.at[e, cut, :] if rows_cut else ref.at[e, :, cut]
        streams[key] = (pltpu.make_async_copy(src, buf.at[i], sems.at[i]), buf, i)
    return Blocks(held_refs, held_at, streams, rows_cut, half, n)


def tile(parts):
    return jnp.concatenate([jnp.concatenate(row, axis=1) for row in parts], axis=0)


def half_products(xs_ref, blocks, scales, o_ref, experts):
    width = xs_ref.shape[1]
    n, half = blocks.n, blocks.half
    per = xs_ref.shape[0] // experts
    columns = [(0, j) for j in range(n)] + [(1, j) for j in range(n)]
    group, deep = 2, 2
    for e in range(experts):
        xs = xs_ref[e * per : (e + 1) * per, :]
        blocks.arrive((0, e))
        blocks.arrive((1, e))
        for at in range(0, len(columns), group):
            acc = jnp.zeros((per, group * QB), F32)
            for d in range(0, width // QB, deep):
                rhs = tile(
                    [
                        [
                            blocks.get((m, e), j, q) * scales[m][half * n + j, e, q].astype(BF)
                            for m, j in columns[at : at + group]
                        ]
                        for q in range(d, d + deep)
                    ]
                )
                acc = acc + jnp.dot(
                    xs[:, d * QB : (d + deep) * QB], rhs, preferred_element_type=F32
                )
            o_ref[e * per : (e + 1) * per, at * QB : (at + group) * QB] = acc.astype(o_ref.dtype)


def up_kernel(first, x, gw, uw, gs, us, held, held_at, top, rows_dev, block_count):
    experts, width, hidden = gw.shape
    n = hidden // 2 // QB
    slots = experts * block_count * CAP
    rows = block_count * rows_dev
    streamed = [(m, e) for e in range(experts) for m in (0, 1) if (m, e) not in held_at]

    def kernel(x_ref, gw_ref, uw_ref, gs_ref, us_ref, *rest):
        held_refs, rest = rest[: len(held)], rest[len(held) :]
        outs, (buf, sems) = rest[:-2], rest[-2:]
        half = lax.rem(lax.axis_index("pool"), 2)
        half = 1 - half if first else half
        sources = [((m, e), (gw_ref, uw_ref)[m], e) for m, e in streamed]
        blocks = blocks_of(held_refs, held_at, sources, buf, sems, False, half, n)
        blocks.start()
        if first:
            o_ref, xs_ref, sel_ref, wt_ref = outs
            sel, weights, slot_rows = dispatch(x_ref[...], width, top, rows_dev, experts, slots)
            sel_ref[...] = sel
            wt_ref[...] = weights
            xs_ref[...] = slot_rows
        else:
            (o_ref,) = outs
            xs_ref = x_ref
        half_products(xs_ref, blocks, (gs_ref, us_ref), o_ref, experts)

    products = sds((slots, hidden), BF if first else F32)
    more = [sds((slots, width), BF), sds((rows, slots), BF), sds((rows, LANES), F32)]
    return run(
        kernel,
        [products] + more if first else products,
        [VM, HB, HB, SM, SM] + [VM] * len(held),
        (x, in_hbm(gw), in_hbm(uw), gs, us, *[in_vmem(h) for h in held]),
        "other_half" if first else "own_half",
        limit=24 << 20,
        flops=2 * slots * width * hidden,
        bytes_=2 * experts * width * hidden,
        scratch_shapes=[
            pltpu.VMEM((max(1, len(streamed)), width, hidden // 2), BF),
            pltpu.SemaphoreType.DMA((max(1, len(streamed)),)),
        ],
    )


def add_round(own, got):
    def kernel(a_ref, b_ref, o_ref, r_ref):
        total = a_ref[...] + b_ref[...].astype(F32)
        o_ref[...] = total
        r_ref[...] = total.astype(BF)

    return run(kernel, [sds(own.shape, F32), sds(own.shape, BF)], [VM] * 2, (own, got), "add_round")


def activate(own, got, after):
    slots, hidden = own.shape
    n = hidden // 2

    def kernel(a_ref, b_ref, *rest):
        o_ref = rest[-1]
        gate = a_ref[:, :n] + b_ref[:, :n].astype(F32)
        up = a_ref[:, n:] + b_ref[:, n:].astype(F32)
        o_ref[...] = (jax.nn.silu(gate) * up).astype(BF)

    return run(
        kernel,
        sds((slots, n), BF),
        [VM] * (2 + len(after)),
        (own, got, *after),
        "activate",
    )


def spread_rows(h_ref, sel_ref, wt_ref, experts):
    rows, slots = sel_ref.shape
    per = slots // experts
    sel = sel_ref[...].astype(F32)
    owner = iota((rows, slots), 1) // per
    stack = jnp.concatenate([jnp.where(owner == e, sel, 0.0) for e in range(experts)], axis=0)
    spread = jnp.dot(stack.astype(BF), h_ref[...], preferred_element_type=F32)
    weights = wt_ref[...]
    return [
        (spread[e * rows : (e + 1) * rows] * weights[:, e : e + 1]).astype(BF)
        for e in range(experts)
    ]


def down_products(parts, blocks, scale, experts, width, put):
    n, half, group = blocks.n, blocks.half, 2
    pieces = [(e, j) for e in range(experts) for j in range(n)]
    kept = [p for p in pieces if p[0] in blocks.held_at]
    rest = [p for p in pieces if p[0] not in blocks.held_at]
    for use in (kept, rest):
        if not use:
            continue
        for e in sorted({e for e, _ in use}):
            blocks.arrive(e)
        deep = 2 if len(use) % 2 == 0 else 1
        for c in range(0, width // QB, group):
            acc = None
            for at in range(0, len(use), deep):
                some = use[at : at + deep]
                lhs = jnp.concatenate([parts[e][:, j * QB : (j + 1) * QB] for e, j in some], axis=1)
                rhs = tile(
                    [
                        [
                            blocks.get(e, j, q) * scale[half * n + j, e, q].astype(BF)
                            for q in range(c, c + group)
                        ]
                        for e, j in some
                    ]
                )
                more = jnp.dot(lhs, rhs, preferred_element_type=F32)
                acc = more if acc is None else acc + more
            put(slice(c * QB, (c + group) * QB), acc, use is kept or not kept)


def down_kernel(hid, sel, wt, dw, ds, held, held_at, own):
    experts, hidden, width = dw.shape
    n = hidden // 2 // QB
    rows = sel.shape[0]
    keep = rows // 2
    last = own is not None
    streamed = [e for e in range(experts) if e not in held_at]
    given = [own] if last else []

    def kernel(h_ref, sel_ref, wt_ref, dw_ref, ds_ref, *rest):
        held_refs, rest = rest[: len(held)], rest[len(held) :]
        given_refs, rest = rest[: len(given)], rest[len(given) :]
        outs, (total, buf, sems) = rest[:-3], rest[-3:]
        half = lax.rem(lax.axis_index("pool"), 2)
        half = 1 - half if last else half
        sources = [(e, dw_ref, e) for e in streamed]
        blocks = blocks_of(held_refs, held_at, sources, buf, sems, True, half, n)
        blocks.start()
        parts = spread_rows(h_ref, sel_ref, wt_ref, experts)
        o_ref = total if last else outs[0]

        def put(at, acc, fresh):
            if not fresh:
                acc = acc + o_ref[:, at]
            elif last:
                acc = acc + given_refs[0][:, at]
            o_ref[:, at] = acc

        down_products(parts, blocks, ds_ref, experts, width, put)
        if last:
            outs[0][...] = total[:keep]
            outs[1][...] = total[keep:].astype(BF)

    return run(
        kernel,
        [sds((keep, width), F32), sds((rows - keep, width), BF)] if last else sds((rows, width), F32),
        [VM, VM, VM, HB, SM] + [VM] * (len(held) + len(given)),
        (hid, sel, wt, in_hbm(dw), ds, *[in_vmem(h) for h in held], *given),
        "down_other" if last else "down_own",
        limit=24 << 20,
        flops=experts * rows * width * hidden,
        bytes_=experts * width * hidden,
        scratch_shapes=[
            pltpu.VMEM((rows if last else 8, width), F32),
            pltpu.VMEM((max(1, len(streamed)), hidden // 2, width), BF),
            pltpu.SemaphoreType.DMA((max(1, len(streamed)),)),
        ],
    )


def fold(own, got):
    rows, width = own.shape
    keep = rows // 2

    def kernel(a_ref, b_ref, o_ref, s_ref):
        o_ref[...] = a_ref[:keep] + b_ref[:keep].astype(F32)
        s_ref[...] = (a_ref[keep:] + b_ref[keep:].astype(F32)).astype(BF)

    return run(
        kernel, [sds((keep, width), F32), sds((keep, width), BF)], [VM] * 2, (own, got), "fold"
    )


def finish(own, got):
    def kernel(a_ref, b_ref, o_ref):
        o_ref[...] = (a_ref[...] + b_ref[...].astype(F32)).astype(BF)

    return run(kernel, sds(own.shape, BF), [VM] * 2, (own, got), "finish")


def swap(x, axis, bit):
    return lax.ppermute(x, axis, [(j, j ^ bit) for j in range(lax.axis_size(axis))])


def bits(count):
    return [1 << i for i in range(count.bit_length() - 1)]


def per_device(tokens, routes, gate_fixed, gw, uw, dw, gs, us, ds):
    n_seq, n_head, n_pool = (lax.axis_size(a) for a in ("seq", "head", "pool"))
    rows_dev, width = tokens.shape
    top = routes.shape[1]
    hops = [("head", b) for b in reversed(bits(n_head))] + [("seq", b) for b in bits(n_seq)]

    experts = gw.shape[0]
    scales = [gs.transpose(2, 0, 1), us.transpose(2, 0, 1), ds.transpose(1, 0, 2)]
    x, gs, us, ds = pack(tokens, routes, gate_fixed, scales)
    waiting = [(m, e) for e in range(experts // 2) for m in (0, 1)]
    held, held_at = [], {}
    for i, (axis, bit) in enumerate(hops):
        got = swap(x, axis, bit)
        take = -(-len(waiting) // (len(hops) - i))
        after = []
        if take:
            use, waiting = waiting[:take], waiting[take:]
            block, token = load([((gw, uw)[m], e) for m, e in use], x)
            held_at.update({key: (len(held), at) for at, key in enumerate(use)})
            held.append(block)
            after = [token]
        x = cat(x, got, after)

    common = (gw, uw, gs, us, held, held_at, top, rows_dev, n_seq * n_head)
    send, xs, sel, wt = up_kernel(True, x, *common)
    got = swap(send, "pool", 1)
    own = up_kernel(False, xs, *common)
    steps = bits(n_pool)[1:]
    waiting = list(range(experts * 3 // 4))
    held, held_at = [], {}
    tokens_of = []
    for i, bit in enumerate(steps):
        own, send = add_round(own, got)
        got = swap(send, "pool", bit)
        take = -(-len(waiting) // (len(steps) - i))
        if take:
            use, waiting = waiting[:take], waiting[take:]
            block, token = load([(dw, e) for e in use], send)
            held_at.update({e: (len(held), at) for at, e in enumerate(use)})
            held.append(block)
            tokens_of.append(token)
    hid = activate(own, got, tokens_of)
    other = swap(hid, "pool", 1)
    acc = down_kernel(hid, sel, wt, dw, ds, held, held_at, None)
    acc, send = down_kernel(other, sel, wt, dw, ds, held, held_at, acc)
    for axis, bit in reversed(hops[1:]):
        acc, send = fold(acc, swap(send, axis, bit))
    axis, bit = hops[0]
    return finish(acc, swap(send, axis, bit))


def solution(mesh):
    return jax.shard_map(
        per_device,
        mesh=mesh,
        in_specs=(
            P(("seq", "head"), "pool"),
            P(("seq", "head"), None),
            P(("seq", "head"), None),
            P("seq", "pool", "head"),
            P("seq", "pool", "head"),
            P("seq", "head", "pool"),
            P("seq", "pool", "head"),
            P("seq", "pool", "head"),
            P("seq", "head", "pool"),
        ),
        out_specs=P(("seq", "head"), "pool"),
        check_vma=False,
    )
```

time: 63.4 us -> 55 us (0.87)
  local copies, waits for them, and re-layouts: 17.8 us -> 0 us
  Pallas kernels: 13.3 us -> 30.6 us
  waiting for transfers between devices: 15 us -> 9.9 us
  starting transfers between devices: 16.7 us -> 14.1 us
    unnamed x25 -> x0, local copies, waits for them, and re-layouts: 17.8 us -> none
    pallas_call x0 -> x4, Pallas kernels: none -> 10.4 us  [load(): pl.pallas_call(kernel, out_shape=[pltpu.VMEM((count,) + shape, BF), sds((...]
    pallas_call x13, Pallas kernels: 13.3 us -> 20.2 us  [run(): pl.pallas_call(kernel, out_shape=out_shape, in_specs=in_specs, out_specs=...]
    ppermute x9, waiting for transfers between devices: 15 us -> 9.9 us  [swap(): lax.ppermute(x, axis, [(j, j ^ bit) for j in range(lax.axis_size(axis))])]
    ppermute x9, starting transfers between devices: 16.7 us -> 14.1 us  [swap(): lax.ppermute(x, axis, [(j, j ^ bit) for j in range(lax.axis_size(axis))])]
  transfers between devices with their start and end apart: 9 -> 9, of which waited for: 7 -> 5; matrix products, arithmetic and copies ran while one was open for 0% -> 0% of each run, Pallas kernels for 9% -> 35%
where the time goes in v2:
time: 55 us; the launch traced here: 54.8 us
  Pallas kernels  30.6 us (56%)
  starting transfers between devices  14.1 us (26%)
  waiting for transfers between devices  9.9 us (18%)
    pallas_call x13, Pallas kernels, run(): pl.pallas_call(kernel, out_shape=out_shape, in_specs=in_specs, out_specs=...  20.2 us
    ppermute x9, starting transfers between devices, swap(): lax.ppermute(x, axis, [(j, j ^ bit) for j in range(lax.axis_size(axis))])  14.1 us
    pallas_call x4, Pallas kernels, load(): pl.pallas_call(kernel, out_shape=[pltpu.VMEM((count,) + shape, BF), sds((...  10.4 us
    ppermute x9, waiting for transfers between devices, swap(): lax.ppermute(x, axis, [(j, j ^ bit) for j in range(lax.axis_size(axis))])  9.9 us
  transfers between devices with their start and end apart: 9, of which 5 were waited for; matrix products, arithmetic and copies ran while one was open for 0% of the time, Pallas kernels for 35%

profile of v2, /device:TPU:0, one launch (start us, length us, event | category | flops | bytes accessed | tf_op | source)
XLA Modules:
  0.0 54.8 jit_solution(5336665580365919741)
XLA Ops:
  0.0 1.0 %pack.1 = (bf16[4,1152]{1,0:T(4,128)(2,1)S(1)}, f32[6,8,8]{2,1,0:T(8,128)S(1)}, f32[6,8,8]{2,1,0:T(8,128)S(1)}, f32[6,8,8]{2,1,0:T(8,128)S(1)}) custom-call(bf16[4,1024]{1,0:T(4,128)(2,1)} %t_in.1, s32[4,8]{1,0:T(4,128)} %r_in.1, s32[4,8]{1,0:T(4,128)} %g_in.1, bf16[6,8,8]{2,1,0:T(8,128)(2,1)} %bitcast.3, bf16[6,8,8]{2,1,0:T(8,128)(2,1)} %bitcast.4, ...), custom_call_target="tpu_custom_call" | custom-call | tf_op jit(solution)/shard_map/pack/pallas_call | solution.py:29
  1.0 4.1 %collective-permute-start = (bf16[4,1152]{1,0:T(4,128)(2,1)S(1)}, bf16[4,1152]{1,0:T(4,128)(2,1)S(1)}, u32[]{:S(2)}, u32[]{:S(2)}) collective-permute-start(bf16[4,1152]{1,0:T(4,128)(2,1)S(1)} %get-tuple-element.29.refs_2_.a_ref), channel_id=1, source_target_pairs={{0,8},{4,12},{8,0},{12,4},{1,9},{5,13},{9,1},{13,5},{2,10},{6,14},... | collective-permute-start | bytes 27656 | tf_op jit(solution)/shard_map/ppermute | solution.py:437
  5.1 2.4 %load.4 = (bf16[3,1024,768]{2,1,0:T(8,128)(2,1)S(1)}, f32[8,128]{1,0:T(8,128)S(1)}) custom-call(bf16[8,1024,768]{2,1,0:T(8,128)(2,1)} %gw_ref.3, bf16[8,1024,768]{2,1,0:T(8,128)(2,1)} %uw_ref.3, bf16[4,1152]{1,0:T(4,128)(2,1)S(1)} %get-tuple-element.29.refs_2_.a_ref), custom_call_target="tpu_custom_call" | custom-call | bytes 9437184 | tf_op jit(solution)/shard_map/load/pallas_call | solution.py:140
  7.5 0.0 collective-permute-done.b_ref
  7.5 1.6 %collective-permute-start.1 = (bf16[8,1152]{1,0:T(8,128)(2,1)S(1)}, bf16[8,1152]{1,0:T(8,128)(2,1)S(1)}, u32[]{:S(2)}, u32[]{:S(2)}) collective-permute-start(bf16[8,1152]{1,0:T(8,128)(2,1)S(1)} %cat.3.refs_2_.a_ref), channel_id=1, source_target_pairs={{0,4},{4,0},{8,12},{12,8},{1,5},{5,1},{9,13},{13,9},{2,6},{6,2},{1... | collective-permute-start | bytes 55304 | tf_op jit(solution)/shard_map/ppermute | solution.py:437
  9.2 2.4 %load.5 = (bf16[3,1024,768]{2,1,0:T(8,128)(2,1)S(1)}, f32[8,128]{1,0:T(8,128)S(1)}) custom-call(bf16[8,1024,768]{2,1,0:T(8,128)(2,1)} %uw_ref.3, bf16[8,1024,768]{2,1,0:T(8,128)(2,1)} %gw_ref.3, bf16[8,1152]{1,0:T(8,128)(2,1)S(1)} %cat.3.refs_2_.a_ref), custom_call_target="tpu_custom_call" | custom-call | bytes 9437184 | tf_op jit(solution)/shard_map/load/pallas_call | solution.py:140
  11.5 0.0 collective-permute-done.1.b_ref
  11.6 1.6 %collective-permute-start.2 = (bf16[16,1152]{1,0:T(8,128)(2,1)S(1)}, bf16[16,1152]{1,0:T(8,128)(2,1)S(1)}, u32[]{:S(2)}, u32[]{:S(2)}) collective-permute-start(bf16[16,1152]{1,0:T(8,128)(2,1)S(1)} %cat.4.refs_2_.a_ref), channel_id=1, source_target_pairs={{0,16},{16,0},{1,17},{17,1},{2,18},{18,2},{3,19},{19,3},{4,20},{20... | collective-permute-start | bytes 110600 | tf_op jit(solution)/shard_map/ppermute | solution.py:437
  13.1 1.9 %load.6 = (bf16[2,1024,768]{2,1,0:T(8,128)(2,1)S(1)}, f32[8,128]{1,0:T(8,128)S(1)}) custom-call(bf16[8,1024,768]{2,1,0:T(8,128)(2,1)} %gw_ref.3, bf16[8,1024,768]{2,1,0:T(8,128)(2,1)} %uw_ref.3, bf16[16,1152]{1,0:T(8,128)(2,1)S(1)} %cat.4.refs_2_.a_ref), custom_call_target="tpu_custom_call" | custom-call | bytes 6291456 | tf_op jit(solution)/shard_map/load/pallas_call | solution.py:140
  15.0 0.6 %collective-permute-done.2.b_ref = bf16[16,1152]{1,0:T(8,128)(2,1)S(1)} collective-permute-done((bf16[16,1152]{1,0:T(8,128)(2,1)S(1)}, bf16[16,1152]{1,0:T(8,128)(2,1)S(1)}, u32[]{:S(2)}, u32[]{:S(2)}) %collective-permute-start.2) | collective-permute-done | bytes 36896 | tf_op jit(solution)/shard_map/ppermute | solution.py:437
  15.6 5.9 %other_half.1 = (bf16[128,768]{1,0:T(8,128)(2,1)S(1)}, bf16[128,1024]{1,0:T(8,128)(2,1)S(1)}, bf16[32,128]{1,0:T(8,128)(2,1)S(1)}, f32[32,128]{1,0:T(8,128)S(1)}) custom-call(bf16[32,1152]{1,0:T(8,128)(2,1)S(1)} %cat.5.x_ref, bf16[8,1024,768]{2,1,0:T(8,128)(2,1)} %gw_ref.3, bf16[8,1024,768]{2,1,0:T(8,128)(2,1)} %uw_ref.3, ...), custom_call_target="tpu_custom_call" | custom-call | flops 201326592 | bytes 12582912 | tf_op jit(solution)/shard_map/other_half/pallas_call | solution.py:29
  21.5 0.1 collective-permute-start.3
  21.6 5.4 %own_half.1.a_ref = f32[128,768]{1,0:T(8,128)S(1)} custom-call(bf16[128,1024]{1,0:T(8,128)(2,1)S(1)} %get-tuple-element.38.x_ref, bf16[8,1024,768]{2,1,0:T(8,128)(2,1)} %gw_ref.3, bf16[8,1024,768]{2,1,0:T(8,128)(2,1)} %uw_ref.3, f32[6,8,8]{2,1,0:T(8,128)S(1)} %get-tuple-element.33.gs_ref, f32[6,8,8]{2,1,0:T(8,128)S(1)} %get-tuple-element.34.us_ref, ...), custom_call_target="tpu_custom_call" | custom-call | flops 201326592 | bytes 12582912 | tf_op jit(solution)/shard_map/own_half/pallas_call | solution.py:29
  27.0 0.0 collective-permute-done.3.b_ref
  27.0 0.1 add_round.1
  27.1 1.6 %collective-permute-start.4 = (bf16[128,768]{1,0:T(8,128)(2,1)S(1)}, bf16[128,768]{1,0:T(8,128)(2,1)S(1)}, u32[]{:S(2)}, u32[]{:S(2)}) collective-permute-start(bf16[128,768]{1,0:T(8,128)(2,1)S(1)} %get-tuple-element.41.refs_1_), channel_id=1, source_target_pairs={{0,2},{1,3},{2,0},{3,1},{4,6},{5,7},{6,4},{7,5},{8,10},{9,11},{10,... | collective-permute-start | bytes 589832 | tf_op jit(solution)/shard_map/ppermute | solution.py:437
  28.7 3.8 %load.7 = (bf16[6,768,1024]{2,1,0:T(8,128)(2,1)S(1)}, f32[8,128]{1,0:T(8,128)S(1)}) custom-call(bf16[8,768,1024]{2,1,0:T(8,128)(2,1)} %dw_ref.3, bf16[128,768]{1,0:T(8,128)(2,1)S(1)} %get-tuple-element.41.refs_1_), custom_call_target="tpu_custom_call" | custom-call | bytes 18874368 | tf_op jit(solution)/shard_map/load/pallas_call | solution.py:140
  32.5 2.0 %collective-permute-done.4.b_ref = bf16[128,768]{1,0:T(8,128)(2,1)S(1)} collective-permute-done((bf16[128,768]{1,0:T(8,128)(2,1)S(1)}, bf16[128,768]{1,0:T(8,128)(2,1)S(1)}, u32[]{:S(2)}, u32[]{:S(2)}) %collective-permute-start.4) | collective-permute-done | bytes 196640 | tf_op jit(solution)/shard_map/ppermute | solution.py:437
  34.5 0.1 activate.1.h_ref
  34.6 0.1 collective-permute-start.5
  34.6 3.6 %down_own.1.rest_1_ = f32[32,1024]{1,0:T(8,128)S(1)} custom-call(bf16[128,384]{1,0:T(8,128)(2,1)S(1)} %activate.1.h_ref, bf16[32,128]{1,0:T(8,128)(2,1)S(1)} %get-tuple-element.43.sel_ref, f32[32,128]{1,0:T(8,128)S(1)} %get-tuple-element.44.wt_ref, bf16[8,768,1024]{2,1,0:T(8,128)(2,1)} %dw_ref.3, f32[6,8,8]{2,1,0:T(8,128)S(1)} %get-tuple-element.45.ds_ref, ...), custom_call_target="tpu_custom_call" | custom-call | flops 201326592 | bytes 6291456 | tf_op jit(solution)/shard_map/down_own/pallas_call | solution.py:29
  38.2 0.0 collective-permute-done.5.h_ref
  38.2 3.6 %down_other.1 = (f32[16,1024]{1,0:T(8,128)S(1)}, bf16[16,1024]{1,0:T(8,128)(2,1)S(1)}) custom-call(bf16[128,384]{1,0:T(8,128)(2,1)S(1)} %collective-permute-done.5.h_ref, bf16[32,128]{1,0:T(8,128)(2,1)S(1)} %get-tuple-element.43.sel_ref, f32[32,128]{1,0:T(8,128)S(1)} %get-tuple-element.44.wt_ref, bf16[8,768,1024]{2,1,0:T(8,128)(2,1)} %dw_ref.3, ...), custom_call_target="tpu_custom_call" | custom-call | flops 201326592 | bytes 6291456 | tf_op jit(solution)/shard_map/down_other/pallas_call | solution.py:29
  41.8 1.6 %collective-permute-start.6 = (bf16[16,1024]{1,0:T(8,128)(2,1)S(1)}, bf16[16,1024]{1,0:T(8,128)(2,1)S(1)}, u32[]{:S(2)}, u32[]{:S(2)}) collective-permute-start(bf16[16,1024]{1,0:T(8,128)(2,1)S(1)} %get-tuple-element.48), channel_id=1, source_target_pairs={{0,16},{16,0},{1,17},{17,1},{2,18},{18,2},{3,19},{19,3},{4,20},{20... | collective-permute-start | bytes 98312 | tf_op jit(solution)/shard_map/ppermute | solution.py:437
  43.3 2.4 %collective-permute-done.6.b_ref = bf16[16,1024]{1,0:T(8,128)(2,1)S(1)} collective-permute-done((bf16[16,1024]{1,0:T(8,128)(2,1)S(1)}, bf16[16,1024]{1,0:T(8,128)(2,1)S(1)}, u32[]{:S(2)}, u32[]{:S(2)}) %collective-permute-start.6) | collective-permute-done | bytes 32800 | tf_op jit(solution)/shard_map/ppermute | solution.py:437
  45.8 1.4 %collective-permute-start.7 = (bf16[8,1024]{1,0:T(8,128)(2,1)S(1)}, bf16[8,1024]{1,0:T(8,128)(2,1)S(1)}, u32[]{:S(2)}, u32[]{:S(2)}) collective-permute-start(bf16[8,1024]{1,0:T(8,128)(2,1)S(1)} %get-tuple-element.50), channel_id=1, source_target_pairs={{0,4},{4,0},{8,12},{12,8},{1,5},{5,1},{9,13},{13,9},{2,6},{6,2},{1... | collective-permute-start | bytes 49160 | tf_op jit(solution)/shard_map/ppermute | solution.py:437
  47.1 2.4 %collective-permute-done.7.b_ref = bf16[8,1024]{1,0:T(8,128)(2,1)S(1)} collective-permute-done((bf16[8,1024]{1,0:T(8,128)(2,1)S(1)}, bf16[8,1024]{1,0:T(8,128)(2,1)S(1)}, u32[]{:S(2)}, u32[]{:S(2)}) %collective-permute-start.7) | collective-permute-done | bytes 16416 | tf_op jit(solution)/shard_map/ppermute | solution.py:437
  49.6 2.2 %collective-permute-start.8 = (bf16[4,1024]{1,0:T(4,128)(2,1)S(1)}, bf16[4,1024]{1,0:T(4,128)(2,1)S(1)}, u32[]{:S(2)}, u32[]{:S(2)}) collective-permute-start(bf16[4,1024]{1,0:T(4,128)(2,1)S(1)} %get-tuple-element.52), channel_id=1, source_target_pairs={{0,8},{4,12},{8,0},{12,4},{1,9},{5,13},{9,1},{13,5},{2,10},{6,14},... | collective-permute-start | bytes 24584 | tf_op jit(solution)/shard_map/ppermute | solution.py:437
  51.7 2.5 %collective-permute-done.8.b_ref = bf16[4,1024]{1,0:T(4,128)(2,1)S(1)} collective-permute-done((bf16[4,1024]{1,0:T(4,128)(2,1)S(1)}, bf16[4,1024]{1,0:T(4,128)(2,1)S(1)}, u32[]{:S(2)}, u32[]{:S(2)}) %collective-permute-start.8) | collective-permute-done | bytes 8224 | tf_op jit(solution)/shard_map/ppermute | solution.py:437
  54.2 0.6 %finish.1 = bf16[4,1024]{1,0:T(4,128)(2,1)} custom-call(f32[4,1024]{1,0:T(4,128)S(1)} %get-tuple-element.51.a_ref, bf16[4,1024]{1,0:T(4,128)(2,1)S(1)} %collective-permute-done.8.b_ref), custom_call_target="tpu_custom_call" | custom-call | tf_op jit(solution)/shard_map/finish/pallas_call | solution.py:29
  (5 shorter events, 0.0 us)
Async XLA Ops:
  1.0 6.5 %collective-permute-start = (bf16[4,1152]{1,0:T(4,128)(2,1)S(1)}, bf16[4,1152]{1,0:T(4,128)(2,1)S(1)}, u32[]{:S(2)}, u32[]{:S(2)}) collective-permute-start(bf16[4,1152]{1,0:T(4,128)(2,1)S(1)} %get-tuple-element.29.refs_2_.a_ref), channel_id=1, source_target_pairs={{0,8},{4,12},{8,0},{12,4},{1,9},{5,13},{9,1},{13,5},{2,10},{6,14},... | collective-permute-start | bytes 27656 | tf_op jit(solution)/shard_map/ppermute | solution.py:437
  7.5 4.0 %collective-permute-start.1 = (bf16[8,1152]{1,0:T(8,128)(2,1)S(1)}, bf16[8,1152]{1,0:T(8,128)(2,1)S(1)}, u32[]{:S(2)}, u32[]{:S(2)}) collective-permute-start(bf16[8,1152]{1,0:T(8,128)(2,1)S(1)} %cat.3.refs_2_.a_ref), channel_id=1, source_target_pairs={{0,4},{4,0},{8,12},{12,8},{1,5},{5,1},{9,13},{13,9},{2,6},{6,2},{1... | collective-permute-start | bytes 55304 | tf_op jit(solution)/shard_map/ppermute | solution.py:437
  11.6 4.0 %collective-permute-start.2 = (bf16[16,1152]{1,0:T(8,128)(2,1)S(1)}, bf16[16,1152]{1,0:T(8,128)(2,1)S(1)}, u32[]{:S(2)}, u32[]{:S(2)}) collective-permute-start(bf16[16,1152]{1,0:T(8,128)(2,1)S(1)} %cat.4.refs_2_.a_ref), channel_id=1, source_target_pairs={{0,16},{16,0},{1,17},{17,1},{2,18},{18,2},{3,19},{19,3},{4,20},{20... | collective-permute-start | bytes 110600 | tf_op jit(solution)/shard_map/ppermute | solution.py:437
  21.5 5.5 %collective-permute-start.3 = (bf16[128,768]{1,0:T(8,128)(2,1)S(1)}, bf16[128,768]{1,0:T(8,128)(2,1)S(1)}, u32[]{:S(2)}, u32[]{:S(2)}) collective-permute-start(bf16[128,768]{1,0:T(8,128)(2,1)S(1)} %get-tuple-element.39), channel_id=1, source_target_pairs={{0,1},{1,0},{2,3},{3,2},{4,5},{5,4},{6,7},{7,6},{8,9},{9,8},{10,11... | collective-permute-start | bytes 589832 | tf_op jit(solution)/shard_map/ppermute | solution.py:437
  27.1 7.4 %collective-permute-start.4 = (bf16[128,768]{1,0:T(8,128)(2,1)S(1)}, bf16[128,768]{1,0:T(8,128)(2,1)S(1)}, u32[]{:S(2)}, u32[]{:S(2)}) collective-permute-start(bf16[128,768]{1,0:T(8,128)(2,1)S(1)} %get-tuple-element.41.refs_1_), channel_id=1, source_target_pairs={{0,2},{1,3},{2,0},{3,1},{4,6},{5,7},{6,4},{7,5},{8,10},{9,11},{10,... | collective-permute-start | bytes 589832 | tf_op jit(solution)/shard_map/ppermute | solution.py:437
  34.6 3.6 %collective-permute-start.5 = (bf16[128,384]{1,0:T(8,128)(2,1)S(1)}, bf16[128,384]{1,0:T(8,128)(2,1)S(1)}, u32[]{:S(2)}, u32[]{:S(2)}) collective-permute-start(bf16[128,384]{1,0:T(8,128)(2,1)S(1)} %activate.1.h_ref), channel_id=1, source_target_pairs={{0,1},{1,0},{2,3},{3,2},{4,5},{5,4},{6,7},{7,6},{8,9},{9,8},{10,11... | collective-permute-start | bytes 294920 | tf_op jit(solution)/shard_map/ppermute | solution.py:437
  41.8 4.0 %collective-permute-start.6 = (bf16[16,1024]{1,0:T(8,128)(2,1)S(1)}, bf16[16,1024]{1,0:T(8,128)(2,1)S(1)}, u32[]{:S(2)}, u32[]{:S(2)}) collective-permute-start(bf16[16,1024]{1,0:T(8,128)(2,1)S(1)} %get-tuple-element.48), channel_id=1, source_target_pairs={{0,16},{16,0},{1,17},{17,1},{2,18},{18,2},{3,19},{19,3},{4,20},{20... | collective-permute-start | bytes 98312 | tf_op jit(solution)/shard_map/ppermute | solution.py:437
  45.8 3.8 %collective-permute-start.7 = (bf16[8,1024]{1,0:T(8,128)(2,1)S(1)}, bf16[8,1024]{1,0:T(8,128)(2,1)S(1)}, u32[]{:S(2)}, u32[]{:S(2)}) collective-permute-start(bf16[8,1024]{1,0:T(8,128)(2,1)S(1)} %get-tuple-element.50), channel_id=1, source_target_pairs={{0,4},{4,0},{8,12},{12,8},{1,5},{5,1},{9,13},{13,9},{2,6},{6,2},{1... | collective-permute-start | bytes 49160 | tf_op jit(solution)/shard_map/ppermute | solution.py:437
  49.6 4.6 %collective-permute-start.8 = (bf16[4,1024]{1,0:T(4,128)(2,1)S(1)}, bf16[4,1024]{1,0:T(4,128)(2,1)S(1)}, u32[]{:S(2)}, u32[]{:S(2)}) collective-permute-start(bf16[4,1024]{1,0:T(4,128)(2,1)S(1)} %get-tuple-element.52), channel_id=1, source_target_pairs={{0,8},{4,12},{8,0},{12,4},{1,9},{5,13},{9,1},{13,5},{2,10},{6,14},... | collective-permute-start | bytes 24584 | tf_op jit(solution)/shard_map/ppermute | solution.py:437

commit v3 on v2

v3 whole, which is shorter than its diff:
```python
import functools

import jax
import jax.numpy as jnp
from jax import lax
from jax.experimental import pallas as pl
from jax.experimental.pallas import tpu as pltpu
from jax.sharding import PartitionSpec as P

QB = 128
CAP = 2
LANES = 128
BF = jnp.bfloat16
F32 = jnp.float32
I32 = jnp.int32

VM = pl.BlockSpec(memory_space=pltpu.VMEM)
HB = pl.BlockSpec(memory_space=pltpu.HBM)


def sds(shape, dtype):
    return jax.ShapeDtypeStruct(shape, dtype)


def run(kernel, out_shape, in_specs, args, name, limit=2 << 20, flops=0, bytes_=0, **more):
    outs = out_shape if isinstance(out_shape, (list, tuple)) else [out_shape]
    specs = [VM] * len(outs)
    return pl.pallas_call(
        kernel,
        out_shape=out_shape,
        in_specs=in_specs,
        out_specs=specs if isinstance(out_shape, (list, tuple)) else VM,
        compiler_params=pltpu.CompilerParams(vmem_limit_bytes=limit),
        cost_estimate=pl.CostEstimate(flops=flops, bytes_accessed=bytes_, transcendentals=0),
        name=name,
        **more,
    )(*args)


def in_hbm(a):
    return pltpu.with_memory_space_constraint(a, pltpu.HBM)


def in_vmem(a):
    return pltpu.with_memory_space_constraint(a, pltpu.VMEM)


def iota(shape, dim):
    return lax.broadcasted_iota(I32, shape, dim)


def placed(values, start):
    n = values.shape[1]
    spot = (iota((n, LANES), 1) == iota((n, LANES), 0) + start).astype(BF)
    return jnp.dot(values.astype(F32).astype(BF), spot, preferred_element_type=F32)


def pack(tokens, routes, gates):
    rows, width = tokens.shape
    top = routes.shape[1]

    def kernel(t_in, r_in, g_in, x_out, t_v, r_v, g_v, sems):
        copies = [
            pltpu.make_async_copy(src, dst, sems.at[i])
            for i, (src, dst) in enumerate(((r_in, r_v), (g_in, g_v), (t_in, t_v)))
        ]
        for copy in copies:
            copy.start()
        for copy in copies:
            copy.wait()
        x_out[:, :width] = t_v[...]
        gate = g_v[...]
        meta = (
            placed(r_v[...], 0)
            + placed(lax.shift_right_logical(gate, 8), top)
            + placed(gate & 255, 2 * top)
        )
        x_out[:, width:] = meta.astype(BF)

    arrays = [in_hbm(a) for a in (tokens, routes, gates)]
    return run(
        kernel,
        sds((rows, width + LANES), BF),
        [HB] * len(arrays),
        arrays,
        "pack",
        scratch_shapes=[pltpu.VMEM(a.shape, a.dtype) for a in arrays]
        + [pltpu.SemaphoreType.DMA((len(arrays),))],
    )


def cat(a, b, after):
    rows = a.shape[0]

    def kernel(a_ref, b_ref, *rest):
        o_ref = rest[-1]
        o_ref[:rows] = a_ref[...]
        o_ref[rows:] = b_ref[...]

    return run(
        kernel,
        sds((2 * rows,) + a.shape[1:], a.dtype),
        [VM] * (2 + len(after)),
        (a, b, *after),
        "cat",
    )


def moved_bytes(count, rows, columns):
    return 2 * 2 * count * rows * columns


def load(sources, scales, after):
    arrays = []
    for w, _ in sources:
        if not any(w is a for a in arrays):
            arrays.append(w)
    where = [([w is a for a in arrays].index(True), e) for w, e in sources]
    count, n_arrays, n_scales = len(sources), len(arrays), len(scales)
    n_out = 1 if count else 0

    def kernel(*refs):
        w_refs, refs = refs[:n_arrays], refs[n_arrays:]
        s_refs, refs = refs[:n_scales], refs[n_scales + 1 :]
        o_refs, refs = refs[:n_out], refs[n_out:]
        e_refs, refs = refs[:n_scales], refs[n_scales:]
        t_ref, s_v, sems = refs[0], refs[1:-1], refs[-1]
        small = [
            pltpu.make_async_copy(src, dst, sems.at[count + i])
            for i, (src, dst) in enumerate(zip(s_refs, s_v))
        ]
        copies = [
            pltpu.make_async_copy(w_refs[k].at[e], o_refs[0].at[i], sems.at[i])
            for i, (k, e) in enumerate(where)
        ]
        for copy in small + copies:
            copy.start()
        t_ref[...] = jnp.zeros_like(t_ref)
        for copy in small:
            copy.wait()
        for src, dst in zip(s_v, e_refs):
            for a in range(src.shape[0]):
                values = src[a].astype(F32)
                for b in range(src.shape[2]):
                    dst[a, b] = jnp.broadcast_to(values[:, b : b + 1], dst.shape[2:])
        for copy in copies:
            copy.wait()

    spread = [sds((s.shape[0], s.shape[2], s.shape[1], LANES), F32) for s in scales]
    shape = sources[0][0].shape[1:] if count else (0, 0)
    outs = [pltpu.VMEM((count,) + shape, BF)] if count else []
    result = pl.pallas_call(
        kernel,
        out_shape=outs + spread + [sds((8, LANES), F32)],
        in_specs=[HB] * (n_arrays + n_scales) + [VM],
        out_specs=[VM] * (n_out + n_scales + 1),
        scratch_shapes=[pltpu.VMEM(s.shape, s.dtype) for s in scales]
        + [pltpu.SemaphoreType.DMA((count + n_scales,))],
        compiler_params=pltpu.CompilerParams(vmem_limit_bytes=2 << 20),
        cost_estimate=pl.CostEstimate(
            flops=0, bytes_accessed=moved_bytes(count, *shape) + (1 << 20), transcendentals=0
        ),
        name="load",
    )(*[in_hbm(a) for a in arrays + list(scales)], after)
    return result[:n_out], result[n_out:-1], result[-1]


def half_rows(w, other, after):
    experts, hidden, width = w.shape
    n = hidden // 2

    def kernel(w_ref, _, o_ref, t_ref, sems):
        half = lax.rem(lax.axis_index("pool"), 2)
        half = 1 - half if other else half
        cut = pl.ds(pl.multiple_of(half * n, QB), n)
        copies = [
            pltpu.make_async_copy(w_ref.at[e, cut, :], o_ref.at[e], sems.at[e])
            for e in range(experts)
        ]
        for copy in copies:
            copy.start()
        t_ref[...] = jnp.zeros_like(t_ref)
        for copy in copies:
            copy.wait()

    return pl.pallas_call(
        kernel,
        out_shape=[pltpu.VMEM((experts, n, width), BF), sds((8, LANES), F32)],
        in_specs=[HB, VM],
        out_specs=[VM, VM],
        scratch_shapes=[pltpu.SemaphoreType.DMA((experts,))],
        compiler_params=pltpu.CompilerParams(vmem_limit_bytes=1 << 20),
        cost_estimate=pl.CostEstimate(
            flops=0, bytes_accessed=moved_bytes(experts, n, width), transcendentals=0
        ),
        name="half_rows",
    )(in_hbm(w), after)


def dispatch(x, width, top, rows_dev, experts, slots):
    rows = x.shape[0]
    per = slots // experts
    meta = x[:, width:].astype(F32)
    base = (lax.axis_index("seq") * experts).astype(F32)
    lane = iota((rows, LANES), 1)
    named = jnp.where(lane < experts, lane, -LANES).astype(F32) + base
    hits = jnp.zeros((rows, LANES), F32)
    gates = jnp.zeros((rows, LANES), F32)
    total = jnp.zeros((rows, 1), F32)
    for k in range(top):
        gate = meta[:, top + k : top + k + 1] * 256.0 + meta[:, 2 * top + k : 2 * top + k + 1]
        equal = meta[:, k : k + 1] == named
        hits = hits + jnp.where(equal, 1.0, 0.0)
        gates = gates + jnp.where(equal, gate, 0.0)
        total = total + gate
    weights = gates / total
    r0, r1 = iota((rows, rows), 0), iota((rows, rows), 1)
    earlier = ((r0 // rows_dev == r1 // rows_dev) & (r1 < r0)).astype(BF)
    rank = jnp.dot(earlier, hits.astype(BF), preferred_element_type=F32)
    grow = (iota((LANES, slots), 1) // per == iota((LANES, slots), 0)).astype(BF)
    wide_hits = jnp.dot(hits.astype(BF), grow, preferred_element_type=F32)
    wide_rank = jnp.dot(rank.astype(BF), grow, preferred_element_type=F32)
    spot = (iota((rows, slots), 1) % per - (iota((rows, slots), 0) // rows_dev) * CAP).astype(F32)
    sel = jnp.where((wide_hits > 0.5) & (wide_rank == spot), 1.0, 0.0).astype(BF)
    slot_rows = lax.dot_general(
        sel, x[:, :width], (((0,), (0,)), ((), ())), preferred_element_type=F32
    ).astype(BF)
    return sel, weights, slot_rows


def tile(parts):
    return jnp.concatenate([jnp.concatenate(row, axis=1) for row in parts], axis=0)


def scaled(block, scale, a, b, e):
    row = jnp.broadcast_to(scale[a, b, e : e + 1, :], (16, LANES)).astype(BF)
    return (block.reshape(QB // 16, 16, QB) * row[None]).reshape(QB, QB)


def half_products(xs_ref, half, n, place, scales, o_ref, order, before):
    width = xs_ref.shape[1]
    per = xs_ref.shape[0] // len(order)
    columns = [(0, j) for j in range(n)] + [(1, j) for j in range(n)]
    starts = [pl.multiple_of((half * n + j) * QB, QB) for j in range(n)]
    group, deep = 2, 2

    def block(m, e, j, q):
        ref, at, whole = place[m, e]
        cut = pl.ds(starts[j] if whole else j * QB, QB)
        return scaled(ref[at, q * QB : (q + 1) * QB, cut], scales[m], half * n + j, q, e)

    for position, e in enumerate(order):
        before(position)
        xs = xs_ref[e * per : (e + 1) * per, :]
        for at in range(0, len(columns), group):
            acc = jnp.zeros((per, group * QB), F32)
            for d in range(0, width // QB, deep):
                rhs = tile(
                    [[block(m, e, j, q) for m, j in columns[at : at + group]] for q in range(d, d + deep)]
                )
                acc = acc + jnp.dot(
                    xs[:, d * QB : (d + deep) * QB], rhs, preferred_element_type=F32
                )
            o_ref[e * per : (e + 1) * per, at * QB : (at + group) * QB] = acc.astype(o_ref.dtype)


AHEAD = 3


def other_half(x, gw, uw, gs, us, held, held_at, top, rows_dev, block_count):
    experts, width, hidden = gw.shape
    n = hidden // 2 // QB
    slots = experts * block_count * CAP
    rows = block_count * rows_dev
    order = [e for e in range(experts) if (0, e) in held_at]
    kept = len(order)
    order += [e for e in range(experts) if (0, e) not in held_at]
    streamed = [(m, e) for e in order[kept:] for m in (0, 1)]
    count = len(streamed)

    def kernel(x_ref, gw_ref, uw_ref, gs_ref, us_ref, *rest):
        held_refs, rest = rest[: len(held)], rest[len(held) :]
        o_ref, xs_ref, sel_ref, wt_ref, next_ref, buf, sems = rest
        own = lax.rem(lax.axis_index("pool"), 2)

        def copies(half, to, first):
            cut = pl.ds(pl.multiple_of(half * (n * QB), QB), n * QB)
            return [
                pltpu.make_async_copy((gw_ref, uw_ref)[m].at[e, :, cut], to.at[i], sems.at[first + i])
                for i, (m, e) in enumerate(streamed)
            ]

        now, later = copies(1 - own, buf, 0), copies(own, next_ref, count)
        place = {key: (held_refs[ref], at, True) for key, (ref, at) in held_at.items()}
        place.update({key: (buf, i, False) for i, key in enumerate(streamed)})
        due = {}
        for i in range(len(order) - kept):
            due.setdefault(max(-1, kept + i - AHEAD - 1), []).extend(now[2 * i : 2 * i + 2])
        spot = max(-1, len(order) - AHEAD - 1)
        due.setdefault(spot, []).extend(later)

        def before(position):
            for copy in due.get(position, []):
                copy.start()
            i = position - kept
            if i >= 0:
                for copy in now[2 * i : 2 * i + 2]:
                    copy.wait()

        before(-1)
        sel, weights, slot_rows = dispatch(x_ref[...], width, top, rows_dev, experts, slots)
        sel_ref[...] = sel
        wt_ref[...] = weights
        xs_ref[...] = slot_rows
        half_products(xs_ref, 1 - own, n, place, (gs_ref, us_ref), o_ref, order, before)
        for copy in later:
            copy.wait()

    result = run(
        kernel,
        [
            sds((slots, hidden), BF),
            sds((slots, width), BF),
            sds((rows, slots), BF),
            sds((rows, LANES), F32),
            pltpu.VMEM((max(1, count), width, hidden // 2), BF),
        ],
        [VM, HB, HB, VM, VM] + [VM] * len(held),
        (x, in_hbm(gw), in_hbm(uw), gs, us, *[in_vmem(h) for h in held]),
        "other_half",
        limit=16 << 20,
        flops=2 * slots * width * hidden,
        bytes_=2 * experts * width * hidden,
        scratch_shapes=[
            pltpu.VMEM((max(1, count), width, hidden // 2), BF),
            pltpu.SemaphoreType.DMA((max(1, 2 * count),)),
        ],
    )
    return result, {key: i for i, key in enumerate(streamed)}


def own_half(xs, gs, us, dw, held, held_at, half_block, half_at, experts):
    slots, width = xs.shape
    hidden, out_width = dw.shape[1:]
    n = hidden // 2 // QB

    def kernel(xs_ref, gs_ref, us_ref, dw_ref, half_ref, *rest):
        held_refs, (o_ref, d_ref, sems) = rest[: len(held)], rest[len(held) :]
        own = lax.rem(lax.axis_index("pool"), 2)
        cut = pl.ds(pl.multiple_of(own * (n * QB), QB), n * QB)
        copies = [
            pltpu.make_async_copy(dw_ref.at[e, cut, :], d_ref.at[e], sems.at[e])
            for e in range(experts)
        ]
        for copy in copies:
            copy.start()
        place = {key: (held_refs[ref], at, True) for key, (ref, at) in held_at.items()}
        place.update({key: (half_ref, i, False) for key, i in half_at.items()})
        order = list(range(experts))
        half_products(xs_ref, own, n, place, (gs_ref, us_ref), o_ref, order, lambda _: None)
        for copy in copies:
            copy.wait()

    return run(
        kernel,
        [sds((slots, hidden), F32), pltpu.VMEM((experts, hidden // 2, out_width), BF)],
        [VM, VM, VM, HB, VM] + [VM] * len(held),
        (xs, gs, us, in_hbm(dw), in_vmem(half_block), *[in_vmem(h) for h in held]),
        "own_half",
        limit=8 << 20,
        flops=2 * slots * width * hidden,
        bytes_=2 * experts * width * hidden,
        scratch_shapes=[pltpu.SemaphoreType.DMA((experts,))],
    )


def add_round(own, got):
    def kernel(a_ref, b_ref, o_ref, r_ref):
        total = a_ref[...] + b_ref[...].astype(F32)
        o_ref[...] = total
        r_ref[...] = total.astype(BF)

    return run(kernel, [sds(own.shape, F32), sds(own.shape, BF)], [VM] * 2, (own, got), "add_round")


def activate(own, got, after):
    slots, hidden = own.shape
    n = hidden // 2

    def kernel(a_ref, b_ref, *rest):
        o_ref = rest[-1]
        gate = a_ref[:, :n] + b_ref[:, :n].astype(F32)
        up = a_ref[:, n:] + b_ref[:, n:].astype(F32)
        o_ref[...] = (jax.nn.silu(gate) * up).astype(BF)

    return run(
        kernel,
        sds((slots, n), BF),
        [VM] * (2 + len(after)),
        (own, got, *after),
        "activate",
    )


def spread_rows(h_ref, sel_ref, wt_ref, experts):
    rows, slots = sel_ref.shape
    per = slots // experts
    sel = sel_ref[...].astype(F32)
    owner = iota((rows, slots), 1) // per
    stack = jnp.concatenate([jnp.where(owner == e, sel, 0.0) for e in range(experts)], axis=0)
    spread = jnp.dot(stack.astype(BF), h_ref[...], preferred_element_type=F32)
    weights = wt_ref[...]
    return [
        (spread[e * rows : (e + 1) * rows] * weights[:, e : e + 1]).astype(BF)
        for e in range(experts)
    ]


def down_kernel(hid, sel, wt, dw, ds, own):
    experts, half_hidden, width = dw.shape
    n = half_hidden // QB
    rows = sel.shape[0]
    keep = rows // 2
    last = own is not None
    given = [own] if last else []
    group = 2
    pieces = [(e, j) for e in range(experts) for j in range(n)]
    deep = 2 if len(pieces) % 2 == 0 else 1

    def kernel(h_ref, sel_ref, wt_ref, dw_ref, ds_ref, *rest):
        given_refs, outs = rest[: len(given)], rest[len(given) :]
        half = lax.rem(lax.axis_index("pool"), 2)
        half = 1 - half if last else half
        parts = spread_rows(h_ref, sel_ref, wt_ref, experts)

        def block(e, j, q):
            rows_of, columns = slice(j * QB, (j + 1) * QB), slice(q * QB, (q + 1) * QB)
            return scaled(dw_ref[e, rows_of, columns], ds_ref, half * n + j, q, e)

        for c in range(0, width // QB, group):
            at = slice(c * QB, (c + group) * QB)
            acc = given_refs[0][:, at] if last else jnp.zeros((rows, group * QB), F32)
            for p in range(0, len(pieces), deep):
                some = pieces[p : p + deep]
                lhs = jnp.concatenate([parts[e][:, j * QB : (j + 1) * QB] for e, j in some], axis=1)
                rhs = tile([[block(e, j, q) for q in range(c, c + group)] for e, j in some])
                acc = acc + jnp.dot(lhs, rhs, preferred_element_type=F32)
            if last:
                outs[0][:, at] = acc[:keep]
                outs[1][:, at] = acc[keep:].astype(BF)
            else:
                outs[0][:, at] = acc

    return run(
        kernel,
        [sds((keep, width), F32), sds((rows - keep, width), BF)] if last else [sds((rows, width), F32)],
        [VM] * (5 + len(given)),
        (hid, sel, wt, in_vmem(dw), ds, *given),
        "down_other" if last else "down_own",
        limit=8 << 20,
        flops=experts * rows * width * half_hidden * 2,
        bytes_=experts * width * half_hidden * 2,
    )


def fold(own, got):
    rows, width = own.shape
    keep = rows // 2

    def kernel(a_ref, b_ref, o_ref, s_ref):
        o_ref[...] = a_ref[:keep] + b_ref[:keep].astype(F32)
        s_ref[...] = (a_ref[keep:] + b_ref[keep:].astype(F32)).astype(BF)

    return run(
        kernel, [sds((keep, width), F32), sds((keep, width), BF)], [VM] * 2, (own, got), "fold"
    )


def finish(own, got):
    def kernel(a_ref, b_ref, o_ref):
        o_ref[...] = (a_ref[...] + b_ref[...].astype(F32)).astype(BF)

    return run(kernel, sds(own.shape, BF), [VM] * 2, (own, got), "finish")


def swap(x, axis, bit):
    return lax.ppermute(x, axis, [(j, j ^ bit) for j in range(lax.axis_size(axis))])


def bits(count):
    return [1 << i for i in range(count.bit_length() - 1)]


def per_device(tokens, routes, gate_fixed, gw, uw, dw, gs, us, ds):
    n_seq, n_head, n_pool = (lax.axis_size(a) for a in ("seq", "head", "pool"))
    rows_dev, width = tokens.shape
    top = routes.shape[1]
    hops = [("head", b) for b in reversed(bits(n_head))] + [("seq", b) for b in bits(n_seq)]

    experts = gw.shape[0]
    x = pack(tokens, routes, gate_fixed)
    scales = [gs.transpose(2, 0, 1), us.transpose(2, 0, 1), ds.transpose(1, 0, 2)]
    waiting = [(m, e) for e in range(experts * 3 // 8) for m in (0, 1)]
    held, held_at, spread = [], {}, []
    for i, (axis, bit) in enumerate(hops):
        got = swap(x, axis, bit)
        take = -(-len(waiting) // (len(hops) - i))
        after = []
        if take or scales:
            use, waiting = waiting[:take], waiting[take:]
            blocks, rows, token = load([((gw, uw)[m], e) for m, e in use], scales, x)
            held_at.update({key: (len(held), at) for at, key in enumerate(use)})
            held += blocks
            spread += rows
            scales = []
            after = [token]
        x = cat(x, got, after)
    gs, us, ds = spread

    (send, xs, sel, wt, half_block), half_at = other_half(
        x, gw, uw, gs, us, held, held_at, top, rows_dev, n_seq * n_head
    )
    got = swap(send, "pool", 1)
    own, dw_own = own_half(xs, gs, us, dw, held, held_at, half_block, half_at, experts)
    after = []
    for bit in bits(n_pool)[1:]:
        own, send = add_round(own, got)
        got = swap(send, "pool", bit)
        if not after:
            dw_other, token = half_rows(dw, True, send)
            after = [token]
    if not after:
        dw_other, token = half_rows(dw, True, own)
        after = [token]
    hid = activate(own, got, after)
    other = swap(hid, "pool", 1)
    (acc,) = down_kernel(hid, sel, wt, dw_own, ds, None)
    acc, send = down_kernel(other, sel, wt, dw_other, ds, acc)
    for axis, bit in reversed(hops[1:]):
        acc, send = fold(acc, swap(send, axis, bit))
    axis, bit = hops[0]
    return finish(acc, swap(send, axis, bit))


def solution(mesh):
    return jax.shard_map(
        per_device,
        mesh=mesh,
        in_specs=(
            P(("seq", "head"), "pool"),
            P(("seq", "head"), None),
            P(("seq", "head"), None),
            P("seq", "pool", "head"),
            P("seq", "pool", "head"),
            P("seq", "head", "pool"),
            P("seq", "pool", "head"),
            P("seq", "pool", "head"),
            P("seq", "head", "pool"),
        ),
        out_specs=P(("seq", "head"), "pool"),
        check_vma=False,
    )
```

time: 55 us -> 49.5 us (0.900)
  Pallas kernels: 30.6 us -> 23.9 us
  starting transfers between devices: 14.1 us -> 14.8 us
    pallas_call x13, Pallas kernels: 20.2 us -> 15.3 us  [run(): pl.pallas_call(kernel, out_shape=out_shape, in_specs=in_specs, out_specs=...]
    pallas_call x4, Pallas kernels: 10.4 us -> 8.63 us  [the longest x3 5.77 us: load(): pl.pallas_call(kernel, out_shape=outs + spread + [sds((8, LANES), F32)],...]
    ppermute x9, starting transfers between devices: 14.1 us -> 14.8 us  [swap(): lax.ppermute(x, axis, [(j, j ^ bit) for j in range(lax.axis_size(axis))])]
  transfers between devices with their start and end apart: 9 -> 9, of which waited for: 5 -> 6; matrix products, arithmetic and copies ran while one was open for 0% -> 0% of each run, Pallas kernels for 35% -> 28%
where the time goes in v3:
time: 49.5 us; the launch traced here: 49.2 us
  Pallas kernels  23.9 us (48%)
  starting transfers between devices  14.8 us (30%)
  waiting for transfers between devices  10.4 us (21%)
    pallas_call x13, Pallas kernels, run(): pl.pallas_call(kernel, out_shape=out_shape, in_specs=in_specs, out_specs=...  15.3 us
    ppermute x9, starting transfers between devices, swap(): lax.ppermute(x, axis, [(j, j ^ bit) for j in range(lax.axis_size(axis))])  14.8 us
    ppermute x9, waiting for transfers between devices, swap(): lax.ppermute(x, axis, [(j, j ^ bit) for j in range(lax.axis_size(axis))])  10.4 us
    pallas_call x3, Pallas kernels, load(): pl.pallas_call(kernel, out_shape=outs + spread + [sds((8, LANES), F32)],...  5.77 us
    pallas_call x1, Pallas kernels, half_rows(): pl.pallas_call(kernel, out_shape=[pltpu.VMEM((experts, n, width), BF), sd...  2.86 us
  transfers between devices with their start and end apart: 9, of which 6 were waited for; matrix products, arithmetic and copies ran while one was open for 0% of the time, Pallas kernels for 28%

profile of v3, /device:TPU:0, one launch (start us, length us, event | category | flops | bytes accessed | tf_op | source)
XLA Modules:
  0.0 49.2 jit_solution(17743620555282177611)
XLA Ops:
  0.0 0.9 %pack.1.refs_5_.a_ref = bf16[4,1152]{1,0:T(4,128)(2,1)S(1)} custom-call(bf16[4,1024]{1,0:T(4,128)(2,1)} %t_in.1, s32[4,8]{1,0:T(4,128)} %r_in.1, s32[4,8]{1,0:T(4,128)} %g_in.1), custom_call_target="tpu_custom_call" | custom-call | tf_op jit(solution)/shard_map/pack/pallas_call | solution.py:28
  0.9 4.1 %collective-permute-start = (bf16[4,1152]{1,0:T(4,128)(2,1)S(1)}, bf16[4,1152]{1,0:T(4,128)(2,1)S(1)}, u32[]{:S(2)}, u32[]{:S(2)}) collective-permute-start(bf16[4,1152]{1,0:T(4,128)(2,1)S(1)} %pack.1.refs_5_.a_ref), channel_id=1, source_target_pairs={{0,8},{4,12},{8,0},{12,4},{1,9},{5,13},{9,1},{13,5},{2,10},{6,14},... | collective-permute-start | bytes 27656 | tf_op jit(solution)/shard_map/ppermute | solution.py:487
  5.0 2.0 %load.3 = (bf16[2,1024,768]{2,1,0:T(8,128)(2,1)S(1)}, f32[6,8,8,128]{3,2,1,0:T(8,128)S(1)}, f32[6,8,8,128]{3,2,1,0:T(8,128)S(1)}, f32[6,8,8,128]{3,2,1,0:T(8,128)S(1)}, f32[8,128]{1,0:T(8,128)S(1)}) custom-call(bf16[8,1024,768]{2,1,0:T(8,128)(2,1)} %gw_ref.1, bf16[8,1024,768]{2,1,0:T(8,128)(2,1)} %uw_ref.1, bf16[6,8,8]{2,1,0:T(8,128)(2,1)} %bitcast.3, ...), custom_call_target="tpu_custom_call" | custom-call | bytes 7340032 | tf_op jit(solution)/shard_map/load/pallas_call | solution.py:152
  7.0 0.0 collective-permute-done.b_ref
  7.0 1.6 %collective-permute-start.1 = (bf16[8,1152]{1,0:T(8,128)(2,1)S(1)}, bf16[8,1152]{1,0:T(8,128)(2,1)S(1)}, u32[]{:S(2)}, u32[]{:S(2)}) collective-permute-start(bf16[8,1152]{1,0:T(8,128)(2,1)S(1)} %cat.3.refs_2_.a_ref), channel_id=1, source_target_pairs={{0,4},{4,0},{8,12},{12,8},{1,5},{5,1},{9,13},{13,9},{2,6},{6,2},{1... | collective-permute-start | bytes 55304 | tf_op jit(solution)/shard_map/ppermute | solution.py:487
  8.7 1.9 %load.4 = (bf16[2,1024,768]{2,1,0:T(8,128)(2,1)S(1)}, f32[8,128]{1,0:T(8,128)S(1)}) custom-call(bf16[8,1024,768]{2,1,0:T(8,128)(2,1)} %gw_ref.1, bf16[8,1024,768]{2,1,0:T(8,128)(2,1)} %uw_ref.1, bf16[8,1152]{1,0:T(8,128)(2,1)S(1)} %cat.3.refs_2_.a_ref), custom_call_target="tpu_custom_call" | custom-call | bytes 7340032 | tf_op jit(solution)/shard_map/load/pallas_call | solution.py:152
  10.6 0.3 collective-permute-done.1.b_ref
  10.9 1.5 %collective-permute-start.2 = (bf16[16,1152]{1,0:T(8,128)(2,1)S(1)}, bf16[16,1152]{1,0:T(8,128)(2,1)S(1)}, u32[]{:S(2)}, u32[]{:S(2)}) collective-permute-start(bf16[16,1152]{1,0:T(8,128)(2,1)S(1)} %cat.4.refs_2_.a_ref), channel_id=1, source_target_pairs={{0,16},{16,0},{1,17},{17,1},{2,18},{18,2},{3,19},{19,3},{4,20},{20... | collective-permute-start | bytes 110600 | tf_op jit(solution)/shard_map/ppermute | solution.py:487
  12.4 1.9 %load.5 = (bf16[2,1024,768]{2,1,0:T(8,128)(2,1)S(1)}, f32[8,128]{1,0:T(8,128)S(1)}) custom-call(bf16[8,1024,768]{2,1,0:T(8,128)(2,1)} %gw_ref.1, bf16[8,1024,768]{2,1,0:T(8,128)(2,1)} %uw_ref.1, bf16[16,1152]{1,0:T(8,128)(2,1)S(1)} %cat.4.refs_2_.a_ref), custom_call_target="tpu_custom_call" | custom-call | bytes 7340032 | tf_op jit(solution)/shard_map/load/pallas_call | solution.py:152
  14.3 0.6 %collective-permute-done.2.b_ref = bf16[16,1152]{1,0:T(8,128)(2,1)S(1)} collective-permute-done((bf16[16,1152]{1,0:T(8,128)(2,1)S(1)}, bf16[16,1152]{1,0:T(8,128)(2,1)S(1)}, u32[]{:S(2)}, u32[]{:S(2)}) %collective-permute-start.2) | collective-permute-done | bytes 36896 | tf_op jit(solution)/shard_map/ppermute | solution.py:487
  14.8 7.0 %other_half.1 = (bf16[128,768]{1,0:T(8,128)(2,1)S(1)}, bf16[128,1024]{1,0:T(8,128)(2,1)S(1)}, bf16[32,128]{1,0:T(8,128)(2,1)S(1)}, f32[32,128]{1,0:T(8,128)S(1)}, bf16[10,1024,384]{2,1,0:T(8,128)(2,1)S(1)}) custom-call(bf16[32,1152]{1,0:T(8,128)(2,1)S(1)} %cat.5.x_ref, bf16[8,1024,768]{2,1,0:T(8,128)(2,1)} %gw_ref.1, bf16[8,1024,768]{2,1,0:T(8,128)(2,1)} %uw_ref.1, ...), custom_call_target="tpu_custom_call" | custom-call | flops 201326592 | bytes 12582912 | tf_op jit(solution)/shard_map/other_half/pallas_call | solution.py:28
  21.8 0.1 collective-permute-start.3
  21.9 4.0 %own_half.1 = (f32[128,768]{1,0:T(8,128)S(1)}, bf16[8,384,1024]{2,1,0:T(8,128)(2,1)S(1)}) custom-call(bf16[128,1024]{1,0:T(8,128)(2,1)S(1)} %get-tuple-element.39.xs_ref, f32[6,8,8,128]{3,2,1,0:T(8,128)S(1)} %get-tuple-element.34.gs_ref, f32[6,8,8,128]{3,2,1,0:T(8,128)S(1)} %get-tuple-element.35.us_ref, bf16[8,768,1024]{2,1,0:T(8,128)(2,1)} %w_ref.1, ...), custom_call_target="tpu_custom_call" | custom-call | flops 201326592 | bytes 12582912 | tf_op jit(solution)/shard_map/own_half/pallas_call | solution.py:28
  25.9 0.0 collective-permute-done.3.b_ref
  25.9 0.1 add_round.1
  25.9 1.6 %collective-permute-start.4 = (bf16[128,768]{1,0:T(8,128)(2,1)S(1)}, bf16[128,768]{1,0:T(8,128)(2,1)S(1)}, u32[]{:S(2)}, u32[]{:S(2)}) collective-permute-start(bf16[128,768]{1,0:T(8,128)(2,1)S(1)} %get-tuple-element.44._), channel_id=1, source_target_pairs={{0,2},{1,3},{2,0},{3,1},{4,6},{5,7},{6,4},{7,5},{8,10},{9,11},{10,... | collective-permute-start | bytes 589832 | tf_op jit(solution)/shard_map/ppermute | solution.py:487
  27.5 2.9 %half_rows.1 = (bf16[8,384,1024]{2,1,0:T(8,128)(2,1)S(1)}, f32[8,128]{1,0:T(8,128)S(1)}) custom-call(bf16[8,768,1024]{2,1,0:T(8,128)(2,1)} %w_ref.1, bf16[128,768]{1,0:T(8,128)(2,1)S(1)} %get-tuple-element.44._), custom_call_target="tpu_custom_call" | custom-call | bytes 12582912 | tf_op jit(solution)/shard_map/half_rows/pallas_call | solution.py:186
  30.4 2.9 %collective-permute-done.4.b_ref = bf16[128,768]{1,0:T(8,128)(2,1)S(1)} collective-permute-done((bf16[128,768]{1,0:T(8,128)(2,1)S(1)}, bf16[128,768]{1,0:T(8,128)(2,1)S(1)}, u32[]{:S(2)}, u32[]{:S(2)}) %collective-permute-start.4) | collective-permute-done | bytes 196640 | tf_op jit(solution)/shard_map/ppermute | solution.py:487
  33.3 0.1 activate.1.h_ref
  33.4 0.1 collective-permute-start.5
  33.4 1.3 %down_own.1.rest_0_ = f32[32,1024]{1,0:T(8,128)S(1)} custom-call(bf16[128,384]{1,0:T(8,128)(2,1)S(1)} %activate.1.h_ref, bf16[32,128]{1,0:T(8,128)(2,1)S(1)} %get-tuple-element.46.sel_ref, f32[32,128]{1,0:T(8,128)S(1)} %get-tuple-element.47.wt_ref, bf16[8,384,1024]{2,1,0:T(8,128)(2,1)S(1)} %get-tuple-element.50.dw_ref, ...), custom_call_target="tpu_custom_call" | custom-call | flops 201326592 | bytes 6291456 | tf_op jit(solution)/shard_map/down_own/pallas_call | solution.py:28
  34.8 0.0 collective-permute-done.5.h_ref
  34.8 1.3 %down_other.1 = (f32[16,1024]{1,0:T(8,128)S(1)}, bf16[16,1024]{1,0:T(8,128)(2,1)S(1)}) custom-call(bf16[128,384]{1,0:T(8,128)(2,1)S(1)} %collective-permute-done.5.h_ref, bf16[32,128]{1,0:T(8,128)(2,1)S(1)} %get-tuple-element.46.sel_ref, f32[32,128]{1,0:T(8,128)S(1)} %get-tuple-element.47.wt_ref, bf16[8,384,1024]{2,1,0:T(8,128)(2,1)S(1)} %get-tuple-element.48.dw_ref, ...), custom_call_target="tpu_custom_call" | custom-call | flops 201326592 | bytes 6291456 | tf_op jit(solution)/shard_map/down_other/pallas_call | solution.py:28
  36.1 1.6 %collective-permute-start.6 = (bf16[16,1024]{1,0:T(8,128)(2,1)S(1)}, bf16[16,1024]{1,0:T(8,128)(2,1)S(1)}, u32[]{:S(2)}, u32[]{:S(2)}) collective-permute-start(bf16[16,1024]{1,0:T(8,128)(2,1)S(1)} %get-tuple-element.52), channel_id=1, source_target_pairs={{0,16},{16,0},{1,17},{17,1},{2,18},{18,2},{3,19},{19,3},{4,20},{20... | collective-permute-start | bytes 98312 | tf_op jit(solution)/shard_map/ppermute | solution.py:487
  37.7 2.4 %collective-permute-done.6.b_ref = bf16[16,1024]{1,0:T(8,128)(2,1)S(1)} collective-permute-done((bf16[16,1024]{1,0:T(8,128)(2,1)S(1)}, bf16[16,1024]{1,0:T(8,128)(2,1)S(1)}, u32[]{:S(2)}, u32[]{:S(2)}) %collective-permute-start.6) | collective-permute-done | bytes 32800 | tf_op jit(solution)/shard_map/ppermute | solution.py:487
  40.1 1.6 %collective-permute-start.7 = (bf16[8,1024]{1,0:T(8,128)(2,1)S(1)}, bf16[8,1024]{1,0:T(8,128)(2,1)S(1)}, u32[]{:S(2)}, u32[]{:S(2)}) collective-permute-start(bf16[8,1024]{1,0:T(8,128)(2,1)S(1)} %get-tuple-element.54), channel_id=1, source_target_pairs={{0,4},{4,0},{8,12},{12,8},{1,5},{5,1},{9,13},{13,9},{2,6},{6,2},{1... | collective-permute-start | bytes 49160 | tf_op jit(solution)/shard_map/ppermute | solution.py:487
  41.8 2.2 %collective-permute-done.7.b_ref = bf16[8,1024]{1,0:T(8,128)(2,1)S(1)} collective-permute-done((bf16[8,1024]{1,0:T(8,128)(2,1)S(1)}, bf16[8,1024]{1,0:T(8,128)(2,1)S(1)}, u32[]{:S(2)}, u32[]{:S(2)}) %collective-permute-start.7) | collective-permute-done | bytes 16416 | tf_op jit(solution)/shard_map/ppermute | solution.py:487
  43.9 2.6 %collective-permute-start.8 = (bf16[4,1024]{1,0:T(4,128)(2,1)S(1)}, bf16[4,1024]{1,0:T(4,128)(2,1)S(1)}, u32[]{:S(2)}, u32[]{:S(2)}) collective-permute-start(bf16[4,1024]{1,0:T(4,128)(2,1)S(1)} %get-tuple-element.56), channel_id=1, source_target_pairs={{0,8},{4,12},{8,0},{12,4},{1,9},{5,13},{9,1},{13,5},{2,10},{6,14},... | collective-permute-start | bytes 24584 | tf_op jit(solution)/shard_map/ppermute | solution.py:487
  46.5 2.1 %collective-permute-done.8.b_ref = bf16[4,1024]{1,0:T(4,128)(2,1)S(1)} collective-permute-done((bf16[4,1024]{1,0:T(4,128)(2,1)S(1)}, bf16[4,1024]{1,0:T(4,128)(2,1)S(1)}, u32[]{:S(2)}, u32[]{:S(2)}) %collective-permute-start.8) | collective-permute-done | bytes 8224 | tf_op jit(solution)/shard_map/ppermute | solution.py:487
  48.6 0.6 %finish.1 = bf16[4,1024]{1,0:T(4,128)(2,1)} custom-call(f32[4,1024]{1,0:T(4,128)S(1)} %get-tuple-element.55.a_ref, bf16[4,1024]{1,0:T(4,128)(2,1)S(1)} %collective-permute-done.8.b_ref), custom_call_target="tpu_custom_call" | custom-call | tf_op jit(solution)/shard_map/finish/pallas_call | solution.py:28
  (5 shorter events, 0.0 us)
Async XLA Ops:
  0.9 6.1 %collective-permute-start = (bf16[4,1152]{1,0:T(4,128)(2,1)S(1)}, bf16[4,1152]{1,0:T(4,128)(2,1)S(1)}, u32[]{:S(2)}, u32[]{:S(2)}) collective-permute-start(bf16[4,1152]{1,0:T(4,128)(2,1)S(1)} %pack.1.refs_5_.a_ref), channel_id=1, source_target_pairs={{0,8},{4,12},{8,0},{12,4},{1,9},{5,13},{9,1},{13,5},{2,10},{6,14},... | collective-permute-start | bytes 27656 | tf_op jit(solution)/shard_map/ppermute | solution.py:487
  7.0 3.8 %collective-permute-start.1 = (bf16[8,1152]{1,0:T(8,128)(2,1)S(1)}, bf16[8,1152]{1,0:T(8,128)(2,1)S(1)}, u32[]{:S(2)}, u32[]{:S(2)}) collective-permute-start(bf16[8,1152]{1,0:T(8,128)(2,1)S(1)} %cat.3.refs_2_.a_ref), channel_id=1, source_target_pairs={{0,4},{4,0},{8,12},{12,8},{1,5},{5,1},{9,13},{13,9},{2,6},{6,2},{1... | collective-permute-start | bytes 55304 | tf_op jit(solution)/shard_map/ppermute | solution.py:487
  10.9 4.0 %collective-permute-start.2 = (bf16[16,1152]{1,0:T(8,128)(2,1)S(1)}, bf16[16,1152]{1,0:T(8,128)(2,1)S(1)}, u32[]{:S(2)}, u32[]{:S(2)}) collective-permute-start(bf16[16,1152]{1,0:T(8,128)(2,1)S(1)} %cat.4.refs_2_.a_ref), channel_id=1, source_target_pairs={{0,16},{16,0},{1,17},{17,1},{2,18},{18,2},{3,19},{19,3},{4,20},{20... | collective-permute-start | bytes 110600 | tf_op jit(solution)/shard_map/ppermute | solution.py:487
  21.8 4.1 %collective-permute-start.3 = (bf16[128,768]{1,0:T(8,128)(2,1)S(1)}, bf16[128,768]{1,0:T(8,128)(2,1)S(1)}, u32[]{:S(2)}, u32[]{:S(2)}) collective-permute-start(bf16[128,768]{1,0:T(8,128)(2,1)S(1)} %get-tuple-element.42), channel_id=1, source_target_pairs={{0,1},{1,0},{2,3},{3,2},{4,5},{5,4},{6,7},{7,6},{8,9},{9,8},{10,11... | collective-permute-start | bytes 589832 | tf_op jit(solution)/shard_map/ppermute | solution.py:487
  25.9 7.3 %collective-permute-start.4 = (bf16[128,768]{1,0:T(8,128)(2,1)S(1)}, bf16[128,768]{1,0:T(8,128)(2,1)S(1)}, u32[]{:S(2)}, u32[]{:S(2)}) collective-permute-start(bf16[128,768]{1,0:T(8,128)(2,1)S(1)} %get-tuple-element.44._), channel_id=1, source_target_pairs={{0,2},{1,3},{2,0},{3,1},{4,6},{5,7},{6,4},{7,5},{8,10},{9,11},{10,... | collective-permute-start | bytes 589832 | tf_op jit(solution)/shard_map/ppermute | solution.py:487
  33.4 1.4 %collective-permute-start.5 = (bf16[128,384]{1,0:T(8,128)(2,1)S(1)}, bf16[128,384]{1,0:T(8,128)(2,1)S(1)}, u32[]{:S(2)}, u32[]{:S(2)}) collective-permute-start(bf16[128,384]{1,0:T(8,128)(2,1)S(1)} %activate.1.h_ref), channel_id=1, source_target_pairs={{0,1},{1,0},{2,3},{3,2},{4,5},{5,4},{6,7},{7,6},{8,9},{9,8},{10,11... | collective-permute-start | bytes 294920 | tf_op jit(solution)/shard_map/ppermute | solution.py:487
  36.1 4.0 %collective-permute-start.6 = (bf16[16,1024]{1,0:T(8,128)(2,1)S(1)}, bf16[16,1024]{1,0:T(8,128)(2,1)S(1)}, u32[]{:S(2)}, u32[]{:S(2)}) collective-permute-start(bf16[16,1024]{1,0:T(8,128)(2,1)S(1)} %get-tuple-element.52), channel_id=1, source_target_pairs={{0,16},{16,0},{1,17},{17,1},{2,18},{18,2},{3,19},{19,3},{4,20},{20... | collective-permute-start | bytes 98312 | tf_op jit(solution)/shard_map/ppermute | solution.py:487
  40.1 3.8 %collective-permute-start.7 = (bf16[8,1024]{1,0:T(8,128)(2,1)S(1)}, bf16[8,1024]{1,0:T(8,128)(2,1)S(1)}, u32[]{:S(2)}, u32[]{:S(2)}) collective-permute-start(bf16[8,1024]{1,0:T(8,128)(2,1)S(1)} %get-tuple-element.54), channel_id=1, source_target_pairs={{0,4},{4,0},{8,12},{12,8},{1,5},{5,1},{9,13},{13,9},{2,6},{6,2},{1... | collective-permute-start | bytes 49160 | tf_op jit(solution)/shard_map/ppermute | solution.py:487
  43.9 4.6 %collective-permute-start.8 = (bf16[4,1024]{1,0:T(4,128)(2,1)S(1)}, bf16[4,1024]{1,0:T(4,128)(2,1)S(1)}, u32[]{:S(2)}, u32[]{:S(2)}) collective-permute-start(bf16[4,1024]{1,0:T(4,128)(2,1)S(1)} %get-tuple-element.56), channel_id=1, source_target_pairs={{0,8},{4,12},{8,0},{12,4},{1,9},{5,13},{9,1},{13,5},{2,10},{6,14},... | collective-permute-start | bytes 24584 | tf_op jit(solution)/shard_map/ppermute | solution.py:487

commit v4 on v1

v4 whole, which is shorter than its diff:
```python
import functools

import jax
import jax.numpy as jnp
from jax import lax
from jax.experimental import pallas as pl
from jax.experimental.pallas import tpu as pltpu
from jax.sharding import PartitionSpec as P

QB = 128
CAP = 2
HINT = 1000
NEAR = 1 << 16
LANES = 128
BF = jnp.bfloat16
F32 = jnp.float32
I32 = jnp.int32

VM = pl.BlockSpec(memory_space=pltpu.VMEM)
HB = pl.BlockSpec(memory_space=pltpu.HBM)


def sds(shape, dtype):
    return jax.ShapeDtypeStruct(shape, dtype)


def run(kernel, out_shape, in_specs, args, name, limit=2 << 20, flops=0, bytes_=0, **more):
    outs = out_shape if isinstance(out_shape, (list, tuple)) else [out_shape]
    specs = [VM] * len(outs)
    return pl.pallas_call(
        kernel,
        out_shape=out_shape,
        in_specs=in_specs,
        out_specs=specs if isinstance(out_shape, (list, tuple)) else VM,
        compiler_params=pltpu.CompilerParams(vmem_limit_bytes=limit),
        cost_estimate=pl.CostEstimate(flops=flops, bytes_accessed=bytes_, transcendentals=0),
        name=name,
        **more,
    )(*args)


def in_hbm(a):
    return pltpu.with_memory_space_constraint(a, pltpu.HBM)


def in_vmem(a):
    return pltpu.with_memory_space_constraint(a, pltpu.VMEM)


def iota(shape, dim):
    return lax.broadcasted_iota(I32, shape, dim)


def placed(values, start):
    n = values.shape[1]
    spot = (iota((n, LANES), 1) == iota((n, LANES), 0) + start).astype(BF)
    return jnp.dot(values.astype(F32).astype(BF), spot, preferred_element_type=F32)


def pack(tokens, routes, gates, hint):
    rows, width = tokens.shape
    top = routes.shape[1]

    def kernel(t_in, r_in, g_in, x_out, t_v, r_v, g_v, sems):
        copies = [
            pltpu.make_async_copy(src, dst, sems.at[i])
            for i, (src, dst) in enumerate(((r_in, r_v), (g_in, g_v), (t_in, t_v)))
        ]
        for copy in copies:
            copy.start()
        for copy in copies:
            copy.wait()
        x_out[:, :width] = t_v[...]
        gate = g_v[...]
        meta = (
            placed(r_v[...], 0)
            + placed(lax.shift_right_logical(gate, 8), top)
            + placed(gate & 255, 2 * top)
        )
        x_out[:, width:] = meta.astype(BF)

    arrays = [in_hbm(a) for a in (tokens, routes, gates)]
    return run(
        kernel,
        sds((rows, width + LANES), BF),
        [HB] * len(arrays),
        arrays,
        "pack",
        flops=hint,
        scratch_shapes=[pltpu.VMEM(a.shape, a.dtype) for a in arrays]
        + [pltpu.SemaphoreType.DMA((len(arrays),))],
    )


def cat(a, b, after):
    rows = a.shape[0]

    def kernel(a_ref, b_ref, *rest):
        o_ref = rest[-1]
        o_ref[:rows] = a_ref[...]
        o_ref[rows:] = b_ref[...]

    return run(
        kernel,
        sds((2 * rows,) + a.shape[1:], a.dtype),
        [VM] * (2 + len(after)),
        (a, b, *after),
        "cat",
    )


def spread_scales(scales, after):
    def kernel(*refs):
        count = len(scales)
        ins, outs, held, sems = refs[:count], refs[count + 1 : 2 * count + 1], refs[2 * count + 1 : -1], refs[-1]
        copies = [
            pltpu.make_async_copy(src, dst, sems.at[i]) for i, (src, dst) in enumerate(zip(ins, held))
        ]
        for copy in copies:
            copy.start()
        for copy, src, dst in zip(copies, held, outs):
            copy.wait()
            for a in range(src.shape[0]):
                values = src[a].astype(F32)
                for b in range(src.shape[2]):
                    dst[a, b] = jnp.broadcast_to(values[:, b : b + 1], dst.shape[2:])

    return run(
        kernel,
        [sds((s.shape[0], s.shape[2], s.shape[1], LANES), F32) for s in scales],
        [HB] * len(scales) + [VM],
        (*[in_hbm(s) for s in scales], after),
        "spread_scales",
        bytes_=1 << 20,
        scratch_shapes=[pltpu.VMEM(s.shape, s.dtype) for s in scales]
        + [pltpu.SemaphoreType.DMA((len(scales),))],
    )


def dispatch(x, width, top, rows_dev, experts, slots):
    rows = x.shape[0]
    per = slots // experts
    meta = x[:, width:].astype(F32)
    base = (lax.axis_index("seq") * experts).astype(F32)
    lane = iota((rows, LANES), 1)
    named = jnp.where(lane < experts, lane, -LANES).astype(F32) + base
    hits = jnp.zeros((rows, LANES), F32)
    gates = jnp.zeros((rows, LANES), F32)
    total = jnp.zeros((rows, 1), F32)
    for k in range(top):
        gate = meta[:, top + k : top + k + 1] * 256.0 + meta[:, 2 * top + k : 2 * top + k + 1]
        equal = meta[:, k : k + 1] == named
        hits = hits + jnp.where(equal, 1.0, 0.0)
        gates = gates + jnp.where(equal, gate, 0.0)
        total = total + gate
    weights = gates / total
    r0, r1 = iota((rows, rows), 0), iota((rows, rows), 1)
    earlier = ((r0 // rows_dev == r1 // rows_dev) & (r1 < r0)).astype(BF)
    rank = jnp.dot(earlier, hits.astype(BF), preferred_element_type=F32)
    grow = (iota((LANES, slots), 1) // per == iota((LANES, slots), 0)).astype(BF)
    wide_hits = jnp.dot(hits.astype(BF), grow, preferred_element_type=F32)
    wide_rank = jnp.dot(rank.astype(BF), grow, preferred_element_type=F32)
    spot = (iota((rows, slots), 1) % per - (iota((rows, slots), 0) // rows_dev) * CAP).astype(F32)
    sel = jnp.where((wide_hits > 0.5) & (wide_rank == spot), 1.0, 0.0).astype(BF)
    slot_rows = lax.dot_general(
        sel, x[:, :width], (((0,), (0,)), ((), ())), preferred_element_type=F32
    ).astype(BF)
    return sel, weights, slot_rows


def tile(parts):
    return jnp.concatenate([jnp.concatenate(row, axis=1) for row in parts], axis=0)


def scaled(block, scale, a, b, e):
    row = jnp.broadcast_to(scale[a, b, e : e + 1, :], (16, LANES)).astype(BF)
    return (block.reshape(QB // 16, 16, QB) * row[None]).reshape(QB, QB)


def half_products(xs_ref, gw, uw, gs, us, o_ref, half):
    experts, width, hidden = gw.shape
    n = hidden // 2 // QB
    per = xs_ref.shape[0] // experts
    columns = [(gw, gs, j) for j in range(n)] + [(uw, us, j) for j in range(n)]
    starts = [pl.multiple_of((half * n + j) * QB, QB) for j in range(n)]
    group, deep = 2, 2

    def block(w, scale, e, j, q):
        part = w[e, q * QB : (q + 1) * QB, pl.ds(starts[j], QB)]
        return scaled(part, scale, half * n + j, q, e)

    for e in range(experts):
        xs = xs_ref[e * per : (e + 1) * per, :]
        for at in range(0, len(columns), group):
            acc = jnp.zeros((per, group * QB), F32)
            for d in range(0, width // QB, deep):
                rhs = tile(
                    [
                        [block(w, s, e, j, q) for w, s, j in columns[at : at + group]]
                        for q in range(d, d + deep)
                    ]
                )
                acc = acc + jnp.dot(
                    xs[:, d * QB : (d + deep) * QB], rhs, preferred_element_type=F32
                )
            o_ref[e * per : (e + 1) * per, at * QB : (at + group) * QB] = acc.astype(o_ref.dtype)


def other_half(x, gw, uw, gs, us, top, rows_dev, block_count):
    experts, width, hidden = gw.shape
    slots = experts * block_count * CAP
    rows = block_count * rows_dev

    def kernel(x_ref, gw_ref, uw_ref, gs_ref, us_ref, o_ref, xs_ref, sel_ref, wt_ref):
        sel, weights, slot_rows = dispatch(x_ref[...], width, top, rows_dev, experts, slots)
        sel_ref[...] = sel
        wt_ref[...] = weights
        xs_ref[...] = slot_rows
        half = 1 - lax.rem(lax.axis_index("pool"), 2)
        half_products(xs_ref, gw_ref, uw_ref, gs_ref, us_ref, o_ref, half)

    return run(
        kernel,
        [
            sds((slots, hidden), BF),
            sds((slots, width), BF),
            sds((rows, slots), BF),
            sds((rows, LANES), F32),
        ],
        [VM] * 5,
        (x, in_vmem(gw), in_vmem(uw), gs, us),
        "other_half",
        limit=8 << 20,
        flops=NEAR,
        bytes_=NEAR,
    )


def own_half(xs, gw, uw, gs, us):
    experts, width, hidden = gw.shape
    slots = xs.shape[0]

    def kernel(xs_ref, gw_ref, uw_ref, gs_ref, us_ref, o_ref):
        half = lax.rem(lax.axis_index("pool"), 2)
        half_products(xs_ref, gw_ref, uw_ref, gs_ref, us_ref, o_ref, half)

    return run(
        kernel,
        sds((slots, hidden), F32),
        [VM] * 5,
        (xs, in_vmem(gw), in_vmem(uw), gs, us),
        "own_half",
        limit=8 << 20,
        flops=NEAR,
        bytes_=NEAR,
    )


def add_round(own, got, hint):
    def kernel(a_ref, b_ref, o_ref, r_ref):
        total = a_ref[...] + b_ref[...].astype(F32)
        o_ref[...] = total
        r_ref[...] = total.astype(BF)

    return run(kernel, [sds(own.shape, F32), sds(own.shape, BF)], [VM] * 2, (own, got), "add_round", flops=hint)


def activate(own, got):
    slots, hidden = own.shape
    n = hidden // 2

    def kernel(a_ref, b_ref, o_ref):
        gate = a_ref[:, :n] + b_ref[:, :n].astype(F32)
        up = a_ref[:, n:] + b_ref[:, n:].astype(F32)
        o_ref[...] = (jax.nn.silu(gate) * up).astype(BF)

    return run(
        kernel,
        sds((slots, n), BF),
        [VM] * 2,
        (own, got),
        "activate",
    )


def spread_rows(h_ref, sel_ref, wt_ref, experts):
    rows, slots = sel_ref.shape
    per = slots // experts
    sel = sel_ref[...].astype(F32)
    owner = iota((rows, slots), 1) // per
    stack = jnp.concatenate([jnp.where(owner == e, sel, 0.0) for e in range(experts)], axis=0)
    spread = jnp.dot(stack.astype(BF), h_ref[...], preferred_element_type=F32)
    weights = wt_ref[...]
    return [
        (spread[e * rows : (e + 1) * rows] * weights[:, e : e + 1]).astype(BF)
        for e in range(experts)
    ]


def down_kernel(hid, sel, wt, dw, ds, own):
    experts, hidden, width = dw.shape
    n = hidden // 2 // QB
    rows = sel.shape[0]
    keep = rows // 2
    last = own is not None
    given = [own] if last else []
    group = 2
    pieces = [(e, j) for e in range(experts) for j in range(n)]
    deep = 2 if len(pieces) % 2 == 0 else 1

    def kernel(h_ref, sel_ref, wt_ref, dw_ref, ds_ref, *rest):
        given_refs, outs = rest[: len(given)], rest[len(given) :]
        half = lax.rem(lax.axis_index("pool"), 2)
        half = 1 - half if last else half
        parts = spread_rows(h_ref, sel_ref, wt_ref, experts)

        starts = [pl.multiple_of((half * n + j) * QB, QB) for j in range(n)]

        def block(e, j, q):
            part = dw_ref[e, pl.ds(starts[j], QB), q * QB : (q + 1) * QB]
            return scaled(part, ds_ref, half * n + j, q, e)

        for c in range(0, width // QB, group):
            at = slice(c * QB, (c + group) * QB)
            acc = given_refs[0][:, at] if last else jnp.zeros((rows, group * QB), F32)
            for p in range(0, len(pieces), deep):
                some = pieces[p : p + deep]
                lhs = jnp.concatenate([parts[e][:, j * QB : (j + 1) * QB] for e, j in some], axis=1)
                rhs = tile([[block(e, j, q) for q in range(c, c + group)] for e, j in some])
                acc = acc + jnp.dot(lhs, rhs, preferred_element_type=F32)
            if last:
                outs[0][:, at] = acc[:keep]
                outs[1][:, at] = acc[keep:].astype(BF)
            else:
                outs[0][:, at] = acc

    return run(
        kernel,
        [sds((keep, width), F32), sds((rows - keep, width), BF)] if last else [sds((rows, width), F32)],
        [VM] * (5 + len(given)),
        (hid, sel, wt, in_vmem(dw), ds, *given),
        "down_other" if last else "down_own",
        limit=8 << 20,
        flops=NEAR,
        bytes_=NEAR,
    )


def fold(own, got):
    rows, width = own.shape
    keep = rows // 2

    def kernel(a_ref, b_ref, o_ref, s_ref):
        o_ref[...] = a_ref[:keep] + b_ref[:keep].astype(F32)
        s_ref[...] = (a_ref[keep:] + b_ref[keep:].astype(F32)).astype(BF)

    return run(
        kernel, [sds((keep, width), F32), sds((keep, width), BF)], [VM] * 2, (own, got), "fold"
    )


def finish(own, got):
    def kernel(a_ref, b_ref, o_ref):
        o_ref[...] = (a_ref[...] + b_ref[...].astype(F32)).astype(BF)

    return run(kernel, sds(own.shape, BF), [VM] * 2, (own, got), "finish")


def swap(x, axis, bit):
    return lax.ppermute(x, axis, [(j, j ^ bit) for j in range(lax.axis_size(axis))])


def bits(count):
    return [1 << i for i in range(count.bit_length() - 1)]


def per_device(tokens, routes, gate_fixed, gw, uw, dw, gs, us, ds):
    n_seq, n_head, n_pool = (lax.axis_size(a) for a in ("seq", "head", "pool"))
    rows_dev, width = tokens.shape
    top = routes.shape[1]
    hops = [("head", b) for b in reversed(bits(n_head))] + [("seq", b) for b in bits(n_seq)]

    x = pack(tokens, routes, gate_fixed, HINT * (gw.size + uw.size))
    scales = [gs.transpose(2, 0, 1), us.transpose(2, 0, 1), ds.transpose(1, 0, 2)]
    for axis, bit in hops:
        got = swap(x, axis, bit)
        if scales:
            gs, us, ds = spread_scales(scales, x)
        x = cat(x, got, [gs] if scales else [])
        scales = []

    send, xs, sel, wt = other_half(x, gw, uw, gs, us, top, rows_dev, n_seq * n_head)
    got = swap(send, "pool", 1)
    own = own_half(xs, gw, uw, gs, us)
    for bit in bits(n_pool)[1:]:
        own, send = add_round(own, got, HINT * dw.size)
        got = swap(send, "pool", bit)
    hid = activate(own, got)
    other = swap(hid, "pool", 1)
    (acc,) = down_kernel(hid, sel, wt, dw, ds, None)
    acc, send = down_kernel(other, sel, wt, dw, ds, acc)
    for axis, bit in reversed(hops[1:]):
        acc, send = fold(acc, swap(send, axis, bit))
    axis, bit = hops[0]
    return finish(acc, swap(send, axis, bit))


def solution(mesh):
    return jax.shard_map(
        per_device,
        mesh=mesh,
        in_specs=(
            P(("seq", "head"), "pool"),
            P(("seq", "head"), None),
            P(("seq", "head"), None),
            P("seq", "pool", "head"),
            P("seq", "pool", "head"),
            P("seq", "head", "pool"),
            P("seq", "pool", "head"),
            P("seq", "pool", "head"),
            P("seq", "head", "pool"),
        ),
        out_specs=P(("seq", "head"), "pool"),
        check_vma=False,
    )
```

time: 63.4 us -> 42.8 us (0.68)
  local copies, waits for them, and re-layouts: 17.8 us -> 0.02 us
  Pallas kernels: 13.3 us -> 10.6 us
  starting transfers between devices: 16.7 us -> 15.2 us
  waiting for transfers between devices: 15 us -> 16.5 us
    unnamed x25 -> x10, local copies, waits for them, and re-layouts: 17.8 us -> 0.02 us
    pallas_call x13 -> x14, Pallas kernels: 13.3 us -> 10.6 us  [run(): pl.pallas_call(kernel, out_shape=out_shape, in_specs=in_specs, out_specs=...]
    ppermute x9, waiting for transfers between devices: 15 us -> 16.5 us  [swap(): lax.ppermute(x, axis, [(j, j ^ bit) for j in range(lax.axis_size(axis))])]
    ppermute x9, starting transfers between devices: 16.7 us -> 15.2 us  [swap(): lax.ppermute(x, axis, [(j, j ^ bit) for j in range(lax.axis_size(axis))])]
  transfers between devices with their start and end apart: 9 -> 9, of which waited for: 7 -> 6; matrix products, arithmetic and copies ran while one was open for 0% -> 0% of each run, Pallas kernels for 9% -> 12%
where the time goes in v4:
time: 42.8 us; the launch traced here: 42.5 us
  waiting for transfers between devices  16.5 us (39%)
  starting transfers between devices  15.2 us (36%)
  Pallas kernels  10.6 us (25%)
    ppermute x9, waiting for transfers between devices, swap(): lax.ppermute(x, axis, [(j, j ^ bit) for j in range(lax.axis_size(axis))])  16.5 us
    ppermute x9, starting transfers between devices, swap(): lax.ppermute(x, axis, [(j, j ^ bit) for j in range(lax.axis_size(axis))])  15.2 us
    pallas_call x14, Pallas kernels, run(): pl.pallas_call(kernel, out_shape=out_shape, in_specs=in_specs, out_specs=...  10.6 us
  transfers between devices with their start and end apart: 9, of which 6 were waited for; matrix products, arithmetic and copies ran while one was open for 0% of the time, Pallas kernels for 12%

profile of v4, /device:TPU:0, one launch (start us, length us, event | category | flops | bytes accessed | tf_op | source)
XLA Modules:
  0.0 42.5 jit_solution(9549846115592744828)
XLA Ops:
  0.0 0.0 copy-start.1
  0.0 0.0 copy-start
  0.0 1.0 %pack.1.refs_3_.a_ref = bf16[4,1152]{1,0:T(4,128)(2,1)S(1)} custom-call(bf16[4,1024]{1,0:T(4,128)(2,1)} %t_in.1, s32[4,8]{1,0:T(4,128)} %r_in.1, s32[4,8]{1,0:T(4,128)} %g_in.1), custom_call_target="tpu_custom_call" | custom-call | flops 12582912000 | tf_op jit(solution)/shard_map/pack/pallas_call | solution.py:30
  1.0 4.1 %collective-permute-start = (bf16[4,1152]{1,0:T(4,128)(2,1)S(1)}, bf16[4,1152]{1,0:T(4,128)(2,1)S(1)}, u32[]{:S(2)}, u32[]{:S(2)}) collective-permute-start(bf16[4,1152]{1,0:T(4,128)(2,1)S(1)} %pack.1.refs_3_.a_ref), channel_id=1, source_target_pairs={{0,8},{4,12},{8,0},{12,4},{1,9},{5,13},{9,1},{13,5},{2,10},{6,14},... | collective-permute-start | bytes 27656 | tf_op jit(solution)/shard_map/ppermute | solution.py:370
  5.2 1.8 %spread_scales.1 = (f32[6,8,8,128]{3,2,1,0:T(8,128)S(1)}, f32[6,8,8,128]{3,2,1,0:T(8,128)S(1)}, f32[6,8,8,128]{3,2,1,0:T(8,128)S(1)}) custom-call(bf16[6,8,8]{2,1,0:T(8,128)(2,1)} %bitcast.5, bf16[6,8,8]{2,1,0:T(8,128)(2,1)} %bitcast.6, bf16[6,8,8]{2,1,0:T(8,128)(2,1)} %bitcast.7, bf16[4,1152]{1,0:T(4,128)(2,1)S(1)} %pack.1.refs_3_.a_ref), custom_call_target="tpu_custom_call" | custom-call | bytes 1048576 | tf_op jit(solution)/shard_map/spread_scales/pallas_call | solution.py:30
  7.0 0.0 collective-permute-done.b_ref
  7.0 1.7 %collective-permute-start.1 = (bf16[8,1152]{1,0:T(8,128)(2,1)S(1)}, bf16[8,1152]{1,0:T(8,128)(2,1)S(1)}, u32[]{:S(2)}, u32[]{:S(2)}) collective-permute-start(bf16[8,1152]{1,0:T(8,128)(2,1)S(1)} %cat.3.a_ref), channel_id=1, source_target_pairs={{0,4},{4,0},{8,12},{12,8},{1,5},{5,1},{9,13},{13,9},{2,6},{6,2},{1... | collective-permute-start | bytes 55304 | tf_op jit(solution)/shard_map/ppermute | solution.py:370
  8.7 2.1 %collective-permute-done.1.b_ref = bf16[8,1152]{1,0:T(8,128)(2,1)S(1)} collective-permute-done((bf16[8,1152]{1,0:T(8,128)(2,1)S(1)}, bf16[8,1152]{1,0:T(8,128)(2,1)S(1)}, u32[]{:S(2)}, u32[]{:S(2)}) %collective-permute-start.1) | collective-permute-done | bytes 18464 | tf_op jit(solution)/shard_map/ppermute | solution.py:370
  10.8 1.6 %collective-permute-start.2 = (bf16[16,1152]{1,0:T(8,128)(2,1)S(1)}, bf16[16,1152]{1,0:T(8,128)(2,1)S(1)}, u32[]{:S(2)}, u32[]{:S(2)}) collective-permute-start(bf16[16,1152]{1,0:T(8,128)(2,1)S(1)} %cat.4.a_ref), channel_id=1, source_target_pairs={{0,16},{16,0},{1,17},{17,1},{2,18},{18,2},{3,19},{19,3},{4,20},{20... | collective-permute-start | bytes 110600 | tf_op jit(solution)/shard_map/ppermute | solution.py:370
  12.4 2.4 %collective-permute-done.2.b_ref = bf16[16,1152]{1,0:T(8,128)(2,1)S(1)} collective-permute-done((bf16[16,1152]{1,0:T(8,128)(2,1)S(1)}, bf16[16,1152]{1,0:T(8,128)(2,1)S(1)}, u32[]{:S(2)}, u32[]{:S(2)}) %collective-permute-start.2) | collective-permute-done | bytes 36896 | tf_op jit(solution)/shard_map/ppermute | solution.py:370
  14.8 0.0 copy-done.1
  14.8 0.0 copy-done
  14.8 2.4 %other_half.1 = (bf16[128,768]{1,0:T(8,128)(2,1)S(1)}, bf16[128,1024]{1,0:T(8,128)(2,1)S(1)}, bf16[32,128]{1,0:T(8,128)(2,1)S(1)}, f32[32,128]{1,0:T(8,128)S(1)}) custom-call(bf16[32,1152]{1,0:T(8,128)(2,1)S(1)} %cat.5.x_ref, bf16[8,1024,768]{2,1,0:T(8,128)(2,1)S(1)} %copy-done, bf16[8,1024,768]{2,1,0:T(8,128)(2,1)S(1)} %copy-done.1, ...), custom_call_target="tpu_custom_call" | custom-call | flops 65536 | bytes 65536 | tf_op jit(solution)/shard_map/other_half/pallas_call | solution.py:30
  17.2 0.0 collective-permute-start.3
  17.2 0.0 slice-start
  17.2 0.0 slice-start.1
  17.3 1.9 %own_half.1.a_ref = f32[128,768]{1,0:T(8,128)S(1)} custom-call(bf16[128,1024]{1,0:T(8,128)(2,1)S(1)} %get-tuple-element.22.xs_ref, bf16[8,1024,768]{2,1,0:T(8,128)(2,1)S(1)} %copy-done, bf16[8,1024,768]{2,1,0:T(8,128)(2,1)S(1)} %copy-done.1, f32[6,8,8,128]{3,2,1,0:T(8,128)S(1)} %get-tuple-element.20.rest_0_.gs_ref, f32[6,8,8,128]{3,2,1,0:T(8,128)S(1)} %get-tuple-element.21.us_ref), custom_call_target="tpu_custom_call" | custom-call | flops 65536 | bytes 65536 | tf_op jit(solution)/shard_map/own_half/pallas_call | solution.py:30
  19.2 0.0 slice-start.2
  19.2 0.0 collective-permute-done.3.b_ref
  19.2 0.1 add_round.1
  19.3 1.7 %collective-permute-start.4 = (bf16[128,768]{1,0:T(8,128)(2,1)S(1)}, bf16[128,768]{1,0:T(8,128)(2,1)S(1)}, u32[]{:S(2)}, u32[]{:S(2)}) collective-permute-start(bf16[128,768]{1,0:T(8,128)(2,1)S(1)} %get-tuple-element.25), channel_id=1, source_target_pairs={{0,2},{1,3},{2,0},{3,1},{4,6},{5,7},{6,4},{7,5},{8,10},{9,11},{10,... | collective-permute-start | bytes 589832 | tf_op jit(solution)/shard_map/ppermute | solution.py:370
  20.9 5.7 %collective-permute-done.4.b_ref = bf16[128,768]{1,0:T(8,128)(2,1)S(1)} collective-permute-done((bf16[128,768]{1,0:T(8,128)(2,1)S(1)}, bf16[128,768]{1,0:T(8,128)(2,1)S(1)}, u32[]{:S(2)}, u32[]{:S(2)}) %collective-permute-start.4) | collective-permute-done | bytes 196640 | tf_op jit(solution)/shard_map/ppermute | solution.py:370
  26.6 0.1 activate.1.h_ref
  26.7 0.1 collective-permute-start.5
  26.8 0.0 slice-done
  26.8 0.0 slice-done.1
  26.8 0.0 slice-done.2
  26.8 1.3 %down_own.1.rest_0_ = f32[32,1024]{1,0:T(8,128)S(1)} custom-call(bf16[128,384]{1,0:T(8,128)(2,1)S(1)} %activate.1.h_ref, bf16[32,128]{1,0:T(8,128)(2,1)S(1)} %get-tuple-element.26.sel_ref, f32[32,128]{1,0:T(8,128)S(1)} %get-tuple-element.27.wt_ref, bf16[8,768,1024]{2,1,0:T(8,128)(2,1)S(1)} %bitcast.4, f32[6,8,8,128]{3,2,1,0:T(8,128)S(1)} %get-tuple-element.28.ds_ref), custom_call_target="tpu_custom_call" | custom-call | flops 65536 | bytes 65536 | tf_op jit(solution)/shard_map/down_own/pallas_call | solution.py:30
  28.2 0.0 collective-permute-done.5.h_ref
  28.2 1.3 %down_other.1 = (f32[16,1024]{1,0:T(8,128)S(1)}, bf16[16,1024]{1,0:T(8,128)(2,1)S(1)}) custom-call(bf16[128,384]{1,0:T(8,128)(2,1)S(1)} %collective-permute-done.5.h_ref, bf16[32,128]{1,0:T(8,128)(2,1)S(1)} %get-tuple-element.26.sel_ref, f32[32,128]{1,0:T(8,128)S(1)} %get-tuple-element.27.wt_ref, bf16[8,768,1024]{2,1,0:T(8,128)(2,1)S(1)} %bitcast.4, ...), custom_call_target="tpu_custom_call" | custom-call | flops 65536 | bytes 65536 | tf_op jit(solution)/shard_map/down_other/pallas_call | solution.py:30
  29.5 1.6 %collective-permute-start.6 = (bf16[16,1024]{1,0:T(8,128)(2,1)S(1)}, bf16[16,1024]{1,0:T(8,128)(2,1)S(1)}, u32[]{:S(2)}, u32[]{:S(2)}) collective-permute-start(bf16[16,1024]{1,0:T(8,128)(2,1)S(1)} %get-tuple-element.30), channel_id=1, source_target_pairs={{0,16},{16,0},{1,17},{17,1},{2,18},{18,2},{3,19},{19,3},{4,20},{20... | collective-permute-start | bytes 98312 | tf_op jit(solution)/shard_map/ppermute | solution.py:370
  31.1 2.3 %collective-permute-done.6.b_ref = bf16[16,1024]{1,0:T(8,128)(2,1)S(1)} collective-permute-done((bf16[16,1024]{1,0:T(8,128)(2,1)S(1)}, bf16[16,1024]{1,0:T(8,128)(2,1)S(1)}, u32[]{:S(2)}, u32[]{:S(2)}) %collective-permute-start.6) | collective-permute-done | bytes 32800 | tf_op jit(solution)/shard_map/ppermute | solution.py:370
  33.5 1.7 %collective-permute-start.7 = (bf16[8,1024]{1,0:T(8,128)(2,1)S(1)}, bf16[8,1024]{1,0:T(8,128)(2,1)S(1)}, u32[]{:S(2)}, u32[]{:S(2)}) collective-permute-start(bf16[8,1024]{1,0:T(8,128)(2,1)S(1)} %get-tuple-element.32), channel_id=1, source_target_pairs={{0,4},{4,0},{8,12},{12,8},{1,5},{5,1},{9,13},{13,9},{2,6},{6,2},{1... | collective-permute-start | bytes 49160 | tf_op jit(solution)/shard_map/ppermute | solution.py:370
  35.2 2.1 %collective-permute-done.7.b_ref = bf16[8,1024]{1,0:T(8,128)(2,1)S(1)} collective-permute-done((bf16[8,1024]{1,0:T(8,128)(2,1)S(1)}, bf16[8,1024]{1,0:T(8,128)(2,1)S(1)}, u32[]{:S(2)}, u32[]{:S(2)}) %collective-permute-start.7) | collective-permute-done | bytes 16416 | tf_op jit(solution)/shard_map/ppermute | solution.py:370
  37.3 2.7 %collective-permute-start.8 = (bf16[4,1024]{1,0:T(4,128)(2,1)S(1)}, bf16[4,1024]{1,0:T(4,128)(2,1)S(1)}, u32[]{:S(2)}, u32[]{:S(2)}) collective-permute-start(bf16[4,1024]{1,0:T(4,128)(2,1)S(1)} %get-tuple-element.34), channel_id=1, source_target_pairs={{0,8},{4,12},{8,0},{12,4},{1,9},{5,13},{9,1},{13,5},{2,10},{6,14},... | collective-permute-start | bytes 24584 | tf_op jit(solution)/shard_map/ppermute | solution.py:370
  40.0 1.9 %collective-permute-done.8.b_ref = bf16[4,1024]{1,0:T(4,128)(2,1)S(1)} collective-permute-done((bf16[4,1024]{1,0:T(4,128)(2,1)S(1)}, bf16[4,1024]{1,0:T(4,128)(2,1)S(1)}, u32[]{:S(2)}, u32[]{:S(2)}) %collective-permute-start.8) | collective-permute-done | bytes 8224 | tf_op jit(solution)/shard_map/ppermute | solution.py:370
  41.9 0.6 %finish.1 = bf16[4,1024]{1,0:T(4,128)(2,1)} custom-call(f32[4,1024]{1,0:T(4,128)S(1)} %get-tuple-element.33.a_ref, bf16[4,1024]{1,0:T(4,128)(2,1)S(1)} %collective-permute-done.8.b_ref), custom_call_target="tpu_custom_call" | custom-call | tf_op jit(solution)/shard_map/finish/pallas_call | solution.py:30
  (6 shorter events, 0.0 us)
Async XLA Ops:
  0.0 14.8 %copy-start.1 = (bf16[8,1024,768]{2,1,0:T(8,128)(2,1)S(1)}, bf16[8,1024,768]{2,1,0:T(8,128)(2,1)}, u32[]{:S(2)}) copy-start(bf16[8,1024,768]{2,1,0:T(8,128)(2,1)} %uw_ref.3) | copy-start | bytes 37748740
  0.0 14.8 %copy-start = (bf16[8,1024,768]{2,1,0:T(8,128)(2,1)S(1)}, bf16[8,1024,768]{2,1,0:T(8,128)(2,1)}, u32[]{:S(2)}) copy-start(bf16[8,1024,768]{2,1,0:T(8,128)(2,1)} %gw_ref.3) | copy-start | bytes 37748740
  1.0 5.9 %collective-permute-start = (bf16[4,1152]{1,0:T(4,128)(2,1)S(1)}, bf16[4,1152]{1,0:T(4,128)(2,1)S(1)}, u32[]{:S(2)}, u32[]{:S(2)}) collective-permute-start(bf16[4,1152]{1,0:T(4,128)(2,1)S(1)} %pack.1.refs_3_.a_ref), channel_id=1, source_target_pairs={{0,8},{4,12},{8,0},{12,4},{1,9},{5,13},{9,1},{13,5},{2,10},{6,14},... | collective-permute-start | bytes 27656 | tf_op jit(solution)/shard_map/ppermute | solution.py:370
  7.0 3.8 %collective-permute-start.1 = (bf16[8,1152]{1,0:T(8,128)(2,1)S(1)}, bf16[8,1152]{1,0:T(8,128)(2,1)S(1)}, u32[]{:S(2)}, u32[]{:S(2)}) collective-permute-start(bf16[8,1152]{1,0:T(8,128)(2,1)S(1)} %cat.3.a_ref), channel_id=1, source_target_pairs={{0,4},{4,0},{8,12},{12,8},{1,5},{5,1},{9,13},{13,9},{2,6},{6,2},{1... | collective-permute-start | bytes 55304 | tf_op jit(solution)/shard_map/ppermute | solution.py:370
  10.8 4.0 %collective-permute-start.2 = (bf16[16,1152]{1,0:T(8,128)(2,1)S(1)}, bf16[16,1152]{1,0:T(8,128)(2,1)S(1)}, u32[]{:S(2)}, u32[]{:S(2)}) collective-permute-start(bf16[16,1152]{1,0:T(8,128)(2,1)S(1)} %cat.4.a_ref), channel_id=1, source_target_pairs={{0,16},{16,0},{1,17},{17,1},{2,18},{18,2},{3,19},{19,3},{4,20},{20... | collective-permute-start | bytes 110600 | tf_op jit(solution)/shard_map/ppermute | solution.py:370
  17.2 2.0 %collective-permute-start.3 = (bf16[128,768]{1,0:T(8,128)(2,1)S(1)}, bf16[128,768]{1,0:T(8,128)(2,1)S(1)}, u32[]{:S(2)}, u32[]{:S(2)}) collective-permute-start(bf16[128,768]{1,0:T(8,128)(2,1)S(1)} %get-tuple-element.23), channel_id=1, source_target_pairs={{0,1},{1,0},{2,3},{3,2},{4,5},{5,4},{6,7},{7,6},{8,9},{9,8},{10,11... | collective-permute-start | bytes 589832 | tf_op jit(solution)/shard_map/ppermute | solution.py:370
  17.2 9.6 %slice-start = ((s8[12582912]{0:T(1024)(128)(4,1)}), s8[4194304]{0:T(1024)(128)(4,1)S(1)}, s32[]{:S(2)}) async-start(s8[12582912]{0:T(1024)(128)(4,1)} %bitcast.3), calls=%async_computation | async-start | bytes 8388608
  17.2 9.6 %slice-start.1 = ((s8[12582912]{0:T(1024)(128)(4,1)}), s8[4194304]{0:T(1024)(128)(4,1)S(1)}, s32[]{:S(2)}) async-start(s8[12582912]{0:T(1024)(128)(4,1)} %bitcast.3), calls=%async_computation.1 | async-start | bytes 8388608
  19.2 7.6 %slice-start.2 = ((s8[12582912]{0:T(1024)(128)(4,1)}), s8[4194304]{0:T(1024)(128)(4,1)S(1)}, s32[]{:S(2)}) async-start(s8[12582912]{0:T(1024)(128)(4,1)} %bitcast.3), calls=%async_computation.2 | async-start | bytes 8388608
  19.3 7.4 %collective-permute-start.4 = (bf16[128,768]{1,0:T(8,128)(2,1)S(1)}, bf16[128,768]{1,0:T(8,128)(2,1)S(1)}, u32[]{:S(2)}, u32[]{:S(2)}) collective-permute-start(bf16[128,768]{1,0:T(8,128)(2,1)S(1)} %get-tuple-element.25), channel_id=1, source_target_pairs={{0,2},{1,3},{2,0},{3,1},{4,6},{5,7},{6,4},{7,5},{8,10},{9,11},{10,... | collective-permute-start | bytes 589832 | tf_op jit(solution)/shard_map/ppermute | solution.py:370
  26.7 1.5 %collective-permute-start.5 = (bf16[128,384]{1,0:T(8,128)(2,1)S(1)}, bf16[128,384]{1,0:T(8,128)(2,1)S(1)}, u32[]{:S(2)}, u32[]{:S(2)}) collective-permute-start(bf16[128,384]{1,0:T(8,128)(2,1)S(1)} %activate.1.h_ref), channel_id=1, source_target_pairs={{0,1},{1,0},{2,3},{3,2},{4,5},{5,4},{6,7},{7,6},{8,9},{9,8},{10,11... | collective-permute-start | bytes 294920 | tf_op jit(solution)/shard_map/ppermute | solution.py:370
  29.5 4.0 %collective-permute-start.6 = (bf16[16,1024]{1,0:T(8,128)(2,1)S(1)}, bf16[16,1024]{1,0:T(8,128)(2,1)S(1)}, u32[]{:S(2)}, u32[]{:S(2)}) collective-permute-start(bf16[16,1024]{1,0:T(8,128)(2,1)S(1)} %get-tuple-element.30), channel_id=1, source_target_pairs={{0,16},{16,0},{1,17},{17,1},{2,18},{18,2},{3,19},{19,3},{4,20},{20... | collective-permute-start | bytes 98312 | tf_op jit(solution)/shard_map/ppermute | solution.py:370
  33.5 3.8 %collective-permute-start.7 = (bf16[8,1024]{1,0:T(8,128)(2,1)S(1)}, bf16[8,1024]{1,0:T(8,128)(2,1)S(1)}, u32[]{:S(2)}, u32[]{:S(2)}) collective-permute-start(bf16[8,1024]{1,0:T(8,128)(2,1)S(1)} %get-tuple-element.32), channel_id=1, source_target_pairs={{0,4},{4,0},{8,12},{12,8},{1,5},{5,1},{9,13},{13,9},{2,6},{6,2},{1... | collective-permute-start | bytes 49160 | tf_op jit(solution)/shard_map/ppermute | solution.py:370
  37.3 4.6 %collective-permute-start.8 = (bf16[4,1024]{1,0:T(4,128)(2,1)S(1)}, bf16[4,1024]{1,0:T(4,128)(2,1)S(1)}, u32[]{:S(2)}, u32[]{:S(2)}) collective-permute-start(bf16[4,1024]{1,0:T(4,128)(2,1)S(1)} %get-tuple-element.34), channel_id=1, source_target_pairs={{0,8},{4,12},{8,0},{12,4},{1,9},{5,13},{9,1},{13,5},{2,10},{6,14},... | collective-permute-start | bytes 24584 | tf_op jit(solution)/shard_map/ppermute | solution.py:370

commit v5 on v4

--- a/solution.py
+++ b/solution.py
@@ -11,6 +11,7 @@
 CAP = 2
 HINT = 1000
 NEAR = 1 << 16
+LATE = 0
 LANES = 128
 BF = jnp.bfloat16
 F32 = jnp.float32
@@ -92,20 +93,20 @@
     )
 
 
-def cat(a, b, after):
-    rows = a.shape[0]
-
-    def kernel(a_ref, b_ref, *rest):
-        o_ref = rest[-1]
-        o_ref[:rows] = a_ref[...]
-        o_ref[rows:] = b_ref[...]
-
-    return run(
-        kernel,
-        sds((2 * rows,) + a.shape[1:], a.dtype),
-        [VM] * (2 + len(after)),
-        (a, b, *after),
+def cat(pieces, after, hint=0):
+    rows = pieces[0].shape[0]
+
+    def kernel(*refs):
+        for i in range(len(pieces)):
+            refs[-1][i * rows : (i + 1) * rows] = refs[i][...]
+
+    return run(
+        kernel,
+        sds((len(pieces) * rows,) + pieces[0].shape[1:], pieces[0].dtype),
+        [VM] * (len(pieces) + len(after)),
+        (*pieces, *after),
         "cat",
+        flops=hint,
     )
 
 
@@ -297,11 +298,11 @@
     ]
 
 
-def down_kernel(hid, sel, wt, dw, ds, own):
+def down_kernel(hid, sel, wt, dw, ds, own, parts_out):
     experts, hidden, width = dw.shape
     n = hidden // 2 // QB
     rows = sel.shape[0]
-    keep = rows // 2
+    keep = rows // parts_out
     last = own is not None
     given = [own] if last else []
     group = 2
@@ -330,13 +331,14 @@
                 acc = acc + jnp.dot(lhs, rhs, preferred_element_type=F32)
             if last:
                 outs[0][:, at] = acc[:keep]
-                outs[1][:, at] = acc[keep:].astype(BF)
+                for g in range(1, parts_out):
+                    outs[g][:, at] = acc[g * keep : (g + 1) * keep].astype(BF)
             else:
                 outs[0][:, at] = acc
 
     return run(
         kernel,
-        [sds((keep, width), F32), sds((rows - keep, width), BF)] if last else [sds((rows, width), F32)],
+        [sds((keep, width), F32)] + [sds((keep, width), BF)] * (parts_out - 1) if last else [sds((rows, width), F32)],
         [VM] * (5 + len(given)),
         (hid, sel, wt, in_vmem(dw), ds, *given),
         "down_other" if last else "down_own",
@@ -350,24 +352,46 @@
     rows, width = own.shape
     keep = rows // 2
 
-    def kernel(a_ref, b_ref, o_ref, s_ref):
-        o_ref[...] = a_ref[:keep] + b_ref[:keep].astype(F32)
-        s_ref[...] = (a_ref[keep:] + b_ref[keep:].astype(F32)).astype(BF)
-
-    return run(
-        kernel, [sds((keep, width), F32), sds((keep, width), BF)], [VM] * 2, (own, got), "fold"
+    def kernel(a_ref, *rest):
+        total = a_ref[...]
+        for ref in rest[: len(got)]:
+            total = total + ref[...].astype(F32)
+        o_ref, s_ref = rest[len(got) :]
+        o_ref[...] = total[:keep]
+        s_ref[...] = total[keep:].astype(BF)
+
+    return run(
+        kernel,
+        [sds((keep, width), F32), sds((keep, width), BF)],
+        [VM] * (1 + len(got)),
+        (own, *got),
+        "fold",
     )
 
 
 def finish(own, got):
-    def kernel(a_ref, b_ref, o_ref):
-        o_ref[...] = (a_ref[...] + b_ref[...].astype(F32)).astype(BF)
-
-    return run(kernel, sds(own.shape, BF), [VM] * 2, (own, got), "finish")
+    def kernel(a_ref, *rest):
+        total = a_ref[...]
+        for ref in rest[:-1]:
+            total = total + ref[...].astype(F32)
+        rest[-1][...] = total.astype(BF)
+
+    return run(kernel, sds(own.shape, BF), [VM] * (1 + len(got)), (own, *got), "finish")
 
 
 def swap(x, axis, bit):
     return lax.ppermute(x, axis, [(j, j ^ bit) for j in range(lax.axis_size(axis))])
+
+
+def hop(x, *steps):
+    n_seq, n_head = lax.axis_size("seq"), lax.axis_size("head")
+    flip = {axis: sum(b for a, b in steps if a == axis) for axis in ("seq", "head")}
+    pairs = [
+        (s * n_head + h, (s ^ flip["seq"]) * n_head + (h ^ flip["head"]))
+        for s in range(n_seq)
+        for h in range(n_head)
+    ]
+    return lax.ppermute(x, ("seq", "head"), pairs)
 
 
 def bits(count):
@@ -382,12 +406,15 @@
 
     x = pack(tokens, routes, gate_fixed, HINT * (gw.size + uw.size))
     scales = [gs.transpose(2, 0, 1), us.transpose(2, 0, 1), ds.transpose(1, 0, 2)]
-    for axis, bit in hops:
-        got = swap(x, axis, bit)
+    single, (a, b) = hops[:-2], hops[-2:]
+    for step in single:
+        got = hop(x, step)
         if scales:
             gs, us, ds = spread_scales(scales, x)
-        x = cat(x, got, [gs] if scales else [])
+        x = cat([x, got], [gs] if scales else [], HINT * dw.size * LATE if scales else 0)
         scales = []
+    far, near_a, near_b = hop(x, a, b), hop(x, a), hop(x, b)
+    x = cat([x, near_a, near_b, far], [])
 
     send, xs, sel, wt = other_half(x, gw, uw, gs, us, top, rows_dev, n_seq * n_head)
     got = swap(send, "pool", 1)
@@ -397,12 +424,14 @@
         got = swap(send, "pool", bit)
     hid = activate(own, got)
     other = swap(hid, "pool", 1)
-    (acc,) = down_kernel(hid, sel, wt, dw, ds, None)
-    acc, send = down_kernel(other, sel, wt, dw, ds, acc)
-    for axis, bit in reversed(hops[1:]):
-        acc, send = fold(acc, swap(send, axis, bit))
-    axis, bit = hops[0]
-    return finish(acc, swap(send, axis, bit))
+    (acc,) = down_kernel(hid, sel, wt, dw, ds, None, 4)
+    acc, to_a, to_b, to_far = down_kernel(other, sel, wt, dw, ds, acc, 4)
+    far, near_a, near_b = hop(to_far, a, b), hop(to_a, a), hop(to_b, b)
+    got = [far, near_b, near_a]
+    for step in reversed(single):
+        acc, send = fold(acc, got)
+        got = [hop(send, step)]
+    return finish(acc, got)
 
 
 def solution(mesh):

time: 42.8 us -> 39.9 us (0.932)
  waiting for transfers between devices: 16.5 us -> 13.2 us
    ppermute x0 -> x8, starting transfers between devices: none -> 14 us  [hop(): return lax.ppermute(x, ('seq', 'head'), pairs)]
    ppermute x9 -> x3, starting transfers between devices: 15.2 us -> 1.66 us  [swap(): lax.ppermute(x, axis, [(j, j ^ bit) for j in range(lax.axis_size(axis))])]
    ppermute x9 -> x3, waiting for transfers between devices: 16.5 us -> 5.79 us  [swap(): lax.ppermute(x, axis, [(j, j ^ bit) for j in range(lax.axis_size(axis))])]
    ppermute x0 -> x8, waiting for transfers between devices: none -> 7.37 us  [hop(): return lax.ppermute(x, ('seq', 'head'), pairs)]
    pallas_call x14 -> x12, Pallas kernels: 10.6 us -> 10.6 us  [run(): pl.pallas_call(kernel, out_shape=out_shape, in_specs=in_specs, out_specs=...]
  transfers between devices with their start and end apart: 9 -> 11, of which waited for: 6 -> 8; matrix products, arithmetic and copies ran while one was open for 0% -> 0% of each run, Pallas kernels for 12% -> 13%
where the time goes in v5:
time: 39.9 us; the launch traced here: 39.5 us
  starting transfers between devices  15.6 us (39%)
  waiting for transfers between devices  13.2 us (33%)
  Pallas kernels  10.6 us (27%)
    ppermute x8, starting transfers between devices, hop(): return lax.ppermute(x, ('seq', 'head'), pairs)  14 us
    pallas_call x12, Pallas kernels, run(): pl.pallas_call(kernel, out_shape=out_shape, in_specs=in_specs, out_specs=...  10.6 us
    ppermute x8, waiting for transfers between devices, hop(): return lax.ppermute(x, ('seq', 'head'), pairs)  7.37 us
    ppermute x3, waiting for transfers between devices, swap(): lax.ppermute(x, axis, [(j, j ^ bit) for j in range(lax.axis_size(axis))])  5.79 us
    ppermute x3, starting transfers between devices, swap(): lax.ppermute(x, axis, [(j, j ^ bit) for j in range(lax.axis_size(axis))])  1.66 us
  transfers between devices with their start and end apart: 11, of which 8 were waited for; matrix products, arithmetic and copies ran while one was open for 0% of the time, Pallas kernels for 13%

profile of v5, /device:TPU:0, one launch (start us, length us, event | category | flops | bytes accessed | tf_op | source)
XLA Modules:
  0.0 39.5 jit_solution(10718935009871717891)
XLA Ops:
  0.0 0.0 copy-start.1
  0.0 0.0 copy-start
  0.0 1.0 %pack.1.refs_3_.refs_0_ = bf16[4,1152]{1,0:T(4,128)(2,1)S(1)} custom-call(bf16[4,1024]{1,0:T(4,128)(2,1)} %t_in.1, s32[4,8]{1,0:T(4,128)} %r_in.1, s32[4,8]{1,0:T(4,128)} %g_in.1), custom_call_target="tpu_custom_call" | custom-call | flops 12582912000 | tf_op jit(solution)/shard_map/pack/pallas_call | solution.py:31
  1.0 4.1 %collective-permute-start = (bf16[4,1152]{1,0:T(4,128)(2,1)S(1)}, bf16[4,1152]{1,0:T(4,128)(2,1)S(1)}, u32[]{:S(2)}, u32[]{:S(2)}) collective-permute-start(bf16[4,1152]{1,0:T(4,128)(2,1)S(1)} %pack.1.refs_3_.refs_0_), channel_id=1, source_target_pairs={{0,8},{4,12},{8,0},{12,4},{16,24},{20,28},{24,16},{28,20},{1,9},{5... | collective-permute-start | bytes 27656 | tf_op jit(solution)/shard_map/ppermute | solution.py:394
  5.2 1.8 %spread_scales.1 = (f32[6,8,8,128]{3,2,1,0:T(8,128)S(1)}, f32[6,8,8,128]{3,2,1,0:T(8,128)S(1)}, f32[6,8,8,128]{3,2,1,0:T(8,128)S(1)}) custom-call(bf16[6,8,8]{2,1,0:T(8,128)(2,1)} %bitcast.5, bf16[6,8,8]{2,1,0:T(8,128)(2,1)} %bitcast.6, bf16[6,8,8]{2,1,0:T(8,128)(2,1)} %bitcast.7, bf16[4,1152]{1,0:T(4,128)(2,1)S(1)} %pack.1.refs_3_.refs_0_), custom_call_target="tpu_custom_call" | custom-call | bytes 1048576 | tf_op jit(solution)/shard_map/spread_scales/pallas_call | solution.py:31
  7.0 0.0 collective-permute-done.refs_1_
  7.0 2.6 %collective-permute-start.3 = (bf16[8,1152]{1,0:T(8,128)(2,1)S(1)}, bf16[8,1152]{1,0:T(8,128)(2,1)S(1)}, u32[]{:S(2)}, u32[]{:S(2)}) collective-permute-start(bf16[8,1152]{1,0:T(8,128)(2,1)S(1)} %cat.2.refs_0_), channel_id=1, source_target_pairs={{0,20},{4,16},{8,28},{12,24},{16,4},{20,0},{24,12},{28,8},{1,21},{... | collective-permute-start | bytes 55304 | tf_op jit(solution)/shard_map/ppermute | solution.py:394
  9.7 0.5 %collective-permute-start.2 = (bf16[8,1152]{1,0:T(8,128)(2,1)S(1)}, bf16[8,1152]{1,0:T(8,128)(2,1)S(1)}, u32[]{:S(2)}, u32[]{:S(2)}) collective-permute-start(bf16[8,1152]{1,0:T(8,128)(2,1)S(1)} %cat.2.refs_0_), channel_id=1, source_target_pairs={{0,16},{4,20},{8,24},{12,28},{16,0},{20,4},{24,8},{28,12},{1,17},{... | collective-permute-start | bytes 55304 | tf_op jit(solution)/shard_map/ppermute | solution.py:394
  10.2 0.4 collective-permute-start.1
  10.6 1.3 %collective-permute-done.3.refs_3_ = bf16[8,1152]{1,0:T(8,128)(2,1)S(1)} collective-permute-done((bf16[8,1152]{1,0:T(8,128)(2,1)S(1)}, bf16[8,1152]{1,0:T(8,128)(2,1)S(1)}, u32[]{:S(2)}, u32[]{:S(2)}) %collective-permute-start.3) | collective-permute-done | bytes 18464 | tf_op jit(solution)/shard_map/ppermute | solution.py:394
  11.8 1.6 %collective-permute-done.2.refs_2_ = bf16[8,1152]{1,0:T(8,128)(2,1)S(1)} collective-permute-done((bf16[8,1152]{1,0:T(8,128)(2,1)S(1)}, bf16[8,1152]{1,0:T(8,128)(2,1)S(1)}, u32[]{:S(2)}, u32[]{:S(2)}) %collective-permute-start.2) | collective-permute-done | bytes 18464 | tf_op jit(solution)/shard_map/ppermute | solution.py:394
  13.4 0.5 %collective-permute-done.1.refs_1_ = bf16[8,1152]{1,0:T(8,128)(2,1)S(1)} collective-permute-done((bf16[8,1152]{1,0:T(8,128)(2,1)S(1)}, bf16[8,1152]{1,0:T(8,128)(2,1)S(1)}, u32[]{:S(2)}, u32[]{:S(2)}) %collective-permute-start.1) | collective-permute-done | bytes 18464 | tf_op jit(solution)/shard_map/ppermute | solution.py:394
  14.0 0.0 copy-done.1
  14.0 0.0 copy-done
  14.0 2.4 %other_half.1 = (bf16[128,768]{1,0:T(8,128)(2,1)S(1)}, bf16[128,1024]{1,0:T(8,128)(2,1)S(1)}, bf16[32,128]{1,0:T(8,128)(2,1)S(1)}, f32[32,128]{1,0:T(8,128)S(1)}) custom-call(bf16[32,1152]{1,0:T(8,128)(2,1)S(1)} %cat.3.x_ref, bf16[8,1024,768]{2,1,0:T(8,128)(2,1)S(1)} %copy-done, bf16[8,1024,768]{2,1,0:T(8,128)(2,1)S(1)} %copy-done.1, ...), custom_call_target="tpu_custom_call" | custom-call | flops 65536 | bytes 65536 | tf_op jit(solution)/shard_map/other_half/pallas_call | solution.py:31
  16.4 0.0 collective-permute-start.4
  16.4 0.0 slice-start
  16.4 0.0 slice-start.1
  16.4 1.9 %own_half.1.a_ref = f32[128,768]{1,0:T(8,128)S(1)} custom-call(bf16[128,1024]{1,0:T(8,128)(2,1)S(1)} %get-tuple-element.22.xs_ref, bf16[8,1024,768]{2,1,0:T(8,128)(2,1)S(1)} %copy-done, bf16[8,1024,768]{2,1,0:T(8,128)(2,1)S(1)} %copy-done.1, f32[6,8,8,128]{3,2,1,0:T(8,128)S(1)} %get-tuple-element.20.refs_2_.gs_ref, f32[6,8,8,128]{3,2,1,0:T(8,128)S(1)} %get-tuple-element.21.us_ref), custom_call_target="tpu_custom_call" | custom-call | flops 65536 | bytes 65536 | tf_op jit(solution)/shard_map/own_half/pallas_call | solution.py:31
  18.3 0.0 slice-start.2
  18.3 0.0 collective-permute-done.4.b_ref
  18.3 0.1 add_round.1
  18.4 1.6 %collective-permute-start.5 = (bf16[128,768]{1,0:T(8,128)(2,1)S(1)}, bf16[128,768]{1,0:T(8,128)(2,1)S(1)}, u32[]{:S(2)}, u32[]{:S(2)}) collective-permute-start(bf16[128,768]{1,0:T(8,128)(2,1)S(1)} %get-tuple-element.25), channel_id=1, source_target_pairs={{0,2},{1,3},{2,0},{3,1},{4,6},{5,7},{6,4},{7,5},{8,10},{9,11},{10,... | collective-permute-start | bytes 589832 | tf_op jit(solution)/shard_map/ppermute | solution.py:383
  20.0 5.8 %collective-permute-done.5.b_ref = bf16[128,768]{1,0:T(8,128)(2,1)S(1)} collective-permute-done((bf16[128,768]{1,0:T(8,128)(2,1)S(1)}, bf16[128,768]{1,0:T(8,128)(2,1)S(1)}, u32[]{:S(2)}, u32[]{:S(2)}) %collective-permute-start.5) | collective-permute-done | bytes 196640 | tf_op jit(solution)/shard_map/ppermute | solution.py:383
  25.8 0.1 activate.1.h_ref
  25.9 0.1 collective-permute-start.6
  25.9 0.0 slice-done
  26.0 0.0 slice-done.1
  26.0 0.0 slice-done.2
  26.0 1.3 %down_own.1.rest_0_ = f32[32,1024]{1,0:T(8,128)S(1)} custom-call(bf16[128,384]{1,0:T(8,128)(2,1)S(1)} %activate.1.h_ref, bf16[32,128]{1,0:T(8,128)(2,1)S(1)} %get-tuple-element.26.sel_ref, f32[32,128]{1,0:T(8,128)S(1)} %get-tuple-element.27.wt_ref, bf16[8,768,1024]{2,1,0:T(8,128)(2,1)S(1)} %bitcast.4, f32[6,8,8,128]{3,2,1,0:T(8,128)S(1)} %get-tuple-element.28.ds_ref), custom_call_target="tpu_custom_call" | custom-call | flops 65536 | bytes 65536 | tf_op jit(solution)/shard_map/down_own/pallas_call | solution.py:31
  27.3 0.0 collective-permute-done.6.h_ref
  27.3 1.3 %down_other.1 = (f32[8,1024]{1,0:T(8,128)S(1)}, bf16[8,1024]{1,0:T(8,128)(2,1)S(1)}, bf16[8,1024]{1,0:T(8,128)(2,1)S(1)}, bf16[8,1024]{1,0:T(8,128)(2,1)S(1)}) custom-call(bf16[128,384]{1,0:T(8,128)(2,1)S(1)} %collective-permute-done.6.h_ref, bf16[32,128]{1,0:T(8,128)(2,1)S(1)} %get-tuple-element.26.sel_ref, f32[32,128]{1,0:T(8,128)S(1)} %get-tuple-element.27.wt_ref, ...), custom_call_target="tpu_custom_call" | custom-call | flops 65536 | bytes 65536 | tf_op jit(solution)/shard_map/down_other/pallas_call | solution.py:31
  28.7 1.4 %collective-permute-start.7 = (bf16[8,1024]{1,0:T(8,128)(2,1)S(1)}, bf16[8,1024]{1,0:T(8,128)(2,1)S(1)}, u32[]{:S(2)}, u32[]{:S(2)}) collective-permute-start(bf16[8,1024]{1,0:T(8,128)(2,1)S(1)} %get-tuple-element.30), channel_id=1, source_target_pairs={{0,20},{4,16},{8,28},{12,24},{16,4},{20,0},{24,12},{28,8},{1,21},{... | collective-permute-start | bytes 49160 | tf_op jit(solution)/shard_map/ppermute | solution.py:394
  30.1 0.5 %collective-permute-start.8 = (bf16[8,1024]{1,0:T(8,128)(2,1)S(1)}, bf16[8,1024]{1,0:T(8,128)(2,1)S(1)}, u32[]{:S(2)}, u32[]{:S(2)}) collective-permute-start(bf16[8,1024]{1,0:T(8,128)(2,1)S(1)} %get-tuple-element.31), channel_id=1, source_target_pairs={{0,16},{4,20},{8,24},{12,28},{16,0},{20,4},{24,8},{28,12},{1,17},{... | collective-permute-start | bytes 49160 | tf_op jit(solution)/shard_map/ppermute | solution.py:394
  30.6 1.6 %collective-permute-start.9 = (bf16[8,1024]{1,0:T(8,128)(2,1)S(1)}, bf16[8,1024]{1,0:T(8,128)(2,1)S(1)}, u32[]{:S(2)}, u32[]{:S(2)}) collective-permute-start(bf16[8,1024]{1,0:T(8,128)(2,1)S(1)} %get-tuple-element.32), channel_id=1, source_target_pairs={{0,4},{4,0},{8,12},{12,8},{16,20},{20,16},{24,28},{28,24},{1,5},{5... | collective-permute-start | bytes 49160 | tf_op jit(solution)/shard_map/ppermute | solution.py:394
  32.2 1.1 %collective-permute-done.7.rest_0_ = bf16[8,1024]{1,0:T(8,128)(2,1)S(1)} collective-permute-done((bf16[8,1024]{1,0:T(8,128)(2,1)S(1)}, bf16[8,1024]{1,0:T(8,128)(2,1)S(1)}, u32[]{:S(2)}, u32[]{:S(2)}) %collective-permute-start.7) | collective-permute-done | bytes 16416 | tf_op jit(solution)/shard_map/ppermute | solution.py:394
  33.4 0.5 %collective-permute-done.8.rest_1_ = bf16[8,1024]{1,0:T(8,128)(2,1)S(1)} collective-permute-done((bf16[8,1024]{1,0:T(8,128)(2,1)S(1)}, bf16[8,1024]{1,0:T(8,128)(2,1)S(1)}, u32[]{:S(2)}, u32[]{:S(2)}) %collective-permute-start.8) | collective-permute-done | bytes 16416 | tf_op jit(solution)/shard_map/ppermute | solution.py:394
  33.8 0.5 %collective-permute-done.9.rest_2_ = bf16[8,1024]{1,0:T(8,128)(2,1)S(1)} collective-permute-done((bf16[8,1024]{1,0:T(8,128)(2,1)S(1)}, bf16[8,1024]{1,0:T(8,128)(2,1)S(1)}, u32[]{:S(2)}, u32[]{:S(2)}) %collective-permute-start.9) | collective-permute-done | bytes 16416 | tf_op jit(solution)/shard_map/ppermute | solution.py:394
  34.3 2.7 %collective-permute-start.10 = (bf16[4,1024]{1,0:T(4,128)(2,1)S(1)}, bf16[4,1024]{1,0:T(4,128)(2,1)S(1)}, u32[]{:S(2)}, u32[]{:S(2)}) collective-permute-start(bf16[4,1024]{1,0:T(4,128)(2,1)S(1)} %get-tuple-element.34), channel_id=1, source_target_pairs={{0,8},{4,12},{8,0},{12,4},{16,24},{20,28},{24,16},{28,20},{1,9},{5... | collective-permute-start | bytes 24584 | tf_op jit(solution)/shard_map/ppermute | solution.py:394
  37.0 1.9 %collective-permute-done.10.rest_0_ = bf16[4,1024]{1,0:T(4,128)(2,1)S(1)} collective-permute-done((bf16[4,1024]{1,0:T(4,128)(2,1)S(1)}, bf16[4,1024]{1,0:T(4,128)(2,1)S(1)}, u32[]{:S(2)}, u32[]{:S(2)}) %collective-permute-start.10) | collective-permute-done | bytes 8224 | tf_op jit(solution)/shard_map/ppermute | solution.py:394
  38.9 0.6 %finish.1 = bf16[4,1024]{1,0:T(4,128)(2,1)} custom-call(f32[4,1024]{1,0:T(4,128)S(1)} %get-tuple-element.33.a_ref, bf16[4,1024]{1,0:T(4,128)(2,1)S(1)} %collective-permute-done.10.rest_0_), custom_call_target="tpu_custom_call" | custom-call | tf_op jit(solution)/shard_map/finish/pallas_call | solution.py:31
  (4 shorter events, 0.0 us)
Async XLA Ops:
  0.0 14.0 %copy-start.1 = (bf16[8,1024,768]{2,1,0:T(8,128)(2,1)S(1)}, bf16[8,1024,768]{2,1,0:T(8,128)(2,1)}, u32[]{:S(2)}) copy-start(bf16[8,1024,768]{2,1,0:T(8,128)(2,1)} %uw_ref.3) | copy-start | bytes 37748740
  0.0 14.0 %copy-start = (bf16[8,1024,768]{2,1,0:T(8,128)(2,1)S(1)}, bf16[8,1024,768]{2,1,0:T(8,128)(2,1)}, u32[]{:S(2)}) copy-start(bf16[8,1024,768]{2,1,0:T(8,128)(2,1)} %gw_ref.3) | copy-start | bytes 37748740
  1.0 5.9 %collective-permute-start = (bf16[4,1152]{1,0:T(4,128)(2,1)S(1)}, bf16[4,1152]{1,0:T(4,128)(2,1)S(1)}, u32[]{:S(2)}, u32[]{:S(2)}) collective-permute-start(bf16[4,1152]{1,0:T(4,128)(2,1)S(1)} %pack.1.refs_3_.refs_0_), channel_id=1, source_target_pairs={{0,8},{4,12},{8,0},{12,4},{16,24},{20,28},{24,16},{28,20},{1,9},{5... | collective-permute-start | bytes 27656 | tf_op jit(solution)/shard_map/ppermute | solution.py:394
  7.0 4.8 %collective-permute-start.3 = (bf16[8,1152]{1,0:T(8,128)(2,1)S(1)}, bf16[8,1152]{1,0:T(8,128)(2,1)S(1)}, u32[]{:S(2)}, u32[]{:S(2)}) collective-permute-start(bf16[8,1152]{1,0:T(8,128)(2,1)S(1)} %cat.2.refs_0_), channel_id=1, source_target_pairs={{0,20},{4,16},{8,28},{12,24},{16,4},{20,0},{24,12},{28,8},{1,21},{... | collective-permute-start | bytes 55304 | tf_op jit(solution)/shard_map/ppermute | solution.py:394
  9.7 3.8 %collective-permute-start.2 = (bf16[8,1152]{1,0:T(8,128)(2,1)S(1)}, bf16[8,1152]{1,0:T(8,128)(2,1)S(1)}, u32[]{:S(2)}, u32[]{:S(2)}) collective-permute-start(bf16[8,1152]{1,0:T(8,128)(2,1)S(1)} %cat.2.refs_0_), channel_id=1, source_target_pairs={{0,16},{4,20},{8,24},{12,28},{16,0},{20,4},{24,8},{28,12},{1,17},{... | collective-permute-start | bytes 55304 | tf_op jit(solution)/shard_map/ppermute | solution.py:394
  10.2 3.8 %collective-permute-start.1 = (bf16[8,1152]{1,0:T(8,128)(2,1)S(1)}, bf16[8,1152]{1,0:T(8,128)(2,1)S(1)}, u32[]{:S(2)}, u32[]{:S(2)}) collective-permute-start(bf16[8,1152]{1,0:T(8,128)(2,1)S(1)} %cat.2.refs_0_), channel_id=1, source_target_pairs={{0,4},{4,0},{8,12},{12,8},{16,20},{20,16},{24,28},{28,24},{1,5},{5... | collective-permute-start | bytes 55304 | tf_op jit(solution)/shard_map/ppermute | solution.py:394
  16.4 2.0 %collective-permute-start.4 = (bf16[128,768]{1,0:T(8,128)(2,1)S(1)}, bf16[128,768]{1,0:T(8,128)(2,1)S(1)}, u32[]{:S(2)}, u32[]{:S(2)}) collective-permute-start(bf16[128,768]{1,0:T(8,128)(2,1)S(1)} %get-tuple-element.23), channel_id=1, source_target_pairs={{0,1},{1,0},{2,3},{3,2},{4,5},{5,4},{6,7},{7,6},{8,9},{9,8},{10,11... | collective-permute-start | bytes 589832 | tf_op jit(solution)/shard_map/ppermute | solution.py:383
  16.4 9.6 %slice-start = ((s8[12582912]{0:T(1024)(128)(4,1)}), s8[4194304]{0:T(1024)(128)(4,1)S(1)}, s32[]{:S(2)}) async-start(s8[12582912]{0:T(1024)(128)(4,1)} %bitcast.3), calls=%async_computation | async-start | bytes 8388608
  16.4 9.6 %slice-start.1 = ((s8[12582912]{0:T(1024)(128)(4,1)}), s8[4194304]{0:T(1024)(128)(4,1)S(1)}, s32[]{:S(2)}) async-start(s8[12582912]{0:T(1024)(128)(4,1)} %bitcast.3), calls=%async_computation.1 | async-start | bytes 8388608
  18.3 7.6 %slice-start.2 = ((s8[12582912]{0:T(1024)(128)(4,1)}), s8[4194304]{0:T(1024)(128)(4,1)S(1)}, s32[]{:S(2)}) async-start(s8[12582912]{0:T(1024)(128)(4,1)} %bitcast.3), calls=%async_computation.2 | async-start | bytes 8388608
  18.4 7.4 %collective-permute-start.5 = (bf16[128,768]{1,0:T(8,128)(2,1)S(1)}, bf16[128,768]{1,0:T(8,128)(2,1)S(1)}, u32[]{:S(2)}, u32[]{:S(2)}) collective-permute-start(bf16[128,768]{1,0:T(8,128)(2,1)S(1)} %get-tuple-element.25), channel_id=1, source_target_pairs={{0,2},{1,3},{2,0},{3,1},{4,6},{5,7},{6,4},{7,5},{8,10},{9,11},{10,... | collective-permute-start | bytes 589832 | tf_op jit(solution)/shard_map/ppermute | solution.py:383
  25.9 1.5 %collective-permute-start.6 = (bf16[128,384]{1,0:T(8,128)(2,1)S(1)}, bf16[128,384]{1,0:T(8,128)(2,1)S(1)}, u32[]{:S(2)}, u32[]{:S(2)}) collective-permute-start(bf16[128,384]{1,0:T(8,128)(2,1)S(1)} %activate.1.h_ref), channel_id=1, source_target_pairs={{0,1},{1,0},{2,3},{3,2},{4,5},{5,4},{6,7},{7,6},{8,9},{9,8},{10,11... | collective-permute-start | bytes 294920 | tf_op jit(solution)/shard_map/ppermute | solution.py:383
  28.7 4.7 %collective-permute-start.7 = (bf16[8,1024]{1,0:T(8,128)(2,1)S(1)}, bf16[8,1024]{1,0:T(8,128)(2,1)S(1)}, u32[]{:S(2)}, u32[]{:S(2)}) collective-permute-start(bf16[8,1024]{1,0:T(8,128)(2,1)S(1)} %get-tuple-element.30), channel_id=1, source_target_pairs={{0,20},{4,16},{8,28},{12,24},{16,4},{20,0},{24,12},{28,8},{1,21},{... | collective-permute-start | bytes 49160 | tf_op jit(solution)/shard_map/ppermute | solution.py:394
  30.1 3.7 %collective-permute-start.8 = (bf16[8,1024]{1,0:T(8,128)(2,1)S(1)}, bf16[8,1024]{1,0:T(8,128)(2,1)S(1)}, u32[]{:S(2)}, u32[]{:S(2)}) collective-permute-start(bf16[8,1024]{1,0:T(8,128)(2,1)S(1)} %get-tuple-element.31), channel_id=1, source_target_pairs={{0,16},{4,20},{8,24},{12,28},{16,0},{20,4},{24,8},{28,12},{1,17},{... | collective-permute-start | bytes 49160 | tf_op jit(solution)/shard_map/ppermute | solution.py:394
  30.6 3.7 %collective-permute-start.9 = (bf16[8,1024]{1,0:T(8,128)(2,1)S(1)}, bf16[8,1024]{1,0:T(8,128)(2,1)S(1)}, u32[]{:S(2)}, u32[]{:S(2)}) collective-permute-start(bf16[8,1024]{1,0:T(8,128)(2,1)S(1)} %get-tuple-element.32), channel_id=1, source_target_pairs={{0,4},{4,0},{8,12},{12,8},{16,20},{20,16},{24,28},{28,24},{1,5},{5... | collective-permute-start | bytes 49160 | tf_op jit(solution)/shard_map/ppermute | solution.py:394
  34.3 4.6 %collective-permute-start.10 = (bf16[4,1024]{1,0:T(4,128)(2,1)S(1)}, bf16[4,1024]{1,0:T(4,128)(2,1)S(1)}, u32[]{:S(2)}, u32[]{:S(2)}) collective-permute-start(bf16[4,1024]{1,0:T(4,128)(2,1)S(1)} %get-tuple-element.34), channel_id=1, source_target_pairs={{0,8},{4,12},{8,0},{12,4},{16,24},{20,28},{24,16},{28,20},{1,9},{5... | collective-permute-start | bytes 24584 | tf_op jit(solution)/shard_map/ppermute | solution.py:394

commit v6 on v5

--- a/solution.py
+++ b/solution.py
@@ -1,5 +1,3 @@
-import functools
-
 import jax
 import jax.numpy as jnp
 from jax import lax
@@ -25,7 +23,7 @@
     return jax.ShapeDtypeStruct(shape, dtype)
 
 
-def run(kernel, out_shape, in_specs, args, name, limit=2 << 20, flops=0, bytes_=0, **more):
+def run(kernel, out_shape, in_specs, args, limit=2 << 20, flops=0, bytes_=0, **more):
     outs = out_shape if isinstance(out_shape, (list, tuple)) else [out_shape]
     specs = [VM] * len(outs)
     return pl.pallas_call(
@@ -35,7 +33,6 @@
         out_specs=specs if isinstance(out_shape, (list, tuple)) else VM,
         compiler_params=pltpu.CompilerParams(vmem_limit_bytes=limit),
         cost_estimate=pl.CostEstimate(flops=flops, bytes_accessed=bytes_, transcendentals=0),
-        name=name,
         **more,
     )(*args)
 
@@ -86,7 +83,6 @@
         sds((rows, width + LANES), BF),
         [HB] * len(arrays),
         arrays,
-        "pack",
         flops=hint,
         scratch_shapes=[pltpu.VMEM(a.shape, a.dtype) for a in arrays]
         + [pltpu.SemaphoreType.DMA((len(arrays),))],
@@ -105,7 +101,6 @@
         sds((len(pieces) * rows,) + pieces[0].shape[1:], pieces[0].dtype),
         [VM] * (len(pieces) + len(after)),
         (*pieces, *after),
-        "cat",
         flops=hint,
     )
 
@@ -131,7 +126,6 @@
         [sds((s.shape[0], s.shape[2], s.shape[1], LANES), F32) for s in scales],
         [HB] * len(scales) + [VM],
         (*[in_hbm(s) for s in scales], after),
-        "spread_scales",
         bytes_=1 << 20,
         scratch_shapes=[pltpu.VMEM(s.shape, s.dtype) for s in scales]
         + [pltpu.SemaphoreType.DMA((len(scales),))],
@@ -178,7 +172,7 @@
     return (block.reshape(QB // 16, 16, QB) * row[None]).reshape(QB, QB)
 
 
-def half_products(xs_ref, gw, uw, gs, us, o_ref, half):
+def half_products(xs_ref, gw, uw, gs, us, o_ref, half, chosen):
     experts, width, hidden = gw.shape
     n = hidden // 2 // QB
     per = xs_ref.shape[0] // experts
@@ -190,7 +184,7 @@
         part = w[e, q * QB : (q + 1) * QB, pl.ds(starts[j], QB)]
         return scaled(part, scale, half * n + j, q, e)
 
-    for e in range(experts):
+    for row, e in enumerate(chosen):
         xs = xs_ref[e * per : (e + 1) * per, :]
         for at in range(0, len(columns), group):
             acc = jnp.zeros((per, group * QB), F32)
@@ -204,7 +198,7 @@
                 acc = acc + jnp.dot(
                     xs[:, d * QB : (d + deep) * QB], rhs, preferred_element_type=F32
                 )
-            o_ref[e * per : (e + 1) * per, at * QB : (at + group) * QB] = acc.astype(o_ref.dtype)
+            o_ref[row * per : (row + 1) * per, at * QB : (at + group) * QB] = acc.astype(o_ref.dtype)
 
 
 def other_half(x, gw, uw, gs, us, top, rows_dev, block_count):
@@ -218,7 +212,7 @@
         wt_ref[...] = weights
         xs_ref[...] = slot_rows
         half = 1 - lax.rem(lax.axis_index("pool"), 2)
-        half_products(xs_ref, gw_ref, uw_ref, gs_ref, us_ref, o_ref, half)
+        half_products(xs_ref, gw_ref, uw_ref, gs_ref, us_ref, o_ref, half, range(experts))
 
     return run(
         kernel,
@@ -230,91 +224,90 @@
         ],
         [VM] * 5,
         (x, in_vmem(gw), in_vmem(uw), gs, us),
-        "other_half",
         limit=8 << 20,
         flops=NEAR,
         bytes_=NEAR,
     )
 
 
-def own_half(xs, gw, uw, gs, us):
-    experts, width, hidden = gw.shape
-    slots = xs.shape[0]
-
-    def kernel(xs_ref, gw_ref, uw_ref, gs_ref, us_ref, o_ref):
+def own_half(xs, gw, uw, gs, us, chosen, after):
+    experts, _, hidden = gw.shape
+    slots = xs.shape[0] // experts * len(chosen)
+
+    def kernel(xs_ref, gw_ref, uw_ref, gs_ref, us_ref, *rest):
+        o_ref = rest[-1]
         half = lax.rem(lax.axis_index("pool"), 2)
-        half_products(xs_ref, gw_ref, uw_ref, gs_ref, us_ref, o_ref, half)
+        half_products(xs_ref, gw_ref, uw_ref, gs_ref, us_ref, o_ref, half, chosen)
 
     return run(
         kernel,
         sds((slots, hidden), F32),
-        [VM] * 5,
-        (xs, in_vmem(gw), in_vmem(uw), gs, us),
-        "own_half",
+        [VM] * (5 + len(after)),
+        (xs, in_vmem(gw), in_vmem(uw), gs, us, *after),
         limit=8 << 20,
         flops=NEAR,
         bytes_=NEAR,
     )
 
 
-def add_round(own, got, hint):
+def add_round(own, got, first, hint):
+    rows = own.shape[0]
+
     def kernel(a_ref, b_ref, o_ref, r_ref):
-        total = a_ref[...] + b_ref[...].astype(F32)
+        total = a_ref[...] + b_ref[first : first + rows].astype(F32)
         o_ref[...] = total
         r_ref[...] = total.astype(BF)
 
-    return run(kernel, [sds(own.shape, F32), sds(own.shape, BF)], [VM] * 2, (own, got), "add_round", flops=hint)
-
-
-def activate(own, got):
+    return run(kernel, [sds(own.shape, F32), sds(own.shape, BF)], [VM] * 2, (own, got), flops=hint)
+
+
+def activate(own, got, after):
     slots, hidden = own.shape
     n = hidden // 2
 
-    def kernel(a_ref, b_ref, o_ref):
+    def kernel(a_ref, b_ref, *rest):
+        o_ref = rest[-1]
         gate = a_ref[:, :n] + b_ref[:, :n].astype(F32)
         up = a_ref[:, n:] + b_ref[:, n:].astype(F32)
         o_ref[...] = (jax.nn.silu(gate) * up).astype(BF)
 
-    return run(
-        kernel,
-        sds((slots, n), BF),
-        [VM] * 2,
-        (own, got),
-        "activate",
-    )
-
-
-def spread_rows(h_ref, sel_ref, wt_ref, experts):
-    rows, slots = sel_ref.shape
-    per = slots // experts
-    sel = sel_ref[...].astype(F32)
+    return run(kernel, sds((slots, n), BF), [VM] * (2 + len(after)), (own, got, *after))
+
+
+def spread_rows(h_ref, sel_ref, wt_ref, per, chosen):
+    rows = sel_ref.shape[0]
+    low = chosen[0] * per
+    slots = h_ref.shape[0]
+    sel = sel_ref[:, low : low + slots].astype(F32)
     owner = iota((rows, slots), 1) // per
-    stack = jnp.concatenate([jnp.where(owner == e, sel, 0.0) for e in range(experts)], axis=0)
+    stack = jnp.concatenate(
+        [jnp.where(owner == i, sel, 0.0) for i in range(len(chosen))], axis=0
+    )
     spread = jnp.dot(stack.astype(BF), h_ref[...], preferred_element_type=F32)
     weights = wt_ref[...]
-    return [
-        (spread[e * rows : (e + 1) * rows] * weights[:, e : e + 1]).astype(BF)
-        for e in range(experts)
-    ]
-
-
-def down_kernel(hid, sel, wt, dw, ds, own, parts_out):
+    return {
+        e: (spread[i * rows : (i + 1) * rows] * weights[:, e : e + 1]).astype(BF)
+        for i, e in enumerate(chosen)
+    }
+
+
+def down_kernel(hid, sel, wt, dw, ds, acc_in, chosen, other, parts_out):
     experts, hidden, width = dw.shape
     n = hidden // 2 // QB
-    rows = sel.shape[0]
+    rows, slots = sel.shape
+    per = slots // experts
     keep = rows // parts_out
-    last = own is not None
-    given = [own] if last else []
+    last = parts_out > 1
+    given = [] if acc_in is None else [acc_in]
     group = 2
-    pieces = [(e, j) for e in range(experts) for j in range(n)]
+    pieces = [(e, j) for e in chosen for j in range(n)]
     deep = 2 if len(pieces) % 2 == 0 else 1
 
     def kernel(h_ref, sel_ref, wt_ref, dw_ref, ds_ref, *rest):
         given_refs, outs = rest[: len(given)], rest[len(given) :]
         half = lax.rem(lax.axis_index("pool"), 2)
-        half = 1 - half if last else half
-        parts = spread_rows(h_ref, sel_ref, wt_ref, experts)
-
+        half = 1 - half if other else half
+        parts = spread_rows(h_ref, sel_ref, wt_ref, per, chosen)
         starts = [pl.multiple_of((half * n + j) * QB, QB) for j in range(n)]
 
         def block(e, j, q):
@@ -323,7 +316,7 @@
 
         for c in range(0, width // QB, group):
             at = slice(c * QB, (c + group) * QB)
-            acc = given_refs[0][:, at] if last else jnp.zeros((rows, group * QB), F32)
+            acc = given_refs[0][:, at] if given else jnp.zeros((rows, group * QB), F32)
             for p in range(0, len(pieces), deep):
                 some = pieces[p : p + deep]
                 lhs = jnp.concatenate([parts[e][:, j * QB : (j + 1) * QB] for e, j in some], axis=1)
@@ -338,10 +331,9 @@
 
     return run(
         kernel,
-        [sds((keep, width), F32)] + [sds((keep, width), BF)] * (parts_out - 1) if last else [sds((rows, width), F32)],
+        [sds((keep, width), F32)] + [sds((keep, width), BF)] * (parts_out - 1),
         [VM] * (5 + len(given)),
         (hid, sel, wt, in_vmem(dw), ds, *given),
-        "down_other" if last else "down_own",
         limit=8 << 20,
         flops=NEAR,
         bytes_=NEAR,
@@ -365,7 +357,6 @@
         [sds((keep, width), F32), sds((keep, width), BF)],
         [VM] * (1 + len(got)),
         (own, *got),
-        "fold",
     )
 
 
@@ -376,7 +367,7 @@
             total = total + ref[...].astype(F32)
         rest[-1][...] = total.astype(BF)
 
-    return run(kernel, sds(own.shape, BF), [VM] * (1 + len(got)), (own, *got), "finish")
+    return run(kernel, sds(own.shape, BF), [VM] * (1 + len(got)), (own, *got))
 
 
 def swap(x, axis, bit):
@@ -400,7 +391,7 @@
 
 def per_device(tokens, routes, gate_fixed, gw, uw, dw, gs, us, ds):
     n_seq, n_head, n_pool = (lax.axis_size(a) for a in ("seq", "head", "pool"))
-    rows_dev, width = tokens.shape
+    rows_dev, _ = tokens.shape
     top = routes.shape[1]
     hops = [("head", b) for b in reversed(bits(n_head))] + [("seq", b) for b in bits(n_seq)]
 
@@ -418,14 +409,29 @@
 
     send, xs, sel, wt = other_half(x, gw, uw, gs, us, top, rows_dev, n_seq * n_head)
     got = swap(send, "pool", 1)
-    own = own_half(xs, gw, uw, gs, us)
-    for bit in bits(n_pool)[1:]:
-        own, send = add_round(own, got, HINT * dw.size)
-        got = swap(send, "pool", bit)
-    hid = activate(own, got)
-    other = swap(hid, "pool", 1)
-    (acc,) = down_kernel(hid, sel, wt, dw, ds, None, 4)
-    acc, to_a, to_b, to_far = down_kernel(other, sel, wt, dw, ds, acc, 4)
+    experts = gw.shape[0]
+    per = xs.shape[0] // experts
+    cut = experts // 2
+    parts = [range(cut), range(cut, experts)] if cut else [range(experts)]
+    steps = bits(n_pool)[1:]
+    sums, after = [], []
+    for i, part in enumerate(parts):
+        own = own_half(xs, gw, uw, gs, us, part, after)
+        first, hint = part[0] * per, HINT * dw.size
+        arrived = got
+        for bit in steps:
+            own, send = add_round(own, arrived, first, hint if i + 1 == len(parts) else 0)
+            arrived, first = swap(send, "pool", bit), 0
+            after = [send]
+        sums.append((own, arrived))
+    acc = None
+    for i, (part, pair) in enumerate(zip(parts, sums)):
+        hid = activate(*pair, [] if acc is None else [acc])
+        other = swap(hid, "pool", 1)
+        (acc,) = down_kernel(hid, sel, wt, dw, ds, acc, part, False, 1)
+        ends = i + 1 == len(parts)
+        acc, *sends = down_kernel(other, sel, wt, dw, ds, acc, part, True, 4 if ends else 1)
+    to_a, to_b, to_far = sends
     far, near_a, near_b = hop(to_far, a, b), hop(to_a, a), hop(to_b, b)
     got = [far, near_b, near_a]
     for step in reversed(single):

time: 39.9 us -> 40.1 us (level)
  waiting for transfers between devices: 13.2 us -> 11.7 us
  Pallas kernels: 10.6 us -> 11.4 us
  starting transfers between devices: 15.6 us -> 16.4 us
    ppermute x3 -> x5, waiting for transfers between devices: 5.79 us -> 4.52 us  [swap(): lax.ppermute(x, axis, [(j, j ^ bit) for j in range(lax.axis_size(axis))])]
    pallas_call x12 -> x17, Pallas kernels: 10.6 us -> 11.4 us  [run(): pl.pallas_call(kernel, out_shape=out_shape, in_specs=in_specs, out_specs=...]
    ppermute x3 -> x5, starting transfers between devices: 1.66 us -> 2.39 us  [swap(): lax.ppermute(x, axis, [(j, j ^ bit) for j in range(lax.axis_size(axis))])]
  transfers between devices with their start and end apart: 11 -> 13, of which waited for: 8 -> 11; matrix products, arithmetic and copies ran while one was open for 0% -> 0% of each run, Pallas kernels for 13% -> 13%
where the time goes in v6:
time: 40.1 us; the launch traced here: 39.7 us
  starting transfers between devices  16.4 us (41%)
  waiting for transfers between devices  11.7 us (29%)
  Pallas kernels  11.4 us (28%)
    ppermute x8, starting transfers between devices, hop(): return lax.ppermute(x, ('seq', 'head'), pairs)  14 us
    pallas_call x17, Pallas kernels, run(): pl.pallas_call(kernel, out_shape=out_shape, in_specs=in_specs, out_specs=...  11.4 us
    ppermute x8, waiting for transfers between devices, hop(): return lax.ppermute(x, ('seq', 'head'), pairs)  7.21 us
    ppermute x5, waiting for transfers between devices, swap(): lax.ppermute(x, axis, [(j, j ^ bit) for j in range(lax.axis_size(axis))])  4.52 us
    ppermute x5, starting transfers between devices, swap(): lax.ppermute(x, axis, [(j, j ^ bit) for j in range(lax.axis_size(axis))])  2.39 us
  transfers between devices with their start and end apart: 13, of which 11 were waited for; matrix products, arithmetic and copies ran while one was open for 0% of the time, Pallas kernels for 13%

profile of v6, /device:TPU:0, one launch (start us, length us, event | category | flops | bytes accessed | tf_op | source)
XLA Modules:
  0.0 39.7 jit_solution(13044882084794234619)
XLA Ops:
  0.0 0.0 copy-start.1
  0.0 0.0 copy-start
  0.0 1.0 %shard_map.91.refs_3_.refs_0_ = bf16[4,1152]{1,0:T(4,128)(2,1)S(1)} custom-call(bf16[4,1024]{1,0:T(4,128)(2,1)} %t_in.1, s32[4,8]{1,0:T(4,128)} %r_in.1, s32[4,8]{1,0:T(4,128)} %g_in.1), custom_call_target="tpu_custom_call" | custom-call | flops 12582912000 | tf_op jit(solution)/shard_map/pallas_call | solution.py:29
  1.0 4.1 %collective-permute-start = (bf16[4,1152]{1,0:T(4,128)(2,1)S(1)}, bf16[4,1152]{1,0:T(4,128)(2,1)S(1)}, u32[]{:S(2)}, u32[]{:S(2)}) collective-permute-start(bf16[4,1152]{1,0:T(4,128)(2,1)S(1)} %shard_map.91.refs_3_.refs_0_), channel_id=1, source_target_pairs={{0,8},{4,12},{8,0},{12,4},{16,24},{20,28},{24,16},{28,20},{1,9},{5... | collective-permute-start | bytes 27656 | tf_op jit(solution)/shard_map/ppermute | solution.py:385
  5.2 1.8 %shard_map.92 = (f32[6,8,8,128]{3,2,1,0:T(8,128)S(1)}, f32[6,8,8,128]{3,2,1,0:T(8,128)S(1)}, f32[6,8,8,128]{3,2,1,0:T(8,128)S(1)}) custom-call(bf16[6,8,8]{2,1,0:T(8,128)(2,1)} %bitcast.5, bf16[6,8,8]{2,1,0:T(8,128)(2,1)} %bitcast.6, bf16[6,8,8]{2,1,0:T(8,128)(2,1)} %bitcast.7, bf16[4,1152]{1,0:T(4,128)(2,1)S(1)} %shard_map.91.refs_3_.refs_0_), custom_call_target="tpu_custom_call" | custom-call | bytes 1048576 | tf_op jit(solution)/shard_map/pallas_call | solution.py:29
  7.0 0.0 collective-permute-done.refs_1_
  7.0 2.6 %collective-permute-start.3 = (bf16[8,1152]{1,0:T(8,128)(2,1)S(1)}, bf16[8,1152]{1,0:T(8,128)(2,1)S(1)}, u32[]{:S(2)}, u32[]{:S(2)}) collective-permute-start(bf16[8,1152]{1,0:T(8,128)(2,1)S(1)} %shard_map.93.refs_0_), channel_id=1, source_target_pairs={{0,20},{4,16},{8,28},{12,24},{16,4},{20,0},{24,12},{28,8},{1,21},{... | collective-permute-start | bytes 55304 | tf_op jit(solution)/shard_map/ppermute | solution.py:385
  9.7 0.5 %collective-permute-start.2 = (bf16[8,1152]{1,0:T(8,128)(2,1)S(1)}, bf16[8,1152]{1,0:T(8,128)(2,1)S(1)}, u32[]{:S(2)}, u32[]{:S(2)}) collective-permute-start(bf16[8,1152]{1,0:T(8,128)(2,1)S(1)} %shard_map.93.refs_0_), channel_id=1, source_target_pairs={{0,16},{4,20},{8,24},{12,28},{16,0},{20,4},{24,8},{28,12},{1,17},{... | collective-permute-start | bytes 55304 | tf_op jit(solution)/shard_map/ppermute | solution.py:385
  10.2 0.4 collective-permute-start.1
  10.6 1.3 %collective-permute-done.3.refs_3_ = bf16[8,1152]{1,0:T(8,128)(2,1)S(1)} collective-permute-done((bf16[8,1152]{1,0:T(8,128)(2,1)S(1)}, bf16[8,1152]{1,0:T(8,128)(2,1)S(1)}, u32[]{:S(2)}, u32[]{:S(2)}) %collective-permute-start.3) | collective-permute-done | bytes 18464 | tf_op jit(solution)/shard_map/ppermute | solution.py:385
  11.8 1.6 %collective-permute-done.2.refs_2_ = bf16[8,1152]{1,0:T(8,128)(2,1)S(1)} collective-permute-done((bf16[8,1152]{1,0:T(8,128)(2,1)S(1)}, bf16[8,1152]{1,0:T(8,128)(2,1)S(1)}, u32[]{:S(2)}, u32[]{:S(2)}) %collective-permute-start.2) | collective-permute-done | bytes 18464 | tf_op jit(solution)/shard_map/ppermute | solution.py:385
  13.4 0.5 %collective-permute-done.1.refs_1_ = bf16[8,1152]{1,0:T(8,128)(2,1)S(1)} collective-permute-done((bf16[8,1152]{1,0:T(8,128)(2,1)S(1)}, bf16[8,1152]{1,0:T(8,128)(2,1)S(1)}, u32[]{:S(2)}, u32[]{:S(2)}) %collective-permute-start.1) | collective-permute-done | bytes 18464 | tf_op jit(solution)/shard_map/ppermute | solution.py:385
  14.0 0.0 copy-done.1
  14.0 0.0 copy-done
  14.0 2.5 %shard_map.95 = (bf16[128,768]{1,0:T(8,128)(2,1)S(1)}, bf16[128,1024]{1,0:T(8,128)(2,1)S(1)}, bf16[32,128]{1,0:T(8,128)(2,1)S(1)}, f32[32,128]{1,0:T(8,128)S(1)}) custom-call(bf16[32,1152]{1,0:T(8,128)(2,1)S(1)} %shard_map.94.x_ref, bf16[8,1024,768]{2,1,0:T(8,128)(2,1)S(1)} %copy-done, bf16[8,1024,768]{2,1,0:T(8,128)(2,1)S(1)} %copy-done.1, ...), custom_call_target="tpu_custom_call" | custom-call | flops 65536 | bytes 65536 | tf_op jit(solution)/shard_map/pallas_call | solution.py:29
  16.4 0.0 collective-permute-start.4
  16.5 1.1 %shard_map.96.a_ref = f32[64,768]{1,0:T(8,128)S(1)} custom-call(bf16[128,1024]{1,0:T(8,128)(2,1)S(1)} %get-tuple-element.24.xs_ref, bf16[8,1024,768]{2,1,0:T(8,128)(2,1)S(1)} %copy-done, bf16[8,1024,768]{2,1,0:T(8,128)(2,1)S(1)} %copy-done.1, f32[6,8,8,128]{3,2,1,0:T(8,128)S(1)} %get-tuple-element.22.refs_2_.gs_ref, ...), custom_call_target="tpu_custom_call" | custom-call | flops 65536 | bytes 65536 | tf_op jit(solution)/shard_map/pallas_call | solution.py:29
  17.5 0.4 collective-permute-done.4.b_ref
  17.9 0.0 slice-start
  17.9 0.0 slice-start.1
  18.0 1.1 %shard_map.98.a_ref = f32[64,768]{1,0:T(8,128)S(1)} custom-call(bf16[128,1024]{1,0:T(8,128)(2,1)S(1)} %get-tuple-element.24.xs_ref, bf16[8,1024,768]{2,1,0:T(8,128)(2,1)S(1)} %copy-done, bf16[8,1024,768]{2,1,0:T(8,128)(2,1)S(1)} %copy-done.1, f32[6,8,8,128]{3,2,1,0:T(8,128)S(1)} %get-tuple-element.22.refs_2_.gs_ref, ...), custom_call_target="tpu_custom_call" | custom-call | flops 65536 | bytes 65536 | tf_op jit(solution)/shard_map/pallas_call | solution.py:29
  19.0 0.0 slice-start.2
  19.0 1.5 %collective-permute-start.6 = (bf16[64,768]{1,0:T(8,128)(2,1)S(1)}, bf16[64,768]{1,0:T(8,128)(2,1)S(1)}, u32[]{:S(2)}, u32[]{:S(2)}) collective-permute-start(bf16[64,768]{1,0:T(8,128)(2,1)S(1)} %get-tuple-element.26.rest_0_), channel_id=1, source_target_pairs={{0,2},{1,3},{2,0},{3,1},{4,6},{5,7},{6,4},{7,5},{8,10},{9,11},{10,... | collective-permute-start | bytes 294920 | tf_op jit(solution)/shard_map/ppermute | solution.py:374
  20.6 0.6 %collective-permute-start.5 = (bf16[64,768]{1,0:T(8,128)(2,1)S(1)}, bf16[64,768]{1,0:T(8,128)(2,1)S(1)}, u32[]{:S(2)}, u32[]{:S(2)}) collective-permute-start(bf16[64,768]{1,0:T(8,128)(2,1)S(1)} %get-tuple-element.28), channel_id=1, source_target_pairs={{0,2},{1,3},{2,0},{3,1},{4,6},{5,7},{6,4},{7,5},{8,10},{9,11},{10,... | collective-permute-start | bytes 294920 | tf_op jit(solution)/shard_map/ppermute | solution.py:374
  21.2 3.5 %collective-permute-done.6.b_ref = bf16[64,768]{1,0:T(8,128)(2,1)S(1)} collective-permute-done((bf16[64,768]{1,0:T(8,128)(2,1)S(1)}, bf16[64,768]{1,0:T(8,128)(2,1)S(1)}, u32[]{:S(2)}, u32[]{:S(2)}) %collective-permute-start.6) | collective-permute-done | bytes 98336 | tf_op jit(solution)/shard_map/ppermute | solution.py:374
  24.7 0.1 collective-permute-start.7
  24.8 0.0 slice-done
  24.8 0.0 slice-done.1
  24.8 0.0 slice-done.2
  24.8 0.8 %shard_map.101.rest_0_ = f32[32,1024]{1,0:T(8,128)S(1)} custom-call(bf16[64,384]{1,0:T(8,128)(2,1)S(1)} %shard_map.100.h_ref, bf16[32,128]{1,0:T(8,128)(2,1)S(1)} %get-tuple-element.30.sel_ref, f32[32,128]{1,0:T(8,128)S(1)} %get-tuple-element.31.wt_ref, bf16[8,768,1024]{2,1,0:T(8,128)(2,1)S(1)} %bitcast.4, f32[6,8,8,128]{3,2,1,0:T(8,128)S(1)} %get-tuple-element.32.ds_ref), custom_call_target="tpu_custom_call" | custom-call | flops 65536 | bytes 65536 | tf_op jit(solution)/shard_map/pallas_call | solution.py:29
  25.6 0.4 %collective-permute-done.7.h_ref = bf16[64,384]{1,0:T(8,128)(2,1)S(1)} collective-permute-done((bf16[64,384]{1,0:T(8,128)(2,1)S(1)}, bf16[64,384]{1,0:T(8,128)(2,1)S(1)}, u32[]{:S(2)}, u32[]{:S(2)}) %collective-permute-start.7) | collective-permute-done | bytes 49184 | tf_op jit(solution)/shard_map/ppermute | solution.py:374
  26.0 0.8 %shard_map.102.rest_0_ = f32[32,1024]{1,0:T(8,128)S(1)} custom-call(bf16[64,384]{1,0:T(8,128)(2,1)S(1)} %collective-permute-done.7.h_ref, bf16[32,128]{1,0:T(8,128)(2,1)S(1)} %get-tuple-element.30.sel_ref, f32[32,128]{1,0:T(8,128)S(1)} %get-tuple-element.31.wt_ref, bf16[8,768,1024]{2,1,0:T(8,128)(2,1)S(1)} %bitcast.4, ...), custom_call_target="tpu_custom_call" | custom-call | flops 65536 | bytes 65536 | tf_op jit(solution)/shard_map/pallas_call | solution.py:29
  26.8 0.0 collective-permute-done.5.b_ref
  26.8 0.2 collective-permute-start.8
  27.0 0.8 %shard_map.104.rest_0_ = f32[32,1024]{1,0:T(8,128)S(1)} custom-call(bf16[64,384]{1,0:T(8,128)(2,1)S(1)} %shard_map.103.h_ref, bf16[32,128]{1,0:T(8,128)(2,1)S(1)} %get-tuple-element.30.sel_ref, f32[32,128]{1,0:T(8,128)S(1)} %get-tuple-element.31.wt_ref, bf16[8,768,1024]{2,1,0:T(8,128)(2,1)S(1)} %bitcast.4, f32[6,8,8,128]{3,2,1,0:T(8,128)S(1)} %get-tuple-element.32.ds_ref, ...), custom_call_target="tpu_custom_call" | custom-call | flops 65536 | bytes 65536 | tf_op jit(solution)/shard_map/pallas_call | solution.py:29
  27.8 0.3 collective-permute-done.8.h_ref
  28.1 0.8 %shard_map.105 = (f32[8,1024]{1,0:T(8,128)S(1)}, bf16[8,1024]{1,0:T(8,128)(2,1)S(1)}, bf16[8,1024]{1,0:T(8,128)(2,1)S(1)}, bf16[8,1024]{1,0:T(8,128)(2,1)S(1)}) custom-call(bf16[64,384]{1,0:T(8,128)(2,1)S(1)} %collective-permute-done.8.h_ref, bf16[32,128]{1,0:T(8,128)(2,1)S(1)} %get-tuple-element.30.sel_ref, f32[32,128]{1,0:T(8,128)S(1)} %get-tuple-element.31.wt_ref, ...), custom_call_target="tpu_custom_call" | custom-call | flops 65536 | bytes 65536 | tf_op jit(solution)/shard_map/pallas_call | solution.py:29
  28.9 1.5 %collective-permute-start.9 = (bf16[8,1024]{1,0:T(8,128)(2,1)S(1)}, bf16[8,1024]{1,0:T(8,128)(2,1)S(1)}, u32[]{:S(2)}, u32[]{:S(2)}) collective-permute-start(bf16[8,1024]{1,0:T(8,128)(2,1)S(1)} %get-tuple-element.34), channel_id=1, source_target_pairs={{0,20},{4,16},{8,28},{12,24},{16,4},{20,0},{24,12},{28,8},{1,21},{... | collective-permute-start | bytes 49160 | tf_op jit(solution)/shard_map/ppermute | solution.py:385
  30.4 0.4 collective-permute-start.10
  30.8 1.7 %collective-permute-start.11 = (bf16[8,1024]{1,0:T(8,128)(2,1)S(1)}, bf16[8,1024]{1,0:T(8,128)(2,1)S(1)}, u32[]{:S(2)}, u32[]{:S(2)}) collective-permute-start(bf16[8,1024]{1,0:T(8,128)(2,1)S(1)} %get-tuple-element.36), channel_id=1, source_target_pairs={{0,4},{4,0},{8,12},{12,8},{16,20},{20,16},{24,28},{28,24},{1,5},{5... | collective-permute-start | bytes 49160 | tf_op jit(solution)/shard_map/ppermute | solution.py:385
  32.5 1.1 %collective-permute-done.9.rest_0_ = bf16[8,1024]{1,0:T(8,128)(2,1)S(1)} collective-permute-done((bf16[8,1024]{1,0:T(8,128)(2,1)S(1)}, bf16[8,1024]{1,0:T(8,128)(2,1)S(1)}, u32[]{:S(2)}, u32[]{:S(2)}) %collective-permute-start.9) | collective-permute-done | bytes 16416 | tf_op jit(solution)/shard_map/ppermute | solution.py:385
  33.6 0.5 %collective-permute-done.10.rest_1_ = bf16[8,1024]{1,0:T(8,128)(2,1)S(1)} collective-permute-done((bf16[8,1024]{1,0:T(8,128)(2,1)S(1)}, bf16[8,1024]{1,0:T(8,128)(2,1)S(1)}, u32[]{:S(2)}, u32[]{:S(2)}) %collective-permute-start.10) | collective-permute-done | bytes 16416 | tf_op jit(solution)/shard_map/ppermute | solution.py:385
  34.1 0.4 collective-permute-done.11.rest_2_
  34.5 2.8 %collective-permute-start.12 = (bf16[4,1024]{1,0:T(4,128)(2,1)S(1)}, bf16[4,1024]{1,0:T(4,128)(2,1)S(1)}, u32[]{:S(2)}, u32[]{:S(2)}) collective-permute-start(bf16[4,1024]{1,0:T(4,128)(2,1)S(1)} %get-tuple-element.38), channel_id=1, source_target_pairs={{0,8},{4,12},{8,0},{12,4},{16,24},{20,28},{24,16},{28,20},{1,9},{5... | collective-permute-start | bytes 24584 | tf_op jit(solution)/shard_map/ppermute | solution.py:385
  37.3 1.8 %collective-permute-done.12.rest_0_ = bf16[4,1024]{1,0:T(4,128)(2,1)S(1)} collective-permute-done((bf16[4,1024]{1,0:T(4,128)(2,1)S(1)}, bf16[4,1024]{1,0:T(4,128)(2,1)S(1)}, u32[]{:S(2)}, u32[]{:S(2)}) %collective-permute-start.12) | collective-permute-done | bytes 8224 | tf_op jit(solution)/shard_map/ppermute | solution.py:385
  39.1 0.6 %shard_map.107 = bf16[4,1024]{1,0:T(4,128)(2,1)} custom-call(f32[4,1024]{1,0:T(4,128)S(1)} %get-tuple-element.37.a_ref, bf16[4,1024]{1,0:T(4,128)(2,1)S(1)} %collective-permute-done.12.rest_0_), custom_call_target="tpu_custom_call" | custom-call | tf_op jit(solution)/shard_map/pallas_call | solution.py:29
  (8 shorter events, 0.2 us)
Async XLA Ops:
  0.0 14.0 %copy-start.1 = (bf16[8,1024,768]{2,1,0:T(8,128)(2,1)S(1)}, bf16[8,1024,768]{2,1,0:T(8,128)(2,1)}, u32[]{:S(2)}) copy-start(bf16[8,1024,768]{2,1,0:T(8,128)(2,1)} %uw_ref.5) | copy-start | bytes 37748740
  0.0 14.0 %copy-start = (bf16[8,1024,768]{2,1,0:T(8,128)(2,1)S(1)}, bf16[8,1024,768]{2,1,0:T(8,128)(2,1)}, u32[]{:S(2)}) copy-start(bf16[8,1024,768]{2,1,0:T(8,128)(2,1)} %gw_ref.5) | copy-start | bytes 37748740
  1.0 5.9 %collective-permute-start = (bf16[4,1152]{1,0:T(4,128)(2,1)S(1)}, bf16[4,1152]{1,0:T(4,128)(2,1)S(1)}, u32[]{:S(2)}, u32[]{:S(2)}) collective-permute-start(bf16[4,1152]{1,0:T(4,128)(2,1)S(1)} %shard_map.91.refs_3_.refs_0_), channel_id=1, source_target_pairs={{0,8},{4,12},{8,0},{12,4},{16,24},{20,28},{24,16},{28,20},{1,9},{5... | collective-permute-start | bytes 27656 | tf_op jit(solution)/shard_map/ppermute | solution.py:385
  7.0 4.8 %collective-permute-start.3 = (bf16[8,1152]{1,0:T(8,128)(2,1)S(1)}, bf16[8,1152]{1,0:T(8,128)(2,1)S(1)}, u32[]{:S(2)}, u32[]{:S(2)}) collective-permute-start(bf16[8,1152]{1,0:T(8,128)(2,1)S(1)} %shard_map.93.refs_0_), channel_id=1, source_target_pairs={{0,20},{4,16},{8,28},{12,24},{16,4},{20,0},{24,12},{28,8},{1,21},{... | collective-permute-start | bytes 55304 | tf_op jit(solution)/shard_map/ppermute | solution.py:385
  9.7 3.8 %collective-permute-start.2 = (bf16[8,1152]{1,0:T(8,128)(2,1)S(1)}, bf16[8,1152]{1,0:T(8,128)(2,1)S(1)}, u32[]{:S(2)}, u32[]{:S(2)}) collective-permute-start(bf16[8,1152]{1,0:T(8,128)(2,1)S(1)} %shard_map.93.refs_0_), channel_id=1, source_target_pairs={{0,16},{4,20},{8,24},{12,28},{16,0},{20,4},{24,8},{28,12},{1,17},{... | collective-permute-start | bytes 55304 | tf_op jit(solution)/shard_map/ppermute | solution.py:385
  10.2 3.8 %collective-permute-start.1 = (bf16[8,1152]{1,0:T(8,128)(2,1)S(1)}, bf16[8,1152]{1,0:T(8,128)(2,1)S(1)}, u32[]{:S(2)}, u32[]{:S(2)}) collective-permute-start(bf16[8,1152]{1,0:T(8,128)(2,1)S(1)} %shard_map.93.refs_0_), channel_id=1, source_target_pairs={{0,4},{4,0},{8,12},{12,8},{16,20},{20,16},{24,28},{28,24},{1,5},{5... | collective-permute-start | bytes 55304 | tf_op jit(solution)/shard_map/ppermute | solution.py:385
  16.4 1.4 %collective-permute-start.4 = (bf16[128,768]{1,0:T(8,128)(2,1)S(1)}, bf16[128,768]{1,0:T(8,128)(2,1)S(1)}, u32[]{:S(2)}, u32[]{:S(2)}) collective-permute-start(bf16[128,768]{1,0:T(8,128)(2,1)S(1)} %get-tuple-element.25), channel_id=1, source_target_pairs={{0,1},{1,0},{2,3},{3,2},{4,5},{5,4},{6,7},{7,6},{8,9},{9,8},{10,11... | collective-permute-start | bytes 589832 | tf_op jit(solution)/shard_map/ppermute | solution.py:374
  17.9 6.8 %slice-start = ((s8[12582912]{0:T(1024)(128)(4,1)}), s8[4194304]{0:T(1024)(128)(4,1)S(1)}, s32[]{:S(2)}) async-start(s8[12582912]{0:T(1024)(128)(4,1)} %bitcast.3), calls=%async_computation | async-start | bytes 8388608
  17.9 6.8 %slice-start.1 = ((s8[12582912]{0:T(1024)(128)(4,1)}), s8[4194304]{0:T(1024)(128)(4,1)S(1)}, s32[]{:S(2)}) async-start(s8[12582912]{0:T(1024)(128)(4,1)} %bitcast.3), calls=%async_computation.1 | async-start | bytes 8388608
  19.0 5.8 %slice-start.2 = ((s8[12582912]{0:T(1024)(128)(4,1)}), s8[4194304]{0:T(1024)(128)(4,1)S(1)}, s32[]{:S(2)}) async-start(s8[12582912]{0:T(1024)(128)(4,1)} %bitcast.3), calls=%async_computation.2 | async-start | bytes 8388608
  19.0 5.6 %collective-permute-start.6 = (bf16[64,768]{1,0:T(8,128)(2,1)S(1)}, bf16[64,768]{1,0:T(8,128)(2,1)S(1)}, u32[]{:S(2)}, u32[]{:S(2)}) collective-permute-start(bf16[64,768]{1,0:T(8,128)(2,1)S(1)} %get-tuple-element.26.rest_0_), channel_id=1, source_target_pairs={{0,2},{1,3},{2,0},{3,1},{4,6},{5,7},{6,4},{7,5},{8,10},{9,11},{10,... | collective-permute-start | bytes 294920 | tf_op jit(solution)/shard_map/ppermute | solution.py:374
  20.6 6.2 %collective-permute-start.5 = (bf16[64,768]{1,0:T(8,128)(2,1)S(1)}, bf16[64,768]{1,0:T(8,128)(2,1)S(1)}, u32[]{:S(2)}, u32[]{:S(2)}) collective-permute-start(bf16[64,768]{1,0:T(8,128)(2,1)S(1)} %get-tuple-element.28), channel_id=1, source_target_pairs={{0,2},{1,3},{2,0},{3,1},{4,6},{5,7},{6,4},{7,5},{8,10},{9,11},{10,... | collective-permute-start | bytes 294920 | tf_op jit(solution)/shard_map/ppermute | solution.py:374
  24.7 1.3 %collective-permute-start.7 = (bf16[64,384]{1,0:T(8,128)(2,1)S(1)}, bf16[64,384]{1,0:T(8,128)(2,1)S(1)}, u32[]{:S(2)}, u32[]{:S(2)}) collective-permute-start(bf16[64,384]{1,0:T(8,128)(2,1)S(1)} %shard_map.100.h_ref), channel_id=1, source_target_pairs={{0,1},{1,0},{2,3},{3,2},{4,5},{5,4},{6,7},{7,6},{8,9},{9,8},{10,11... | collective-permute-start | bytes 147464 | tf_op jit(solution)/shard_map/ppermute | solution.py:374
  26.8 1.3 %collective-permute-start.8 = (bf16[64,384]{1,0:T(8,128)(2,1)S(1)}, bf16[64,384]{1,0:T(8,128)(2,1)S(1)}, u32[]{:S(2)}, u32[]{:S(2)}) collective-permute-start(bf16[64,384]{1,0:T(8,128)(2,1)S(1)} %shard_map.103.h_ref), channel_id=1, source_target_pairs={{0,1},{1,0},{2,3},{3,2},{4,5},{5,4},{6,7},{7,6},{8,9},{9,8},{10,11... | collective-permute-start | bytes 147464 | tf_op jit(solution)/shard_map/ppermute | solution.py:374
  28.9 4.7 %collective-permute-start.9 = (bf16[8,1024]{1,0:T(8,128)(2,1)S(1)}, bf16[8,1024]{1,0:T(8,128)(2,1)S(1)}, u32[]{:S(2)}, u32[]{:S(2)}) collective-permute-start(bf16[8,1024]{1,0:T(8,128)(2,1)S(1)} %get-tuple-element.34), channel_id=1, source_target_pairs={{0,20},{4,16},{8,28},{12,24},{16,4},{20,0},{24,12},{28,8},{1,21},{... | collective-permute-start | bytes 49160 | tf_op jit(solution)/shard_map/ppermute | solution.py:385
  30.4 3.7 %collective-permute-start.10 = (bf16[8,1024]{1,0:T(8,128)(2,1)S(1)}, bf16[8,1024]{1,0:T(8,128)(2,1)S(1)}, u32[]{:S(2)}, u32[]{:S(2)}) collective-permute-start(bf16[8,1024]{1,0:T(8,128)(2,1)S(1)} %get-tuple-element.35), channel_id=1, source_target_pairs={{0,16},{4,20},{8,24},{12,28},{16,0},{20,4},{24,8},{28,12},{1,17},{... | collective-permute-start | bytes 49160 | tf_op jit(solution)/shard_map/ppermute | solution.py:385
  30.8 3.7 %collective-permute-start.11 = (bf16[8,1024]{1,0:T(8,128)(2,1)S(1)}, bf16[8,1024]{1,0:T(8,128)(2,1)S(1)}, u32[]{:S(2)}, u32[]{:S(2)}) collective-permute-start(bf16[8,1024]{1,0:T(8,128)(2,1)S(1)} %get-tuple-element.36), channel_id=1, source_target_pairs={{0,4},{4,0},{8,12},{12,8},{16,20},{20,16},{24,28},{28,24},{1,5},{5... | collective-permute-start | bytes 49160 | tf_op jit(solution)/shard_map/ppermute | solution.py:385
  34.5 4.6 %collective-permute-start.12 = (bf16[4,1024]{1,0:T(4,128)(2,1)S(1)}, bf16[4,1024]{1,0:T(4,128)(2,1)S(1)}, u32[]{:S(2)}, u32[]{:S(2)}) collective-permute-start(bf16[4,1024]{1,0:T(4,128)(2,1)S(1)} %get-tuple-element.38), channel_id=1, source_target_pairs={{0,8},{4,12},{8,0},{12,4},{16,24},{20,28},{24,16},{28,20},{1,9},{5... | collective-permute-start | bytes 24584 | tf_op jit(solution)/shard_map/ppermute | solution.py:385

commit v7 on v6

--- a/solution.py
+++ b/solution.py
@@ -130,6 +130,38 @@
         scratch_shapes=[pltpu.VMEM(s.shape, s.dtype) for s in scales]
         + [pltpu.SemaphoreType.DMA((len(scales),))],
     )
+
+
+def half_rows(w, other, after):
+    experts, hidden, width = w.shape
+    n = hidden // 2
+
+    def kernel(w_ref, _, o_ref, t_ref, sems):
+        half = lax.rem(lax.axis_index("pool"), 2)
+        half = 1 - half if other else half
+        cut = pl.ds(pl.multiple_of(half * n, QB), n)
+        copies = [
+            pltpu.make_async_copy(w_ref.at[e, cut, :], o_ref.at[e], sems.at[e])
+            for e in range(experts)
+        ]
+        for copy in copies:
+            copy.start()
+        t_ref[...] = jnp.zeros_like(t_ref)
+        for copy in copies:
+            copy.wait()
+
+    return pl.pallas_call(
+        kernel,
+        out_shape=[pltpu.VMEM((experts, n, width), BF), sds((8, LANES), F32)],
+        in_specs=[HB, VM],
+        out_specs=[VM, VM],
+        scratch_shapes=[pltpu.SemaphoreType.DMA((experts,))],
+        compiler_params=pltpu.CompilerParams(vmem_limit_bytes=1 << 20),
+        cost_estimate=pl.CostEstimate(
+            flops=NEAR, bytes_accessed=NEAR, transcendentals=0
+        ),
+        name="half_rows",
+    )(in_hbm(w), after)
 
 
 def dispatch(x, width, top, rows_dev, experts, slots):
@@ -250,7 +282,7 @@
     )
 
 
-def add_round(own, got, first, hint):
+def add_round(own, got, first):
     rows = own.shape[0]
 
     def kernel(a_ref, b_ref, o_ref, r_ref):
@@ -258,20 +290,29 @@
         o_ref[...] = total
         r_ref[...] = total.astype(BF)
 
-    return run(kernel, [sds(own.shape, F32), sds(own.shape, BF)], [VM] * 2, (own, got), flops=hint)
-
-
-def activate(own, got, after):
-    slots, hidden = own.shape
+    return run(kernel, [sds(own.shape, F32), sds(own.shape, BF)], [VM] * 2, (own, got))
+
+
+def activate(pairs, after):
+    hidden = pairs[0][0].shape[1]
+    rows = [own.shape[0] for own, _ in pairs]
     n = hidden // 2
 
-    def kernel(a_ref, b_ref, *rest):
-        o_ref = rest[-1]
-        gate = a_ref[:, :n] + b_ref[:, :n].astype(F32)
-        up = a_ref[:, n:] + b_ref[:, n:].astype(F32)
-        o_ref[...] = (jax.nn.silu(gate) * up).astype(BF)
-
-    return run(kernel, sds((slots, n), BF), [VM] * (2 + len(after)), (own, got, *after))
+    def kernel(*refs):
+        first = 0
+        for i, count in enumerate(rows):
+            a_ref, b_ref = refs[2 * i : 2 * i + 2]
+            gate = a_ref[:, :n] + b_ref[:, :n].astype(F32)
+            up = a_ref[:, n:] + b_ref[:, n:].astype(F32)
+            refs[-1][first : first + count] = (jax.nn.silu(gate) * up).astype(BF)
+            first += count
+
+    return run(
+        kernel,
+        sds((sum(rows), n), BF),
+        [VM] * (2 * len(pairs) + 1),
+        [a for pair in pairs for a in pair] + [after],
+    )
 
 
 def spread_rows(h_ref, sel_ref, wt_ref, per, chosen):
@@ -292,8 +333,8 @@
 
 
 def down_kernel(hid, sel, wt, dw, ds, acc_in, chosen, other, parts_out):
-    experts, hidden, width = dw.shape
-    n = hidden // 2 // QB
+    experts, half_hidden, width = dw.shape
+    n = half_hidden // QB
     rows, slots = sel.shape
     per = slots // experts
     keep = rows // parts_out
@@ -308,10 +349,9 @@
         half = lax.rem(lax.axis_index("pool"), 2)
         half = 1 - half if other else half
         parts = spread_rows(h_ref, sel_ref, wt_ref, per, chosen)
-        starts = [pl.multiple_of((half * n + j) * QB, QB) for j in range(n)]
 
         def block(e, j, q):
-            part = dw_ref[e, pl.ds(starts[j], QB), q * QB : (q + 1) * QB]
+            part = dw_ref[e, j * QB : (j + 1) * QB, q * QB : (q + 1) * QB]
             return scaled(part, ds_ref, half * n + j, q, e)
 
         for c in range(0, width // QB, group):
@@ -404,34 +444,34 @@
             gs, us, ds = spread_scales(scales, x)
         x = cat([x, got], [gs] if scales else [], HINT * dw.size * LATE if scales else 0)
         scales = []
-    far, near_a, near_b = hop(x, a, b), hop(x, a), hop(x, b)
-    x = cat([x, near_a, near_b, far], [])
+    far, near_b = hop(x, a, b), hop(x, b)
+    near_a = hop(x, a)
+    dw_own, token = half_rows(dw, False, x)
+    x = cat([x, near_a, near_b, far], [token])
 
     send, xs, sel, wt = other_half(x, gw, uw, gs, us, top, rows_dev, n_seq * n_head)
     got = swap(send, "pool", 1)
     experts = gw.shape[0]
     per = xs.shape[0] // experts
-    cut = experts // 2
+    cut = experts * 5 // 8
     parts = [range(cut), range(cut, experts)] if cut else [range(experts)]
     steps = bits(n_pool)[1:]
     sums, after = [], []
-    for i, part in enumerate(parts):
+    for part in parts:
         own = own_half(xs, gw, uw, gs, us, part, after)
-        first, hint = part[0] * per, HINT * dw.size
+        first = part[0] * per
         arrived = got
         for bit in steps:
-            own, send = add_round(own, arrived, first, hint if i + 1 == len(parts) else 0)
+            own, send = add_round(own, arrived, first)
             arrived, first = swap(send, "pool", bit), 0
             after = [send]
         sums.append((own, arrived))
-    acc = None
-    for i, (part, pair) in enumerate(zip(parts, sums)):
-        hid = activate(*pair, [] if acc is None else [acc])
-        other = swap(hid, "pool", 1)
-        (acc,) = down_kernel(hid, sel, wt, dw, ds, acc, part, False, 1)
-        ends = i + 1 == len(parts)
-        acc, *sends = down_kernel(other, sel, wt, dw, ds, acc, part, True, 4 if ends else 1)
-    to_a, to_b, to_far = sends
+    everyone = range(experts)
+    dw_other, token = half_rows(dw, True, sums[-1][0])
+    hid = activate(sums, token)
+    other = swap(hid, "pool", 1)
+    (acc,) = down_kernel(hid, sel, wt, dw_own, ds, None, everyone, False, 1)
+    acc, to_a, to_b, to_far = down_kernel(other, sel, wt, dw_other, ds, acc, everyone, True, 4)
     far, near_a, near_b = hop(to_far, a, b), hop(to_a, a), hop(to_b, b)
     got = [far, near_b, near_a]
     for step in reversed(single):

time: 40.1 us -> 39.8 us (level)
  Pallas kernels: 11.4 us -> 16.4 us
  waiting for transfers between devices: 11.7 us -> 6.87 us
    pallas_call x0 -> x2, Pallas kernels: none -> 5.71 us  [half_rows(): pl.pallas_call(kernel, out_shape=[pltpu.VMEM((experts, n, width), BF), sd...]
    ppermute x5 -> x4, waiting for transfers between devices: 4.52 us -> 1.52 us  [swap(): lax.ppermute(x, axis, [(j, j ^ bit) for j in range(lax.axis_size(axis))])]
    ppermute x8, waiting for transfers between devices: 7.21 us -> 5.35 us  [hop(): return lax.ppermute(x, ('seq', 'head'), pairs)]
    pallas_call x17 -> x14, Pallas kernels: 11.4 us -> 10.7 us  [run(): pl.pallas_call(kernel, out_shape=out_shape, in_specs=in_specs, out_specs=...]
    ppermute x5 -> x4, starting transfers between devices: 2.39 us -> 2.23 us  [swap(): lax.ppermute(x, axis, [(j, j ^ bit) for j in range(lax.axis_size(axis))])]
  transfers between devices with their start and end apart: 13 -> 12, of which waited for: 11 -> 7; matrix products, arithmetic and copies ran while one was open for 0% -> 0% of each run, Pallas kernels for 13% -> 28%
where the time goes in v7:
time: 39.8 us; the launch traced here: 39.6 us
  Pallas kernels  16.4 us (41%)
  starting transfers between devices  16.1 us (40%)
  waiting for transfers between devices  6.87 us (17%)
    ppermute x8, starting transfers between devices, hop(): return lax.ppermute(x, ('seq', 'head'), pairs)  13.9 us
    pallas_call x14, Pallas kernels, run(): pl.pallas_call(kernel, out_shape=out_shape, in_specs=in_specs, out_specs=...  10.7 us
    pallas_call x2, Pallas kernels, half_rows(): pl.pallas_call(kernel, out_shape=[pltpu.VMEM((experts, n, width), BF), sd...  5.71 us
    ppermute x8, waiting for transfers between devices, hop(): return lax.ppermute(x, ('seq', 'head'), pairs)  5.35 us
    ppermute x4, starting transfers between devices, swap(): lax.ppermute(x, axis, [(j, j ^ bit) for j in range(lax.axis_size(axis))])  2.23 us
    ppermute x4, waiting for transfers between devices, swap(): lax.ppermute(x, axis, [(j, j ^ bit) for j in range(lax.axis_size(axis))])  1.52 us
  transfers between devices with their start and end apart: 12, of which 7 were waited for; matrix products, arithmetic and copies ran while one was open for 0% of the time, Pallas kernels for 28%

profile of v7, /device:TPU:0, one launch (start us, length us, event | category | flops | bytes accessed | tf_op | source)
XLA Modules:
  0.0 39.6 jit_solution(11621022798958140807)
XLA Ops:
  0.0 0.0 copy-start.1
  0.0 1.0 %shard_map.91.refs_3_.refs_0_ = bf16[4,1152]{1,0:T(4,128)(2,1)S(1)} custom-call(bf16[4,1024]{1,0:T(4,128)(2,1)} %t_in.1, s32[4,8]{1,0:T(4,128)} %r_in.1, s32[4,8]{1,0:T(4,128)} %g_in.1), custom_call_target="tpu_custom_call" | custom-call | flops 12582912000 | tf_op jit(solution)/shard_map/pallas_call | solution.py:29
  1.0 0.0 copy-start
  1.1 4.1 %collective-permute-start = (bf16[4,1152]{1,0:T(4,128)(2,1)S(1)}, bf16[4,1152]{1,0:T(4,128)(2,1)S(1)}, u32[]{:S(2)}, u32[]{:S(2)}) collective-permute-start(bf16[4,1152]{1,0:T(4,128)(2,1)S(1)} %shard_map.91.refs_3_.refs_0_), channel_id=1, source_target_pairs={{0,8},{4,12},{8,0},{12,4},{16,24},{20,28},{24,16},{28,20},{1,9},{5... | collective-permute-start | bytes 27656 | tf_op jit(solution)/shard_map/ppermute | solution.py:425
  5.2 1.8 %shard_map.92 = (f32[6,8,8,128]{3,2,1,0:T(8,128)S(1)}, f32[6,8,8,128]{3,2,1,0:T(8,128)S(1)}, f32[6,8,8,128]{3,2,1,0:T(8,128)S(1)}) custom-call(bf16[6,8,8]{2,1,0:T(8,128)(2,1)} %bitcast.3, bf16[6,8,8]{2,1,0:T(8,128)(2,1)} %bitcast.4, bf16[6,8,8]{2,1,0:T(8,128)(2,1)} %bitcast.5, bf16[4,1152]{1,0:T(4,128)(2,1)S(1)} %shard_map.91.refs_3_.refs_0_), custom_call_target="tpu_custom_call" | custom-call | bytes 1048576 | tf_op jit(solution)/shard_map/pallas_call | solution.py:29
  7.0 0.0 collective-permute-done.refs_1_
  7.0 2.6 %collective-permute-start.3 = (bf16[8,1152]{1,0:T(8,128)(2,1)S(1)}, bf16[8,1152]{1,0:T(8,128)(2,1)S(1)}, u32[]{:S(2)}, u32[]{:S(2)}) collective-permute-start(bf16[8,1152]{1,0:T(8,128)(2,1)S(1)} %shard_map.93._.refs_0_), channel_id=1, source_target_pairs={{0,20},{4,16},{8,28},{12,24},{16,4},{20,0},{24,12},{28,8},{1,21},{... | collective-permute-start | bytes 55304 | tf_op jit(solution)/shard_map/ppermute | solution.py:425
  9.7 0.5 %collective-permute-start.2 = (bf16[8,1152]{1,0:T(8,128)(2,1)S(1)}, bf16[8,1152]{1,0:T(8,128)(2,1)S(1)}, u32[]{:S(2)}, u32[]{:S(2)}) collective-permute-start(bf16[8,1152]{1,0:T(8,128)(2,1)S(1)} %shard_map.93._.refs_0_), channel_id=1, source_target_pairs={{0,16},{4,20},{8,24},{12,28},{16,0},{20,4},{24,8},{28,12},{1,17},{... | collective-permute-start | bytes 55304 | tf_op jit(solution)/shard_map/ppermute | solution.py:425
  10.2 0.4 collective-permute-start.1
  10.6 2.9 %half_rows.2 = (bf16[8,384,1024]{2,1,0:T(8,128)(2,1)S(1)}, f32[8,128]{1,0:T(8,128)S(1)}) custom-call(bf16[8,768,1024]{2,1,0:T(8,128)(2,1)} %w_ref.3, bf16[8,1152]{1,0:T(8,128)(2,1)S(1)} %shard_map.93._.refs_0_), custom_call_target="tpu_custom_call" | custom-call | flops 65536 | bytes 65536 | tf_op jit(solution)/shard_map/half_rows/pallas_call | solution.py:153
  13.4 0.0 collective-permute-done.3.refs_3_
  13.5 0.0 collective-permute-done.2.refs_2_
  13.5 0.5 %collective-permute-done.1.refs_1_ = bf16[8,1152]{1,0:T(8,128)(2,1)S(1)} collective-permute-done((bf16[8,1152]{1,0:T(8,128)(2,1)S(1)}, bf16[8,1152]{1,0:T(8,128)(2,1)S(1)}, u32[]{:S(2)}, u32[]{:S(2)}) %collective-permute-start.1) | collective-permute-done | bytes 18464 | tf_op jit(solution)/shard_map/ppermute | solution.py:425
  14.0 0.0 copy-done.1
  14.0 0.0 copy-done
  14.0 2.4 %shard_map.95 = (bf16[128,768]{1,0:T(8,128)(2,1)S(1)}, bf16[128,1024]{1,0:T(8,128)(2,1)S(1)}, bf16[32,128]{1,0:T(8,128)(2,1)S(1)}, f32[32,128]{1,0:T(8,128)S(1)}) custom-call(bf16[32,1152]{1,0:T(8,128)(2,1)S(1)} %shard_map.94.x_ref, bf16[8,1024,768]{2,1,0:T(8,128)(2,1)S(1)} %copy-done, bf16[8,1024,768]{2,1,0:T(8,128)(2,1)S(1)} %copy-done.1, ...), custom_call_target="tpu_custom_call" | custom-call | flops 65536 | bytes 65536 | tf_op jit(solution)/shard_map/pallas_call | solution.py:29
  16.4 0.0 collective-permute-start.4
  16.4 1.3 %shard_map.96.a_ref = f32[80,768]{1,0:T(8,128)S(1)} custom-call(bf16[128,1024]{1,0:T(8,128)(2,1)S(1)} %get-tuple-element.29.xs_ref, bf16[8,1024,768]{2,1,0:T(8,128)(2,1)S(1)} %copy-done, bf16[8,1024,768]{2,1,0:T(8,128)(2,1)S(1)} %copy-done.1, f32[6,8,8,128]{3,2,1,0:T(8,128)S(1)} %get-tuple-element.26.refs_2_.gs_ref, ...), custom_call_target="tpu_custom_call" | custom-call | flops 65536 | bytes 65536 | tf_op jit(solution)/shard_map/pallas_call | solution.py:29
  17.7 0.2 collective-permute-done.4.b_ref
  17.9 1.6 %collective-permute-start.5 = (bf16[80,768]{1,0:T(8,128)(2,1)S(1)}, bf16[80,768]{1,0:T(8,128)(2,1)S(1)}, u32[]{:S(2)}, u32[]{:S(2)}) collective-permute-start(bf16[80,768]{1,0:T(8,128)(2,1)S(1)} %get-tuple-element.32.rest_0_), channel_id=1, source_target_pairs={{0,2},{1,3},{2,0},{3,1},{4,6},{5,7},{6,4},{7,5},{8,10},{9,11},{10,... | collective-permute-start | bytes 368648 | tf_op jit(solution)/shard_map/ppermute | solution.py:414
  19.5 0.8 %shard_map.98.a_ref = f32[48,768]{1,0:T(8,128)S(1)} custom-call(bf16[128,1024]{1,0:T(8,128)(2,1)S(1)} %get-tuple-element.29.xs_ref, bf16[8,1024,768]{2,1,0:T(8,128)(2,1)S(1)} %copy-done, bf16[8,1024,768]{2,1,0:T(8,128)(2,1)S(1)} %copy-done.1, f32[6,8,8,128]{3,2,1,0:T(8,128)S(1)} %get-tuple-element.26.refs_2_.gs_ref, ...), custom_call_target="tpu_custom_call" | custom-call | flops 65536 | bytes 65536 | tf_op jit(solution)/shard_map/pallas_call | solution.py:29
  20.3 0.6 %collective-permute-start.6 = (bf16[48,768]{1,0:T(8,128)(2,1)S(1)}, bf16[48,768]{1,0:T(8,128)(2,1)S(1)}, u32[]{:S(2)}, u32[]{:S(2)}) collective-permute-start(bf16[48,768]{1,0:T(8,128)(2,1)S(1)} %get-tuple-element.34), channel_id=1, source_target_pairs={{0,2},{1,3},{2,0},{3,1},{4,6},{5,7},{6,4},{7,5},{8,10},{9,11},{10,... | collective-permute-start | bytes 221192 | tf_op jit(solution)/shard_map/ppermute | solution.py:414
  20.9 2.9 %half_rows.3 = (bf16[8,384,1024]{2,1,0:T(8,128)(2,1)S(1)}, f32[8,128]{1,0:T(8,128)S(1)}) custom-call(bf16[8,768,1024]{2,1,0:T(8,128)(2,1)} %w_ref.3, f32[48,768]{1,0:T(8,128)S(1)} %get-tuple-element.33._.refs_2_), custom_call_target="tpu_custom_call" | custom-call | flops 65536 | bytes 65536 | tf_op jit(solution)/shard_map/half_rows/pallas_call | solution.py:153
  23.7 1.3 %collective-permute-done.6.refs_3_ = bf16[48,768]{1,0:T(8,128)(2,1)S(1)} collective-permute-done((bf16[48,768]{1,0:T(8,128)(2,1)S(1)}, bf16[48,768]{1,0:T(8,128)(2,1)S(1)}, u32[]{:S(2)}, u32[]{:S(2)}) %collective-permute-start.6) | collective-permute-done | bytes 73760 | tf_op jit(solution)/shard_map/ppermute | solution.py:414
  25.1 0.0 collective-permute-done.5.refs_1_
  25.1 0.1 shard_map.100.h_ref
  25.1 0.1 collective-permute-start.7
  25.2 1.3 %shard_map.101.rest_0_ = f32[32,1024]{1,0:T(8,128)S(1)} custom-call(bf16[128,384]{1,0:T(8,128)(2,1)S(1)} %shard_map.100.h_ref, bf16[32,128]{1,0:T(8,128)(2,1)S(1)} %get-tuple-element.36.sel_ref, f32[32,128]{1,0:T(8,128)S(1)} %get-tuple-element.37.wt_ref, bf16[8,384,1024]{2,1,0:T(8,128)(2,1)S(1)} %get-tuple-element.40.dw_ref, ...), custom_call_target="tpu_custom_call" | custom-call | flops 65536 | bytes 65536 | tf_op jit(solution)/shard_map/pallas_call | solution.py:29
  26.6 0.0 collective-permute-done.7.h_ref
  26.6 1.3 %shard_map.102 = (f32[8,1024]{1,0:T(8,128)S(1)}, bf16[8,1024]{1,0:T(8,128)(2,1)S(1)}, bf16[8,1024]{1,0:T(8,128)(2,1)S(1)}, bf16[8,1024]{1,0:T(8,128)(2,1)S(1)}) custom-call(bf16[128,384]{1,0:T(8,128)(2,1)S(1)} %collective-permute-done.7.h_ref, bf16[32,128]{1,0:T(8,128)(2,1)S(1)} %get-tuple-element.36.sel_ref, f32[32,128]{1,0:T(8,128)S(1)} %get-tuple-element.37.wt_ref, ...), custom_call_target="tpu_custom_call" | custom-call | flops 65536 | bytes 65536 | tf_op jit(solution)/shard_map/pallas_call | solution.py:29
  27.9 2.2 %collective-permute-start.8 = (bf16[8,1024]{1,0:T(8,128)(2,1)S(1)}, bf16[8,1024]{1,0:T(8,128)(2,1)S(1)}, u32[]{:S(2)}, u32[]{:S(2)}) collective-permute-start(bf16[8,1024]{1,0:T(8,128)(2,1)S(1)} %get-tuple-element.42), channel_id=1, source_target_pairs={{0,20},{4,16},{8,28},{12,24},{16,4},{20,0},{24,12},{28,8},{1,21},{... | collective-permute-start | bytes 49160 | tf_op jit(solution)/shard_map/ppermute | solution.py:425
  30.1 0.5 %collective-permute-start.9 = (bf16[8,1024]{1,0:T(8,128)(2,1)S(1)}, bf16[8,1024]{1,0:T(8,128)(2,1)S(1)}, u32[]{:S(2)}, u32[]{:S(2)}) collective-permute-start(bf16[8,1024]{1,0:T(8,128)(2,1)S(1)} %get-tuple-element.43), channel_id=1, source_target_pairs={{0,16},{4,20},{8,24},{12,28},{16,0},{20,4},{24,8},{28,12},{1,17},{... | collective-permute-start | bytes 49160 | tf_op jit(solution)/shard_map/ppermute | solution.py:425
  30.6 0.9 %collective-permute-start.10 = (bf16[8,1024]{1,0:T(8,128)(2,1)S(1)}, bf16[8,1024]{1,0:T(8,128)(2,1)S(1)}, u32[]{:S(2)}, u32[]{:S(2)}) collective-permute-start(bf16[8,1024]{1,0:T(8,128)(2,1)S(1)} %get-tuple-element.44), channel_id=1, source_target_pairs={{0,4},{4,0},{8,12},{12,8},{16,20},{20,16},{24,28},{28,24},{1,5},{5... | collective-permute-start | bytes 49160 | tf_op jit(solution)/shard_map/ppermute | solution.py:425
  31.4 1.1 %collective-permute-done.8.rest_0_ = bf16[8,1024]{1,0:T(8,128)(2,1)S(1)} collective-permute-done((bf16[8,1024]{1,0:T(8,128)(2,1)S(1)}, bf16[8,1024]{1,0:T(8,128)(2,1)S(1)}, u32[]{:S(2)}, u32[]{:S(2)}) %collective-permute-start.8) | collective-permute-done | bytes 16416 | tf_op jit(solution)/shard_map/ppermute | solution.py:425
  32.6 1.2 %collective-permute-done.9.rest_1_ = bf16[8,1024]{1,0:T(8,128)(2,1)S(1)} collective-permute-done((bf16[8,1024]{1,0:T(8,128)(2,1)S(1)}, bf16[8,1024]{1,0:T(8,128)(2,1)S(1)}, u32[]{:S(2)}, u32[]{:S(2)}) %collective-permute-start.9) | collective-permute-done | bytes 16416 | tf_op jit(solution)/shard_map/ppermute | solution.py:425
  33.8 0.5 %collective-permute-done.10.rest_2_ = bf16[8,1024]{1,0:T(8,128)(2,1)S(1)} collective-permute-done((bf16[8,1024]{1,0:T(8,128)(2,1)S(1)}, bf16[8,1024]{1,0:T(8,128)(2,1)S(1)}, u32[]{:S(2)}, u32[]{:S(2)}) %collective-permute-start.10) | collective-permute-done | bytes 16416 | tf_op jit(solution)/shard_map/ppermute | solution.py:425
  34.4 2.7 %collective-permute-start.11 = (bf16[4,1024]{1,0:T(4,128)(2,1)S(1)}, bf16[4,1024]{1,0:T(4,128)(2,1)S(1)}, u32[]{:S(2)}, u32[]{:S(2)}) collective-permute-start(bf16[4,1024]{1,0:T(4,128)(2,1)S(1)} %get-tuple-element.46), channel_id=1, source_target_pairs={{0,8},{4,12},{8,0},{12,4},{16,24},{20,28},{24,16},{28,20},{1,9},{5... | collective-permute-start | bytes 24584 | tf_op jit(solution)/shard_map/ppermute | solution.py:425
  37.0 2.0 %collective-permute-done.11.rest_0_ = bf16[4,1024]{1,0:T(4,128)(2,1)S(1)} collective-permute-done((bf16[4,1024]{1,0:T(4,128)(2,1)S(1)}, bf16[4,1024]{1,0:T(4,128)(2,1)S(1)}, u32[]{:S(2)}, u32[]{:S(2)}) %collective-permute-start.11) | collective-permute-done | bytes 8224 | tf_op jit(solution)/shard_map/ppermute | solution.py:425
  39.0 0.6 %shard_map.104 = bf16[4,1024]{1,0:T(4,128)(2,1)} custom-call(f32[4,1024]{1,0:T(4,128)S(1)} %get-tuple-element.45.a_ref, bf16[4,1024]{1,0:T(4,128)(2,1)S(1)} %collective-permute-done.11.rest_0_), custom_call_target="tpu_custom_call" | custom-call | tf_op jit(solution)/shard_map/pallas_call | solution.py:29
  (5 shorter events, 0.1 us)
Async XLA Ops:
  0.0 14.0 %copy-start.1 = (bf16[8,1024,768]{2,1,0:T(8,128)(2,1)S(1)}, bf16[8,1024,768]{2,1,0:T(8,128)(2,1)}, u32[]{:S(2)}) copy-start(bf16[8,1024,768]{2,1,0:T(8,128)(2,1)} %uw_ref.5) | copy-start | bytes 37748740
  1.0 12.9 %copy-start = (bf16[8,1024,768]{2,1,0:T(8,128)(2,1)S(1)}, bf16[8,1024,768]{2,1,0:T(8,128)(2,1)}, u32[]{:S(2)}) copy-start(bf16[8,1024,768]{2,1,0:T(8,128)(2,1)} %gw_ref.5) | copy-start | bytes 37748740
  1.1 5.9 %collective-permute-start = (bf16[4,1152]{1,0:T(4,128)(2,1)S(1)}, bf16[4,1152]{1,0:T(4,128)(2,1)S(1)}, u32[]{:S(2)}, u32[]{:S(2)}) collective-permute-start(bf16[4,1152]{1,0:T(4,128)(2,1)S(1)} %shard_map.91.refs_3_.refs_0_), channel_id=1, source_target_pairs={{0,8},{4,12},{8,0},{12,4},{16,24},{20,28},{24,16},{28,20},{1,9},{5... | collective-permute-start | bytes 27656 | tf_op jit(solution)/shard_map/ppermute | solution.py:425
  7.0 6.4 %collective-permute-start.3 = (bf16[8,1152]{1,0:T(8,128)(2,1)S(1)}, bf16[8,1152]{1,0:T(8,128)(2,1)S(1)}, u32[]{:S(2)}, u32[]{:S(2)}) collective-permute-start(bf16[8,1152]{1,0:T(8,128)(2,1)S(1)} %shard_map.93._.refs_0_), channel_id=1, source_target_pairs={{0,20},{4,16},{8,28},{12,24},{16,4},{20,0},{24,12},{28,8},{1,21},{... | collective-permute-start | bytes 55304 | tf_op jit(solution)/shard_map/ppermute | solution.py:425
  9.7 3.8 %collective-permute-start.2 = (bf16[8,1152]{1,0:T(8,128)(2,1)S(1)}, bf16[8,1152]{1,0:T(8,128)(2,1)S(1)}, u32[]{:S(2)}, u32[]{:S(2)}) collective-permute-start(bf16[8,1152]{1,0:T(8,128)(2,1)S(1)} %shard_map.93._.refs_0_), channel_id=1, source_target_pairs={{0,16},{4,20},{8,24},{12,28},{16,0},{20,4},{24,8},{28,12},{1,17},{... | collective-permute-start | bytes 55304 | tf_op jit(solution)/shard_map/ppermute | solution.py:425
  10.2 3.8 %collective-permute-start.1 = (bf16[8,1152]{1,0:T(8,128)(2,1)S(1)}, bf16[8,1152]{1,0:T(8,128)(2,1)S(1)}, u32[]{:S(2)}, u32[]{:S(2)}) collective-permute-start(bf16[8,1152]{1,0:T(8,128)(2,1)S(1)} %shard_map.93._.refs_0_), channel_id=1, source_target_pairs={{0,4},{4,0},{8,12},{12,8},{16,20},{20,16},{24,28},{28,24},{1,5},{5... | collective-permute-start | bytes 55304 | tf_op jit(solution)/shard_map/ppermute | solution.py:425
  16.4 1.4 %collective-permute-start.4 = (bf16[128,768]{1,0:T(8,128)(2,1)S(1)}, bf16[128,768]{1,0:T(8,128)(2,1)S(1)}, u32[]{:S(2)}, u32[]{:S(2)}) collective-permute-start(bf16[128,768]{1,0:T(8,128)(2,1)S(1)} %get-tuple-element.30), channel_id=1, source_target_pairs={{0,1},{1,0},{2,3},{3,2},{4,5},{5,4},{6,7},{7,6},{8,9},{9,8},{10,11... | collective-permute-start | bytes 589832 | tf_op jit(solution)/shard_map/ppermute | solution.py:414
  17.9 7.2 %collective-permute-start.5 = (bf16[80,768]{1,0:T(8,128)(2,1)S(1)}, bf16[80,768]{1,0:T(8,128)(2,1)S(1)}, u32[]{:S(2)}, u32[]{:S(2)}) collective-permute-start(bf16[80,768]{1,0:T(8,128)(2,1)S(1)} %get-tuple-element.32.rest_0_), channel_id=1, source_target_pairs={{0,2},{1,3},{2,0},{3,1},{4,6},{5,7},{6,4},{7,5},{8,10},{9,11},{10,... | collective-permute-start | bytes 368648 | tf_op jit(solution)/shard_map/ppermute | solution.py:414
  20.3 4.8 %collective-permute-start.6 = (bf16[48,768]{1,0:T(8,128)(2,1)S(1)}, bf16[48,768]{1,0:T(8,128)(2,1)S(1)}, u32[]{:S(2)}, u32[]{:S(2)}) collective-permute-start(bf16[48,768]{1,0:T(8,128)(2,1)S(1)} %get-tuple-element.34), channel_id=1, source_target_pairs={{0,2},{1,3},{2,0},{3,1},{4,6},{5,7},{6,4},{7,5},{8,10},{9,11},{10,... | collective-permute-start | bytes 221192 | tf_op jit(solution)/shard_map/ppermute | solution.py:414
  25.1 1.4 %collective-permute-start.7 = (bf16[128,384]{1,0:T(8,128)(2,1)S(1)}, bf16[128,384]{1,0:T(8,128)(2,1)S(1)}, u32[]{:S(2)}, u32[]{:S(2)}) collective-permute-start(bf16[128,384]{1,0:T(8,128)(2,1)S(1)} %shard_map.100.h_ref), channel_id=1, source_target_pairs={{0,1},{1,0},{2,3},{3,2},{4,5},{5,4},{6,7},{7,6},{8,9},{9,8},{10,11... | collective-permute-start | bytes 294920 | tf_op jit(solution)/shard_map/ppermute | solution.py:414
  27.9 4.7 %collective-permute-start.8 = (bf16[8,1024]{1,0:T(8,128)(2,1)S(1)}, bf16[8,1024]{1,0:T(8,128)(2,1)S(1)}, u32[]{:S(2)}, u32[]{:S(2)}) collective-permute-start(bf16[8,1024]{1,0:T(8,128)(2,1)S(1)} %get-tuple-element.42), channel_id=1, source_target_pairs={{0,20},{4,16},{8,28},{12,24},{16,4},{20,0},{24,12},{28,8},{1,21},{... | collective-permute-start | bytes 49160 | tf_op jit(solution)/shard_map/ppermute | solution.py:425
  30.1 3.7 %collective-permute-start.9 = (bf16[8,1024]{1,0:T(8,128)(2,1)S(1)}, bf16[8,1024]{1,0:T(8,128)(2,1)S(1)}, u32[]{:S(2)}, u32[]{:S(2)}) collective-permute-start(bf16[8,1024]{1,0:T(8,128)(2,1)S(1)} %get-tuple-element.43), channel_id=1, source_target_pairs={{0,16},{4,20},{8,24},{12,28},{16,0},{20,4},{24,8},{28,12},{1,17},{... | collective-permute-start | bytes 49160 | tf_op jit(solution)/shard_map/ppermute | solution.py:425
  30.6 3.7 %collective-permute-start.10 = (bf16[8,1024]{1,0:T(8,128)(2,1)S(1)}, bf16[8,1024]{1,0:T(8,128)(2,1)S(1)}, u32[]{:S(2)}, u32[]{:S(2)}) collective-permute-start(bf16[8,1024]{1,0:T(8,128)(2,1)S(1)} %get-tuple-element.44), channel_id=1, source_target_pairs={{0,4},{4,0},{8,12},{12,8},{16,20},{20,16},{24,28},{28,24},{1,5},{5... | collective-permute-start | bytes 49160 | tf_op jit(solution)/shard_map/ppermute | solution.py:425
  34.4 4.6 %collective-permute-start.11 = (bf16[4,1024]{1,0:T(4,128)(2,1)S(1)}, bf16[4,1024]{1,0:T(4,128)(2,1)S(1)}, u32[]{:S(2)}, u32[]{:S(2)}) collective-permute-start(bf16[4,1024]{1,0:T(4,128)(2,1)S(1)} %get-tuple-element.46), channel_id=1, source_target_pairs={{0,8},{4,12},{8,0},{12,4},{16,24},{20,28},{24,16},{28,20},{1,9},{5... | collective-permute-start | bytes 24584 | tf_op jit(solution)/shard_map/ppermute | solution.py:425

commit v8 on v6

--- a/solution.py
+++ b/solution.py
@@ -261,17 +261,26 @@
     return run(kernel, [sds(own.shape, F32), sds(own.shape, BF)], [VM] * 2, (own, got), flops=hint)
 
 
-def activate(own, got, after):
-    slots, hidden = own.shape
+def activate(pairs):
+    hidden = pairs[0][0].shape[1]
+    rows = [own.shape[0] for own, _ in pairs]
     n = hidden // 2
 
-    def kernel(a_ref, b_ref, *rest):
-        o_ref = rest[-1]
-        gate = a_ref[:, :n] + b_ref[:, :n].astype(F32)
-        up = a_ref[:, n:] + b_ref[:, n:].astype(F32)
-        o_ref[...] = (jax.nn.silu(gate) * up).astype(BF)
-
-    return run(kernel, sds((slots, n), BF), [VM] * (2 + len(after)), (own, got, *after))
+    def kernel(*refs):
+        first = 0
+        for i, count in enumerate(rows):
+            a_ref, b_ref = refs[2 * i : 2 * i + 2]
+            gate = a_ref[:, :n] + b_ref[:, :n].astype(F32)
+            up = a_ref[:, n:] + b_ref[:, n:].astype(F32)
+            refs[-1][first : first + count] = (jax.nn.silu(gate) * up).astype(BF)
+            first += count
+
+    return run(
+        kernel,
+        sds((sum(rows), n), BF),
+        [VM] * (2 * len(pairs)),
+        [a for pair in pairs for a in pair],
+    )
 
 
 def spread_rows(h_ref, sel_ref, wt_ref, per, chosen):
@@ -411,7 +420,7 @@
     got = swap(send, "pool", 1)
     experts = gw.shape[0]
     per = xs.shape[0] // experts
-    cut = experts // 2
+    cut = experts * 6 // 8
     parts = [range(cut), range(cut, experts)] if cut else [range(experts)]
     steps = bits(n_pool)[1:]
     sums, after = [], []
@@ -424,14 +433,11 @@
             arrived, first = swap(send, "pool", bit), 0
             after = [send]
         sums.append((own, arrived))
-    acc = None
-    for i, (part, pair) in enumerate(zip(parts, sums)):
-        hid = activate(*pair, [] if acc is None else [acc])
-        other = swap(hid, "pool", 1)
-        (acc,) = down_kernel(hid, sel, wt, dw, ds, acc, part, False, 1)
-        ends = i + 1 == len(parts)
-        acc, *sends = down_kernel(other, sel, wt, dw, ds, acc, part, True, 4 if ends else 1)
-    to_a, to_b, to_far = sends
+    everyone = range(experts)
+    hid = activate(sums)
+    other = swap(hid, "pool", 1)
+    (acc,) = down_kernel(hid, sel, wt, dw, ds, None, everyone, False, 1)
+    acc, to_a, to_b, to_far = down_kernel(other, sel, wt, dw, ds, acc, everyone, True, 4)
     far, near_a, near_b = hop(to_far, a, b), hop(to_a, a), hop(to_b, b)
     got = [far, near_b, near_a]
     for step in reversed(single):

time: 40.1 us -> 39.9 us (level)
  waiting for transfers between devices: 11.7 us -> 12.6 us
  Pallas kernels: 11.4 us -> 10.7 us
    ppermute x5 -> x4, waiting for transfers between devices: 4.52 us -> 5.2 us  [swap(): lax.ppermute(x, axis, [(j, j ^ bit) for j in range(lax.axis_size(axis))])]
    pallas_call x17 -> x14, Pallas kernels: 11.4 us -> 10.7 us  [run(): pl.pallas_call(kernel, out_shape=out_shape, in_specs=in_specs, out_specs=...]
    ppermute x5 -> x4, starting transfers between devices: 2.39 us -> 2.17 us  [swap(): lax.ppermute(x, axis, [(j, j ^ bit) for j in range(lax.axis_size(axis))])]
  transfers between devices with their start and end apart: 13 -> 12, of which waited for: 11 -> 8; matrix products, arithmetic and copies ran while one was open for 0% -> 0% of each run, Pallas kernels for 13% -> 12%
where the time goes in v8:
time: 39.9 us; the launch traced here: 39.6 us
  starting transfers between devices  16.1 us (40%)
  waiting for transfers between devices  12.6 us (32%)
  Pallas kernels  10.7 us (27%)
    ppermute x8, starting transfers between devices, hop(): return lax.ppermute(x, ('seq', 'head'), pairs)  14 us
    pallas_call x14, Pallas kernels, run(): pl.pallas_call(kernel, out_shape=out_shape, in_specs=in_specs, out_specs=...  10.7 us
    ppermute x8, waiting for transfers between devices, hop(): return lax.ppermute(x, ('seq', 'head'), pairs)  7.37 us
    ppermute x4, waiting for transfers between devices, swap(): lax.ppermute(x, axis, [(j, j ^ bit) for j in range(lax.axis_size(axis))])  5.2 us
    ppermute x4, starting transfers between devices, swap(): lax.ppermute(x, axis, [(j, j ^ bit) for j in range(lax.axis_size(axis))])  2.17 us
  transfers between devices with their start and end apart: 12, of which 8 were waited for; matrix products, arithmetic and copies ran while one was open for 0% of the time, Pallas kernels for 12%

profile of v8, /device:TPU:0, one launch (start us, length us, event | category | flops | bytes accessed | tf_op | source)
XLA Modules:
  0.0 39.6 jit_solution(7348020902972546021)
XLA Ops:
  0.0 0.0 copy-start.1
  0.0 0.0 copy-start
  0.0 1.0 %shard_map.91.refs_3_.refs_0_ = bf16[4,1152]{1,0:T(4,128)(2,1)S(1)} custom-call(bf16[4,1024]{1,0:T(4,128)(2,1)} %t_in.1, s32[4,8]{1,0:T(4,128)} %r_in.1, s32[4,8]{1,0:T(4,128)} %g_in.1), custom_call_target="tpu_custom_call" | custom-call | flops 12582912000 | tf_op jit(solution)/shard_map/pallas_call | solution.py:29
  1.0 4.1 %collective-permute-start = (bf16[4,1152]{1,0:T(4,128)(2,1)S(1)}, bf16[4,1152]{1,0:T(4,128)(2,1)S(1)}, u32[]{:S(2)}, u32[]{:S(2)}) collective-permute-start(bf16[4,1152]{1,0:T(4,128)(2,1)S(1)} %shard_map.91.refs_3_.refs_0_), channel_id=1, source_target_pairs={{0,8},{4,12},{8,0},{12,4},{16,24},{20,28},{24,16},{28,20},{1,9},{5... | collective-permute-start | bytes 27656 | tf_op jit(solution)/shard_map/ppermute | solution.py:394
  5.2 1.8 %shard_map.92 = (f32[6,8,8,128]{3,2,1,0:T(8,128)S(1)}, f32[6,8,8,128]{3,2,1,0:T(8,128)S(1)}, f32[6,8,8,128]{3,2,1,0:T(8,128)S(1)}) custom-call(bf16[6,8,8]{2,1,0:T(8,128)(2,1)} %bitcast.5, bf16[6,8,8]{2,1,0:T(8,128)(2,1)} %bitcast.6, bf16[6,8,8]{2,1,0:T(8,128)(2,1)} %bitcast.7, bf16[4,1152]{1,0:T(4,128)(2,1)S(1)} %shard_map.91.refs_3_.refs_0_), custom_call_target="tpu_custom_call" | custom-call | bytes 1048576 | tf_op jit(solution)/shard_map/pallas_call | solution.py:29
  7.0 0.0 collective-permute-done.refs_1_
  7.0 2.6 %collective-permute-start.3 = (bf16[8,1152]{1,0:T(8,128)(2,1)S(1)}, bf16[8,1152]{1,0:T(8,128)(2,1)S(1)}, u32[]{:S(2)}, u32[]{:S(2)}) collective-permute-start(bf16[8,1152]{1,0:T(8,128)(2,1)S(1)} %shard_map.93.refs_0_), channel_id=1, source_target_pairs={{0,20},{4,16},{8,28},{12,24},{16,4},{20,0},{24,12},{28,8},{1,21},{... | collective-permute-start | bytes 55304 | tf_op jit(solution)/shard_map/ppermute | solution.py:394
  9.7 0.5 %collective-permute-start.2 = (bf16[8,1152]{1,0:T(8,128)(2,1)S(1)}, bf16[8,1152]{1,0:T(8,128)(2,1)S(1)}, u32[]{:S(2)}, u32[]{:S(2)}) collective-permute-start(bf16[8,1152]{1,0:T(8,128)(2,1)S(1)} %shard_map.93.refs_0_), channel_id=1, source_target_pairs={{0,16},{4,20},{8,24},{12,28},{16,0},{20,4},{24,8},{28,12},{1,17},{... | collective-permute-start | bytes 55304 | tf_op jit(solution)/shard_map/ppermute | solution.py:394
  10.2 0.4 collective-permute-start.1
  10.6 1.3 %collective-permute-done.3.refs_3_ = bf16[8,1152]{1,0:T(8,128)(2,1)S(1)} collective-permute-done((bf16[8,1152]{1,0:T(8,128)(2,1)S(1)}, bf16[8,1152]{1,0:T(8,128)(2,1)S(1)}, u32[]{:S(2)}, u32[]{:S(2)}) %collective-permute-start.3) | collective-permute-done | bytes 18464 | tf_op jit(solution)/shard_map/ppermute | solution.py:394
  11.8 1.6 %collective-permute-done.2.refs_2_ = bf16[8,1152]{1,0:T(8,128)(2,1)S(1)} collective-permute-done((bf16[8,1152]{1,0:T(8,128)(2,1)S(1)}, bf16[8,1152]{1,0:T(8,128)(2,1)S(1)}, u32[]{:S(2)}, u32[]{:S(2)}) %collective-permute-start.2) | collective-permute-done | bytes 18464 | tf_op jit(solution)/shard_map/ppermute | solution.py:394
  13.4 0.5 %collective-permute-done.1.refs_1_ = bf16[8,1152]{1,0:T(8,128)(2,1)S(1)} collective-permute-done((bf16[8,1152]{1,0:T(8,128)(2,1)S(1)}, bf16[8,1152]{1,0:T(8,128)(2,1)S(1)}, u32[]{:S(2)}, u32[]{:S(2)}) %collective-permute-start.1) | collective-permute-done | bytes 18464 | tf_op jit(solution)/shard_map/ppermute | solution.py:394
  14.0 0.0 copy-done.1
  14.0 0.0 copy-done
  14.0 2.4 %shard_map.95 = (bf16[128,768]{1,0:T(8,128)(2,1)S(1)}, bf16[128,1024]{1,0:T(8,128)(2,1)S(1)}, bf16[32,128]{1,0:T(8,128)(2,1)S(1)}, f32[32,128]{1,0:T(8,128)S(1)}) custom-call(bf16[32,1152]{1,0:T(8,128)(2,1)S(1)} %shard_map.94.x_ref, bf16[8,1024,768]{2,1,0:T(8,128)(2,1)S(1)} %copy-done, bf16[8,1024,768]{2,1,0:T(8,128)(2,1)S(1)} %copy-done.1, ...), custom_call_target="tpu_custom_call" | custom-call | flops 65536 | bytes 65536 | tf_op jit(solution)/shard_map/pallas_call | solution.py:29
  16.4 0.0 collective-permute-start.4
  16.4 1.5 %shard_map.96.a_ref = f32[96,768]{1,0:T(8,128)S(1)} custom-call(bf16[128,1024]{1,0:T(8,128)(2,1)S(1)} %get-tuple-element.24.xs_ref, bf16[8,1024,768]{2,1,0:T(8,128)(2,1)S(1)} %copy-done, bf16[8,1024,768]{2,1,0:T(8,128)(2,1)S(1)} %copy-done.1, f32[6,8,8,128]{3,2,1,0:T(8,128)S(1)} %get-tuple-element.22.refs_2_.gs_ref, ...), custom_call_target="tpu_custom_call" | custom-call | flops 65536 | bytes 65536 | tf_op jit(solution)/shard_map/pallas_call | solution.py:29
  17.9 0.0 collective-permute-done.4.b_ref
  17.9 0.0 slice-start
  17.9 0.0 slice-start.1
  17.9 0.6 %shard_map.98.a_ref = f32[32,768]{1,0:T(8,128)S(1)} custom-call(bf16[128,1024]{1,0:T(8,128)(2,1)S(1)} %get-tuple-element.24.xs_ref, bf16[8,1024,768]{2,1,0:T(8,128)(2,1)S(1)} %copy-done, bf16[8,1024,768]{2,1,0:T(8,128)(2,1)S(1)} %copy-done.1, f32[6,8,8,128]{3,2,1,0:T(8,128)S(1)} %get-tuple-element.22.refs_2_.gs_ref, ...), custom_call_target="tpu_custom_call" | custom-call | flops 65536 | bytes 65536 | tf_op jit(solution)/shard_map/pallas_call | solution.py:29
  18.5 0.0 slice-start.2
  18.5 1.5 %collective-permute-start.5 = (bf16[96,768]{1,0:T(8,128)(2,1)S(1)}, bf16[96,768]{1,0:T(8,128)(2,1)S(1)}, u32[]{:S(2)}, u32[]{:S(2)}) collective-permute-start(bf16[96,768]{1,0:T(8,128)(2,1)S(1)} %get-tuple-element.27.rest_0_), channel_id=1, source_target_pairs={{0,2},{1,3},{2,0},{3,1},{4,6},{5,7},{6,4},{7,5},{8,10},{9,11},{10,... | collective-permute-start | bytes 442376 | tf_op jit(solution)/shard_map/ppermute | solution.py:383
  20.1 0.6 %collective-permute-start.6 = (bf16[32,768]{1,0:T(8,128)(2,1)S(1)}, bf16[32,768]{1,0:T(8,128)(2,1)S(1)}, u32[]{:S(2)}, u32[]{:S(2)}) collective-permute-start(bf16[32,768]{1,0:T(8,128)(2,1)S(1)} %get-tuple-element.29), channel_id=1, source_target_pairs={{0,2},{1,3},{2,0},{3,1},{4,6},{5,7},{6,4},{7,5},{8,10},{9,11},{10,... | collective-permute-start | bytes 147464 | tf_op jit(solution)/shard_map/ppermute | solution.py:383
  20.6 5.2 %collective-permute-done.6.refs_3_ = bf16[32,768]{1,0:T(8,128)(2,1)S(1)} collective-permute-done((bf16[32,768]{1,0:T(8,128)(2,1)S(1)}, bf16[32,768]{1,0:T(8,128)(2,1)S(1)}, u32[]{:S(2)}, u32[]{:S(2)}) %collective-permute-start.6) | collective-permute-done | bytes 49184 | tf_op jit(solution)/shard_map/ppermute | solution.py:383
  25.8 0.0 collective-permute-done.5.refs_1_
  25.8 0.1 shard_map.100.h_ref
  25.9 0.1 collective-permute-start.7
  26.0 0.0 slice-done
  26.0 0.0 slice-done.1
  26.0 0.0 slice-done.2
  26.0 1.3 %shard_map.101.rest_0_ = f32[32,1024]{1,0:T(8,128)S(1)} custom-call(bf16[128,384]{1,0:T(8,128)(2,1)S(1)} %shard_map.100.h_ref, bf16[32,128]{1,0:T(8,128)(2,1)S(1)} %get-tuple-element.30.sel_ref, f32[32,128]{1,0:T(8,128)S(1)} %get-tuple-element.31.wt_ref, bf16[8,768,1024]{2,1,0:T(8,128)(2,1)S(1)} %bitcast.4, f32[6,8,8,128]{3,2,1,0:T(8,128)S(1)} %get-tuple-element.32.ds_ref), custom_call_target="tpu_custom_call" | custom-call | flops 65536 | bytes 65536 | tf_op jit(solution)/shard_map/pallas_call | solution.py:29
  27.4 0.0 collective-permute-done.7.h_ref
  27.4 1.3 %shard_map.102 = (f32[8,1024]{1,0:T(8,128)S(1)}, bf16[8,1024]{1,0:T(8,128)(2,1)S(1)}, bf16[8,1024]{1,0:T(8,128)(2,1)S(1)}, bf16[8,1024]{1,0:T(8,128)(2,1)S(1)}) custom-call(bf16[128,384]{1,0:T(8,128)(2,1)S(1)} %collective-permute-done.7.h_ref, bf16[32,128]{1,0:T(8,128)(2,1)S(1)} %get-tuple-element.30.sel_ref, f32[32,128]{1,0:T(8,128)S(1)} %get-tuple-element.31.wt_ref, ...), custom_call_target="tpu_custom_call" | custom-call | flops 65536 | bytes 65536 | tf_op jit(solution)/shard_map/pallas_call | solution.py:29
  28.7 1.4 %collective-permute-start.8 = (bf16[8,1024]{1,0:T(8,128)(2,1)S(1)}, bf16[8,1024]{1,0:T(8,128)(2,1)S(1)}, u32[]{:S(2)}, u32[]{:S(2)}) collective-permute-start(bf16[8,1024]{1,0:T(8,128)(2,1)S(1)} %get-tuple-element.34), channel_id=1, source_target_pairs={{0,20},{4,16},{8,28},{12,24},{16,4},{20,0},{24,12},{28,8},{1,21},{... | collective-permute-start | bytes 49160 | tf_op jit(solution)/shard_map/ppermute | solution.py:394
  30.1 0.5 %collective-permute-start.9 = (bf16[8,1024]{1,0:T(8,128)(2,1)S(1)}, bf16[8,1024]{1,0:T(8,128)(2,1)S(1)}, u32[]{:S(2)}, u32[]{:S(2)}) collective-permute-start(bf16[8,1024]{1,0:T(8,128)(2,1)S(1)} %get-tuple-element.35), channel_id=1, source_target_pairs={{0,16},{4,20},{8,24},{12,28},{16,0},{20,4},{24,8},{28,12},{1,17},{... | collective-permute-start | bytes 49160 | tf_op jit(solution)/shard_map/ppermute | solution.py:394
  30.6 1.6 %collective-permute-start.10 = (bf16[8,1024]{1,0:T(8,128)(2,1)S(1)}, bf16[8,1024]{1,0:T(8,128)(2,1)S(1)}, u32[]{:S(2)}, u32[]{:S(2)}) collective-permute-start(bf16[8,1024]{1,0:T(8,128)(2,1)S(1)} %get-tuple-element.36), channel_id=1, source_target_pairs={{0,4},{4,0},{8,12},{12,8},{16,20},{20,16},{24,28},{28,24},{1,5},{5... | collective-permute-start | bytes 49160 | tf_op jit(solution)/shard_map/ppermute | solution.py:394
  32.3 1.1 %collective-permute-done.8.rest_0_ = bf16[8,1024]{1,0:T(8,128)(2,1)S(1)} collective-permute-done((bf16[8,1024]{1,0:T(8,128)(2,1)S(1)}, bf16[8,1024]{1,0:T(8,128)(2,1)S(1)}, u32[]{:S(2)}, u32[]{:S(2)}) %collective-permute-start.8) | collective-permute-done | bytes 16416 | tf_op jit(solution)/shard_map/ppermute | solution.py:394
  33.4 0.5 %collective-permute-done.9.rest_1_ = bf16[8,1024]{1,0:T(8,128)(2,1)S(1)} collective-permute-done((bf16[8,1024]{1,0:T(8,128)(2,1)S(1)}, bf16[8,1024]{1,0:T(8,128)(2,1)S(1)}, u32[]{:S(2)}, u32[]{:S(2)}) %collective-permute-start.9) | collective-permute-done | bytes 16416 | tf_op jit(solution)/shard_map/ppermute | solution.py:394
  33.9 0.5 %collective-permute-done.10.rest_2_ = bf16[8,1024]{1,0:T(8,128)(2,1)S(1)} collective-permute-done((bf16[8,1024]{1,0:T(8,128)(2,1)S(1)}, bf16[8,1024]{1,0:T(8,128)(2,1)S(1)}, u32[]{:S(2)}, u32[]{:S(2)}) %collective-permute-start.10) | collective-permute-done | bytes 16416 | tf_op jit(solution)/shard_map/ppermute | solution.py:394
  34.4 2.7 %collective-permute-start.11 = (bf16[4,1024]{1,0:T(4,128)(2,1)S(1)}, bf16[4,1024]{1,0:T(4,128)(2,1)S(1)}, u32[]{:S(2)}, u32[]{:S(2)}) collective-permute-start(bf16[4,1024]{1,0:T(4,128)(2,1)S(1)} %get-tuple-element.38), channel_id=1, source_target_pairs={{0,8},{4,12},{8,0},{12,4},{16,24},{20,28},{24,16},{28,20},{1,9},{5... | collective-permute-start | bytes 24584 | tf_op jit(solution)/shard_map/ppermute | solution.py:394
  37.1 1.9 %collective-permute-done.11.rest_0_ = bf16[4,1024]{1,0:T(4,128)(2,1)S(1)} collective-permute-done((bf16[4,1024]{1,0:T(4,128)(2,1)S(1)}, bf16[4,1024]{1,0:T(4,128)(2,1)S(1)}, u32[]{:S(2)}, u32[]{:S(2)}) %collective-permute-start.11) | collective-permute-done | bytes 8224 | tf_op jit(solution)/shard_map/ppermute | solution.py:394
  39.0 0.6 %shard_map.104 = bf16[4,1024]{1,0:T(4,128)(2,1)} custom-call(f32[4,1024]{1,0:T(4,128)S(1)} %get-tuple-element.37.a_ref, bf16[4,1024]{1,0:T(4,128)(2,1)S(1)} %collective-permute-done.11.rest_0_), custom_call_target="tpu_custom_call" | custom-call | tf_op jit(solution)/shard_map/pallas_call | solution.py:29
  (6 shorter events, 0.1 us)
Async XLA Ops:
  0.0 14.0 %copy-start.1 = (bf16[8,1024,768]{2,1,0:T(8,128)(2,1)S(1)}, bf16[8,1024,768]{2,1,0:T(8,128)(2,1)}, u32[]{:S(2)}) copy-start(bf16[8,1024,768]{2,1,0:T(8,128)(2,1)} %uw_ref.5) | copy-start | bytes 37748740
  0.0 14.0 %copy-start = (bf16[8,1024,768]{2,1,0:T(8,128)(2,1)S(1)}, bf16[8,1024,768]{2,1,0:T(8,128)(2,1)}, u32[]{:S(2)}) copy-start(bf16[8,1024,768]{2,1,0:T(8,128)(2,1)} %gw_ref.5) | copy-start | bytes 37748740
  1.0 5.9 %collective-permute-start = (bf16[4,1152]{1,0:T(4,128)(2,1)S(1)}, bf16[4,1152]{1,0:T(4,128)(2,1)S(1)}, u32[]{:S(2)}, u32[]{:S(2)}) collective-permute-start(bf16[4,1152]{1,0:T(4,128)(2,1)S(1)} %shard_map.91.refs_3_.refs_0_), channel_id=1, source_target_pairs={{0,8},{4,12},{8,0},{12,4},{16,24},{20,28},{24,16},{28,20},{1,9},{5... | collective-permute-start | bytes 27656 | tf_op jit(solution)/shard_map/ppermute | solution.py:394
  7.0 4.8 %collective-permute-start.3 = (bf16[8,1152]{1,0:T(8,128)(2,1)S(1)}, bf16[8,1152]{1,0:T(8,128)(2,1)S(1)}, u32[]{:S(2)}, u32[]{:S(2)}) collective-permute-start(bf16[8,1152]{1,0:T(8,128)(2,1)S(1)} %shard_map.93.refs_0_), channel_id=1, source_target_pairs={{0,20},{4,16},{8,28},{12,24},{16,4},{20,0},{24,12},{28,8},{1,21},{... | collective-permute-start | bytes 55304 | tf_op jit(solution)/shard_map/ppermute | solution.py:394
  9.7 3.8 %collective-permute-start.2 = (bf16[8,1152]{1,0:T(8,128)(2,1)S(1)}, bf16[8,1152]{1,0:T(8,128)(2,1)S(1)}, u32[]{:S(2)}, u32[]{:S(2)}) collective-permute-start(bf16[8,1152]{1,0:T(8,128)(2,1)S(1)} %shard_map.93.refs_0_), channel_id=1, source_target_pairs={{0,16},{4,20},{8,24},{12,28},{16,0},{20,4},{24,8},{28,12},{1,17},{... | collective-permute-start | bytes 55304 | tf_op jit(solution)/shard_map/ppermute | solution.py:394
  10.2 3.8 %collective-permute-start.1 = (bf16[8,1152]{1,0:T(8,128)(2,1)S(1)}, bf16[8,1152]{1,0:T(8,128)(2,1)S(1)}, u32[]{:S(2)}, u32[]{:S(2)}) collective-permute-start(bf16[8,1152]{1,0:T(8,128)(2,1)S(1)} %shard_map.93.refs_0_), channel_id=1, source_target_pairs={{0,4},{4,0},{8,12},{12,8},{16,20},{20,16},{24,28},{28,24},{1,5},{5... | collective-permute-start | bytes 55304 | tf_op jit(solution)/shard_map/ppermute | solution.py:394
  16.4 1.5 %collective-permute-start.4 = (bf16[128,768]{1,0:T(8,128)(2,1)S(1)}, bf16[128,768]{1,0:T(8,128)(2,1)S(1)}, u32[]{:S(2)}, u32[]{:S(2)}) collective-permute-start(bf16[128,768]{1,0:T(8,128)(2,1)S(1)} %get-tuple-element.25), channel_id=1, source_target_pairs={{0,1},{1,0},{2,3},{3,2},{4,5},{5,4},{6,7},{7,6},{8,9},{9,8},{10,11... | collective-permute-start | bytes 589832 | tf_op jit(solution)/shard_map/ppermute | solution.py:383
  17.9 8.1 %slice-start = ((s8[12582912]{0:T(1024)(128)(4,1)}), s8[4194304]{0:T(1024)(128)(4,1)S(1)}, s32[]{:S(2)}) async-start(s8[12582912]{0:T(1024)(128)(4,1)} %bitcast.3), calls=%async_computation | async-start | bytes 8388608
  17.9 8.1 %slice-start.1 = ((s8[12582912]{0:T(1024)(128)(4,1)}), s8[4194304]{0:T(1024)(128)(4,1)S(1)}, s32[]{:S(2)}) async-start(s8[12582912]{0:T(1024)(128)(4,1)} %bitcast.3), calls=%async_computation.1 | async-start | bytes 8388608
  18.5 7.5 %slice-start.2 = ((s8[12582912]{0:T(1024)(128)(4,1)}), s8[4194304]{0:T(1024)(128)(4,1)S(1)}, s32[]{:S(2)}) async-start(s8[12582912]{0:T(1024)(128)(4,1)} %bitcast.3), calls=%async_computation.2 | async-start | bytes 8388608
  18.5 7.3 %collective-permute-start.5 = (bf16[96,768]{1,0:T(8,128)(2,1)S(1)}, bf16[96,768]{1,0:T(8,128)(2,1)S(1)}, u32[]{:S(2)}, u32[]{:S(2)}) collective-permute-start(bf16[96,768]{1,0:T(8,128)(2,1)S(1)} %get-tuple-element.27.rest_0_), channel_id=1, source_target_pairs={{0,2},{1,3},{2,0},{3,1},{4,6},{5,7},{6,4},{7,5},{8,10},{9,11},{10,... | collective-permute-start | bytes 442376 | tf_op jit(solution)/shard_map/ppermute | solution.py:383
  20.1 5.8 %collective-permute-start.6 = (bf16[32,768]{1,0:T(8,128)(2,1)S(1)}, bf16[32,768]{1,0:T(8,128)(2,1)S(1)}, u32[]{:S(2)}, u32[]{:S(2)}) collective-permute-start(bf16[32,768]{1,0:T(8,128)(2,1)S(1)} %get-tuple-element.29), channel_id=1, source_target_pairs={{0,2},{1,3},{2,0},{3,1},{4,6},{5,7},{6,4},{7,5},{8,10},{9,11},{10,... | collective-permute-start | bytes 147464 | tf_op jit(solution)/shard_map/ppermute | solution.py:383
  25.9 1.5 %collective-permute-start.7 = (bf16[128,384]{1,0:T(8,128)(2,1)S(1)}, bf16[128,384]{1,0:T(8,128)(2,1)S(1)}, u32[]{:S(2)}, u32[]{:S(2)}) collective-permute-start(bf16[128,384]{1,0:T(8,128)(2,1)S(1)} %shard_map.100.h_ref), channel_id=1, source_target_pairs={{0,1},{1,0},{2,3},{3,2},{4,5},{5,4},{6,7},{7,6},{8,9},{9,8},{10,11... | collective-permute-start | bytes 294920 | tf_op jit(solution)/shard_map/ppermute | solution.py:383
  28.7 4.7 %collective-permute-start.8 = (bf16[8,1024]{1,0:T(8,128)(2,1)S(1)}, bf16[8,1024]{1,0:T(8,128)(2,1)S(1)}, u32[]{:S(2)}, u32[]{:S(2)}) collective-permute-start(bf16[8,1024]{1,0:T(8,128)(2,1)S(1)} %get-tuple-element.34), channel_id=1, source_target_pairs={{0,20},{4,16},{8,28},{12,24},{16,4},{20,0},{24,12},{28,8},{1,21},{... | collective-permute-start | bytes 49160 | tf_op jit(solution)/shard_map/ppermute | solution.py:394
  30.1 3.7 %collective-permute-start.9 = (bf16[8,1024]{1,0:T(8,128)(2,1)S(1)}, bf16[8,1024]{1,0:T(8,128)(2,1)S(1)}, u32[]{:S(2)}, u32[]{:S(2)}) collective-permute-start(bf16[8,1024]{1,0:T(8,128)(2,1)S(1)} %get-tuple-element.35), channel_id=1, source_target_pairs={{0,16},{4,20},{8,24},{12,28},{16,0},{20,4},{24,8},{28,12},{1,17},{... | collective-permute-start | bytes 49160 | tf_op jit(solution)/shard_map/ppermute | solution.py:394
  30.6 3.7 %collective-permute-start.10 = (bf16[8,1024]{1,0:T(8,128)(2,1)S(1)}, bf16[8,1024]{1,0:T(8,128)(2,1)S(1)}, u32[]{:S(2)}, u32[]{:S(2)}) collective-permute-start(bf16[8,1024]{1,0:T(8,128)(2,1)S(1)} %get-tuple-element.36), channel_id=1, source_target_pairs={{0,4},{4,0},{8,12},{12,8},{16,20},{20,16},{24,28},{28,24},{1,5},{5... | collective-permute-start | bytes 49160 | tf_op jit(solution)/shard_map/ppermute | solution.py:394
  34.4 4.6 %collective-permute-start.11 = (bf16[4,1024]{1,0:T(4,128)(2,1)S(1)}, bf16[4,1024]{1,0:T(4,128)(2,1)S(1)}, u32[]{:S(2)}, u32[]{:S(2)}) collective-permute-start(bf16[4,1024]{1,0:T(4,128)(2,1)S(1)} %get-tuple-element.38), channel_id=1, source_target_pairs={{0,8},{4,12},{8,0},{12,4},{16,24},{20,28},{24,16},{28,20},{1,9},{5... | collective-permute-start | bytes 24584 | tf_op jit(solution)/shard_map/ppermute | solution.py:394

commit v9 on v8

--- a/solution.py
+++ b/solution.py
@@ -59,16 +59,15 @@
     rows, width = tokens.shape
     top = routes.shape[1]
 
-    def kernel(t_in, r_in, g_in, x_out, t_v, r_v, g_v, sems):
+    def kernel(t_in, r_in, g_in, x_out, r_v, g_v, sems):
         copies = [
             pltpu.make_async_copy(src, dst, sems.at[i])
-            for i, (src, dst) in enumerate(((r_in, r_v), (g_in, g_v), (t_in, t_v)))
+            for i, (src, dst) in enumerate(((r_in, r_v), (g_in, g_v), (t_in, x_out.at[:, pl.ds(0, width)])))
         ]
         for copy in copies:
             copy.start()
-        for copy in copies:
+        for copy in copies[:2]:
             copy.wait()
-        x_out[:, :width] = t_v[...]
         gate = g_v[...]
         meta = (
             placed(r_v[...], 0)
@@ -76,6 +75,7 @@
             + placed(gate & 255, 2 * top)
         )
         x_out[:, width:] = meta.astype(BF)
+        copies[2].wait()
 
     arrays = [in_hbm(a) for a in (tokens, routes, gates)]
     return run(
@@ -84,7 +84,7 @@
         [HB] * len(arrays),
         arrays,
         flops=hint,
-        scratch_shapes=[pltpu.VMEM(a.shape, a.dtype) for a in arrays]
+        scratch_shapes=[pltpu.VMEM(a.shape, a.dtype) for a in arrays[1:]]
         + [pltpu.SemaphoreType.DMA((len(arrays),))],
     )
 
@@ -105,7 +105,7 @@
     )
 
 
-def spread_scales(scales, after):
+def spread_scales(scales, after, hint):
     def kernel(*refs):
         count = len(scales)
         ins, outs, held, sems = refs[:count], refs[count + 1 : 2 * count + 1], refs[2 * count + 1 : -1], refs[-1]
@@ -126,6 +126,7 @@
         [sds((s.shape[0], s.shape[2], s.shape[1], LANES), F32) for s in scales],
         [HB] * len(scales) + [VM],
         (*[in_hbm(s) for s in scales], after),
+        flops=hint,
         bytes_=1 << 20,
         scratch_shapes=[pltpu.VMEM(s.shape, s.dtype) for s in scales]
         + [pltpu.SemaphoreType.DMA((len(scales),))],
@@ -404,13 +405,13 @@
     top = routes.shape[1]
     hops = [("head", b) for b in reversed(bits(n_head))] + [("seq", b) for b in bits(n_seq)]
 
-    x = pack(tokens, routes, gate_fixed, HINT * (gw.size + uw.size))
+    x = pack(tokens, routes, gate_fixed, NEAR)
     scales = [gs.transpose(2, 0, 1), us.transpose(2, 0, 1), ds.transpose(1, 0, 2)]
     single, (a, b) = hops[:-2], hops[-2:]
     for step in single:
         got = hop(x, step)
         if scales:
-            gs, us, ds = spread_scales(scales, x)
+            gs, us, ds = spread_scales(scales, x, HINT * (gw.size + uw.size))
         x = cat([x, got], [gs] if scales else [], HINT * dw.size * LATE if scales else 0)
         scales = []
     far, near_a, near_b = hop(x, a, b), hop(x, a), hop(x, b)
@@ -420,7 +421,7 @@
     got = swap(send, "pool", 1)
     experts = gw.shape[0]
     per = xs.shape[0] // experts
-    cut = experts * 6 // 8
+    cut = experts * 5 // 8
     parts = [range(cut), range(cut, experts)] if cut else [range(experts)]
     steps = bits(n_pool)[1:]
     sums, after = [], []

time: 39.9 us -> 40.2 us (level)
  waiting for transfers between devices: 12.6 us -> 14.4 us
  Pallas kernels: 10.7 us -> 9.96 us
  starting transfers between devices: 16.1 us -> 15.5 us
    ppermute x8, waiting for transfers between devices: 7.37 us -> 9.23 us  [hop(): return lax.ppermute(x, ('seq', 'head'), pairs)]
    pallas_call x14, Pallas kernels: 10.7 us -> 9.96 us  [run(): pl.pallas_call(kernel, out_shape=out_shape, in_specs=in_specs, out_specs=...]
    ppermute x8, starting transfers between devices: 14 us -> 13.3 us  [hop(): return lax.ppermute(x, ('seq', 'head'), pairs)]
  transfers between devices with their start and end apart: 12 -> 12, of which waited for: 8 -> 10; matrix products, arithmetic and copies ran while one was open for 0% -> 0% of each run, Pallas kernels for 12% -> 10%
where the time goes in v9:
time: 40.2 us; the launch traced here: 40 us
  starting transfers between devices  15.5 us (39%)
  waiting for transfers between devices  14.4 us (36%)
  Pallas kernels  9.96 us (25%)
    ppermute x8, starting transfers between devices, hop(): return lax.ppermute(x, ('seq', 'head'), pairs)  13.3 us
    pallas_call x14, Pallas kernels, run(): pl.pallas_call(kernel, out_shape=out_shape, in_specs=in_specs, out_specs=...  9.96 us
    ppermute x8, waiting for transfers between devices, hop(): return lax.ppermute(x, ('seq', 'head'), pairs)  9.23 us
    ppermute x4, waiting for transfers between devices, swap(): lax.ppermute(x, axis, [(j, j ^ bit) for j in range(lax.axis_size(axis))])  5.18 us
    ppermute x4, starting transfers between devices, swap(): lax.ppermute(x, axis, [(j, j ^ bit) for j in range(lax.axis_size(axis))])  2.17 us
  transfers between devices with their start and end apart: 12, of which 10 were waited for; matrix products, arithmetic and copies ran while one was open for 0% of the time, Pallas kernels for 10%

profile of v9, /device:TPU:0, one launch (start us, length us, event | category | flops | bytes accessed | tf_op | source)
XLA Modules:
  0.0 40.0 jit_solution(2473391487389618400)
XLA Ops:
  0.0 0.9 %shard_map.91.refs_3_.refs_0_ = bf16[4,1152]{1,0:T(4,128)(2,1)S(1)} custom-call(bf16[4,1024]{1,0:T(4,128)(2,1)} %t_in.1, s32[4,8]{1,0:T(4,128)} %r_in.1, s32[4,8]{1,0:T(4,128)} %g_in.1), custom_call_target="tpu_custom_call" | custom-call | flops 65536 | tf_op jit(solution)/shard_map/pallas_call | solution.py:29
  0.9 4.1 %collective-permute-start = (bf16[4,1152]{1,0:T(4,128)(2,1)S(1)}, bf16[4,1152]{1,0:T(4,128)(2,1)S(1)}, u32[]{:S(2)}, u32[]{:S(2)}) collective-permute-start(bf16[4,1152]{1,0:T(4,128)(2,1)S(1)} %shard_map.91.refs_3_.refs_0_), channel_id=1, source_target_pairs={{0,8},{4,12},{8,0},{12,4},{16,24},{20,28},{24,16},{28,20},{1,9},{5... | collective-permute-start | bytes 27656 | tf_op jit(solution)/shard_map/ppermute | solution.py:395
  5.0 0.0 copy-start
  5.0 0.0 copy-start.1
  5.0 1.2 %shard_map.92 = (f32[6,8,8,128]{3,2,1,0:T(8,128)S(1)}, f32[6,8,8,128]{3,2,1,0:T(8,128)S(1)}, f32[6,8,8,128]{3,2,1,0:T(8,128)S(1)}) custom-call(bf16[6,8,8]{2,1,0:T(8,128)(2,1)} %bitcast.5, bf16[6,8,8]{2,1,0:T(8,128)(2,1)} %bitcast.6, bf16[6,8,8]{2,1,0:T(8,128)(2,1)} %bitcast.7, bf16[4,1152]{1,0:T(4,128)(2,1)S(1)} %shard_map.91.refs_3_.refs_0_), custom_call_target="tpu_custom_call" | custom-call | flops 12582912000 | bytes 1048576 | tf_op jit(solution)/shard_map/pallas_call | solution.py:29
  6.2 0.4 %collective-permute-done.refs_1_ = bf16[4,1152]{1,0:T(4,128)(2,1)S(1)} collective-permute-done((bf16[4,1152]{1,0:T(4,128)(2,1)S(1)}, bf16[4,1152]{1,0:T(4,128)(2,1)S(1)}, u32[]{:S(2)}, u32[]{:S(2)}) %collective-permute-start) | collective-permute-done | bytes 9248 | tf_op jit(solution)/shard_map/ppermute | solution.py:395
  6.6 2.8 %collective-permute-start.3 = (bf16[8,1152]{1,0:T(8,128)(2,1)S(1)}, bf16[8,1152]{1,0:T(8,128)(2,1)S(1)}, u32[]{:S(2)}, u32[]{:S(2)}) collective-permute-start(bf16[8,1152]{1,0:T(8,128)(2,1)S(1)} %shard_map.93.refs_0_), channel_id=1, source_target_pairs={{0,20},{4,16},{8,28},{12,24},{16,4},{20,0},{24,12},{28,8},{1,21},{... | collective-permute-start | bytes 55304 | tf_op jit(solution)/shard_map/ppermute | solution.py:395
  9.5 0.5 %collective-permute-start.2 = (bf16[8,1152]{1,0:T(8,128)(2,1)S(1)}, bf16[8,1152]{1,0:T(8,128)(2,1)S(1)}, u32[]{:S(2)}, u32[]{:S(2)}) collective-permute-start(bf16[8,1152]{1,0:T(8,128)(2,1)S(1)} %shard_map.93.refs_0_), channel_id=1, source_target_pairs={{0,16},{4,20},{8,24},{12,28},{16,0},{20,4},{24,8},{28,12},{1,17},{... | collective-permute-start | bytes 55304 | tf_op jit(solution)/shard_map/ppermute | solution.py:395
  10.0 0.1 collective-permute-start.1
  10.1 1.2 %collective-permute-done.3.refs_3_ = bf16[8,1152]{1,0:T(8,128)(2,1)S(1)} collective-permute-done((bf16[8,1152]{1,0:T(8,128)(2,1)S(1)}, bf16[8,1152]{1,0:T(8,128)(2,1)S(1)}, u32[]{:S(2)}, u32[]{:S(2)}) %collective-permute-start.3) | collective-permute-done | bytes 18464 | tf_op jit(solution)/shard_map/ppermute | solution.py:395
  11.3 1.9 %collective-permute-done.2.refs_2_ = bf16[8,1152]{1,0:T(8,128)(2,1)S(1)} collective-permute-done((bf16[8,1152]{1,0:T(8,128)(2,1)S(1)}, bf16[8,1152]{1,0:T(8,128)(2,1)S(1)}, u32[]{:S(2)}, u32[]{:S(2)}) %collective-permute-start.2) | collective-permute-done | bytes 18464 | tf_op jit(solution)/shard_map/ppermute | solution.py:395
  13.2 0.5 %collective-permute-done.1.refs_1_ = bf16[8,1152]{1,0:T(8,128)(2,1)S(1)} collective-permute-done((bf16[8,1152]{1,0:T(8,128)(2,1)S(1)}, bf16[8,1152]{1,0:T(8,128)(2,1)S(1)}, u32[]{:S(2)}, u32[]{:S(2)}) %collective-permute-start.1) | collective-permute-done | bytes 18464 | tf_op jit(solution)/shard_map/ppermute | solution.py:395
  13.8 0.0 copy-done
  13.8 0.0 copy-done.1
  13.8 2.4 %shard_map.95 = (bf16[128,768]{1,0:T(8,128)(2,1)S(1)}, bf16[128,1024]{1,0:T(8,128)(2,1)S(1)}, bf16[32,128]{1,0:T(8,128)(2,1)S(1)}, f32[32,128]{1,0:T(8,128)S(1)}) custom-call(bf16[32,1152]{1,0:T(8,128)(2,1)S(1)} %shard_map.94.x_ref, bf16[8,1024,768]{2,1,0:T(8,128)(2,1)S(1)} %copy-done, bf16[8,1024,768]{2,1,0:T(8,128)(2,1)S(1)} %copy-done.1, ...), custom_call_target="tpu_custom_call" | custom-call | flops 65536 | bytes 65536 | tf_op jit(solution)/shard_map/pallas_call | solution.py:29
  16.2 0.0 collective-permute-start.4
  16.2 1.3 %shard_map.96.a_ref = f32[80,768]{1,0:T(8,128)S(1)} custom-call(bf16[128,1024]{1,0:T(8,128)(2,1)S(1)} %get-tuple-element.24.xs_ref, bf16[8,1024,768]{2,1,0:T(8,128)(2,1)S(1)} %copy-done, bf16[8,1024,768]{2,1,0:T(8,128)(2,1)S(1)} %copy-done.1, f32[6,8,8,128]{3,2,1,0:T(8,128)S(1)} %get-tuple-element.22.refs_2_.gs_ref, ...), custom_call_target="tpu_custom_call" | custom-call | flops 65536 | bytes 65536 | tf_op jit(solution)/shard_map/pallas_call | solution.py:29
  17.5 0.2 collective-permute-done.4.b_ref
  17.7 0.0 slice-start
  17.7 0.0 slice-start.1
  17.7 0.8 %shard_map.98.a_ref = f32[48,768]{1,0:T(8,128)S(1)} custom-call(bf16[128,1024]{1,0:T(8,128)(2,1)S(1)} %get-tuple-element.24.xs_ref, bf16[8,1024,768]{2,1,0:T(8,128)(2,1)S(1)} %copy-done, bf16[8,1024,768]{2,1,0:T(8,128)(2,1)S(1)} %copy-done.1, f32[6,8,8,128]{3,2,1,0:T(8,128)S(1)} %get-tuple-element.22.refs_2_.gs_ref, ...), custom_call_target="tpu_custom_call" | custom-call | flops 65536 | bytes 65536 | tf_op jit(solution)/shard_map/pallas_call | solution.py:29
  18.5 0.0 slice-start.2
  18.5 1.5 %collective-permute-start.5 = (bf16[80,768]{1,0:T(8,128)(2,1)S(1)}, bf16[80,768]{1,0:T(8,128)(2,1)S(1)}, u32[]{:S(2)}, u32[]{:S(2)}) collective-permute-start(bf16[80,768]{1,0:T(8,128)(2,1)S(1)} %get-tuple-element.27.rest_0_), channel_id=1, source_target_pairs={{0,2},{1,3},{2,0},{3,1},{4,6},{5,7},{6,4},{7,5},{8,10},{9,11},{10,... | collective-permute-start | bytes 368648 | tf_op jit(solution)/shard_map/ppermute | solution.py:384
  20.1 0.6 %collective-permute-start.6 = (bf16[48,768]{1,0:T(8,128)(2,1)S(1)}, bf16[48,768]{1,0:T(8,128)(2,1)S(1)}, u32[]{:S(2)}, u32[]{:S(2)}) collective-permute-start(bf16[48,768]{1,0:T(8,128)(2,1)S(1)} %get-tuple-element.29), channel_id=1, source_target_pairs={{0,2},{1,3},{2,0},{3,1},{4,6},{5,7},{6,4},{7,5},{8,10},{9,11},{10,... | collective-permute-start | bytes 221192 | tf_op jit(solution)/shard_map/ppermute | solution.py:384
  20.6 5.0 %collective-permute-done.6.refs_3_ = bf16[48,768]{1,0:T(8,128)(2,1)S(1)} collective-permute-done((bf16[48,768]{1,0:T(8,128)(2,1)S(1)}, bf16[48,768]{1,0:T(8,128)(2,1)S(1)}, u32[]{:S(2)}, u32[]{:S(2)}) %collective-permute-start.6) | collective-permute-done | bytes 73760 | tf_op jit(solution)/shard_map/ppermute | solution.py:384
  25.6 0.0 collective-permute-done.5.refs_1_
  25.6 0.1 shard_map.100.h_ref
  25.7 0.1 collective-permute-start.7
  25.8 0.0 slice-done
  25.8 0.0 slice-done.1
  25.8 0.0 slice-done.2
  25.8 1.3 %shard_map.101.rest_0_ = f32[32,1024]{1,0:T(8,128)S(1)} custom-call(bf16[128,384]{1,0:T(8,128)(2,1)S(1)} %shard_map.100.h_ref, bf16[32,128]{1,0:T(8,128)(2,1)S(1)} %get-tuple-element.30.sel_ref, f32[32,128]{1,0:T(8,128)S(1)} %get-tuple-element.31.wt_ref, bf16[8,768,1024]{2,1,0:T(8,128)(2,1)S(1)} %bitcast.4, f32[6,8,8,128]{3,2,1,0:T(8,128)S(1)} %get-tuple-element.32.ds_ref), custom_call_target="tpu_custom_call" | custom-call | flops 65536 | bytes 65536 | tf_op jit(solution)/shard_map/pallas_call | solution.py:29
  27.2 0.0 collective-permute-done.7.h_ref
  27.2 1.3 %shard_map.102 = (f32[8,1024]{1,0:T(8,128)S(1)}, bf16[8,1024]{1,0:T(8,128)(2,1)S(1)}, bf16[8,1024]{1,0:T(8,128)(2,1)S(1)}, bf16[8,1024]{1,0:T(8,128)(2,1)S(1)}) custom-call(bf16[128,384]{1,0:T(8,128)(2,1)S(1)} %collective-permute-done.7.h_ref, bf16[32,128]{1,0:T(8,128)(2,1)S(1)} %get-tuple-element.30.sel_ref, f32[32,128]{1,0:T(8,128)S(1)} %get-tuple-element.31.wt_ref, ...), custom_call_target="tpu_custom_call" | custom-call | flops 65536 | bytes 65536 | tf_op jit(solution)/shard_map/pallas_call | solution.py:29
  28.5 2.0 %collective-permute-start.8 = (bf16[8,1024]{1,0:T(8,128)(2,1)S(1)}, bf16[8,1024]{1,0:T(8,128)(2,1)S(1)}, u32[]{:S(2)}, u32[]{:S(2)}) collective-permute-start(bf16[8,1024]{1,0:T(8,128)(2,1)S(1)} %get-tuple-element.34), channel_id=1, source_target_pairs={{0,20},{4,16},{8,28},{12,24},{16,4},{20,0},{24,12},{28,8},{1,21},{... | collective-permute-start | bytes 49160 | tf_op jit(solution)/shard_map/ppermute | solution.py:395
  30.5 0.5 %collective-permute-start.9 = (bf16[8,1024]{1,0:T(8,128)(2,1)S(1)}, bf16[8,1024]{1,0:T(8,128)(2,1)S(1)}, u32[]{:S(2)}, u32[]{:S(2)}) collective-permute-start(bf16[8,1024]{1,0:T(8,128)(2,1)S(1)} %get-tuple-element.35), channel_id=1, source_target_pairs={{0,16},{4,20},{8,24},{12,28},{16,0},{20,4},{24,8},{28,12},{1,17},{... | collective-permute-start | bytes 49160 | tf_op jit(solution)/shard_map/ppermute | solution.py:395
  31.0 1.1 %collective-permute-start.10 = (bf16[8,1024]{1,0:T(8,128)(2,1)S(1)}, bf16[8,1024]{1,0:T(8,128)(2,1)S(1)}, u32[]{:S(2)}, u32[]{:S(2)}) collective-permute-start(bf16[8,1024]{1,0:T(8,128)(2,1)S(1)} %get-tuple-element.36), channel_id=1, source_target_pairs={{0,4},{4,0},{8,12},{12,8},{16,20},{20,16},{24,28},{28,24},{1,5},{5... | collective-permute-start | bytes 49160 | tf_op jit(solution)/shard_map/ppermute | solution.py:395
  32.1 1.1 %collective-permute-done.8.rest_0_ = bf16[8,1024]{1,0:T(8,128)(2,1)S(1)} collective-permute-done((bf16[8,1024]{1,0:T(8,128)(2,1)S(1)}, bf16[8,1024]{1,0:T(8,128)(2,1)S(1)}, u32[]{:S(2)}, u32[]{:S(2)}) %collective-permute-start.8) | collective-permute-done | bytes 16416 | tf_op jit(solution)/shard_map/ppermute | solution.py:395
  33.2 1.0 %collective-permute-done.9.rest_1_ = bf16[8,1024]{1,0:T(8,128)(2,1)S(1)} collective-permute-done((bf16[8,1024]{1,0:T(8,128)(2,1)S(1)}, bf16[8,1024]{1,0:T(8,128)(2,1)S(1)}, u32[]{:S(2)}, u32[]{:S(2)}) %collective-permute-start.9) | collective-permute-done | bytes 16416 | tf_op jit(solution)/shard_map/ppermute | solution.py:395
  34.2 0.5 %collective-permute-done.10.rest_2_ = bf16[8,1024]{1,0:T(8,128)(2,1)S(1)} collective-permute-done((bf16[8,1024]{1,0:T(8,128)(2,1)S(1)}, bf16[8,1024]{1,0:T(8,128)(2,1)S(1)}, u32[]{:S(2)}, u32[]{:S(2)}) %collective-permute-start.10) | collective-permute-done | bytes 16416 | tf_op jit(solution)/shard_map/ppermute | solution.py:395
  34.8 2.1 %collective-permute-start.11 = (bf16[4,1024]{1,0:T(4,128)(2,1)S(1)}, bf16[4,1024]{1,0:T(4,128)(2,1)S(1)}, u32[]{:S(2)}, u32[]{:S(2)}) collective-permute-start(bf16[4,1024]{1,0:T(4,128)(2,1)S(1)} %get-tuple-element.38), channel_id=1, source_target_pairs={{0,8},{4,12},{8,0},{12,4},{16,24},{20,28},{24,16},{28,20},{1,9},{5... | collective-permute-start | bytes 24584 | tf_op jit(solution)/shard_map/ppermute | solution.py:395
  36.9 2.5 %collective-permute-done.11.rest_0_ = bf16[4,1024]{1,0:T(4,128)(2,1)S(1)} collective-permute-done((bf16[4,1024]{1,0:T(4,128)(2,1)S(1)}, bf16[4,1024]{1,0:T(4,128)(2,1)S(1)}, u32[]{:S(2)}, u32[]{:S(2)}) %collective-permute-start.11) | collective-permute-done | bytes 8224 | tf_op jit(solution)/shard_map/ppermute | solution.py:395
  39.4 0.6 %shard_map.104 = bf16[4,1024]{1,0:T(4,128)(2,1)} custom-call(f32[4,1024]{1,0:T(4,128)S(1)} %get-tuple-element.37.a_ref, bf16[4,1024]{1,0:T(4,128)(2,1)S(1)} %collective-permute-done.11.rest_0_), custom_call_target="tpu_custom_call" | custom-call | tf_op jit(solution)/shard_map/pallas_call | solution.py:29
  (6 shorter events, 0.1 us)
Async XLA Ops:
  0.9 5.8 %collective-permute-start = (bf16[4,1152]{1,0:T(4,128)(2,1)S(1)}, bf16[4,1152]{1,0:T(4,128)(2,1)S(1)}, u32[]{:S(2)}, u32[]{:S(2)}) collective-permute-start(bf16[4,1152]{1,0:T(4,128)(2,1)S(1)} %shard_map.91.refs_3_.refs_0_), channel_id=1, source_target_pairs={{0,8},{4,12},{8,0},{12,4},{16,24},{20,28},{24,16},{28,20},{1,9},{5... | collective-permute-start | bytes 27656 | tf_op jit(solution)/shard_map/ppermute | solution.py:395
  5.0 8.8 %copy-start = (bf16[8,1024,768]{2,1,0:T(8,128)(2,1)S(1)}, bf16[8,1024,768]{2,1,0:T(8,128)(2,1)}, u32[]{:S(2)}) copy-start(bf16[8,1024,768]{2,1,0:T(8,128)(2,1)} %gw_ref.5) | copy-start | bytes 37748740
  5.0 8.8 %copy-start.1 = (bf16[8,1024,768]{2,1,0:T(8,128)(2,1)S(1)}, bf16[8,1024,768]{2,1,0:T(8,128)(2,1)}, u32[]{:S(2)}) copy-start(bf16[8,1024,768]{2,1,0:T(8,128)(2,1)} %uw_ref.5) | copy-start | bytes 37748740
  6.6 4.7 %collective-permute-start.3 = (bf16[8,1152]{1,0:T(8,128)(2,1)S(1)}, bf16[8,1152]{1,0:T(8,128)(2,1)S(1)}, u32[]{:S(2)}, u32[]{:S(2)}) collective-permute-start(bf16[8,1152]{1,0:T(8,128)(2,1)S(1)} %shard_map.93.refs_0_), channel_id=1, source_target_pairs={{0,20},{4,16},{8,28},{12,24},{16,4},{20,0},{24,12},{28,8},{1,21},{... | collective-permute-start | bytes 55304 | tf_op jit(solution)/shard_map/ppermute | solution.py:395
  9.5 3.8 %collective-permute-start.2 = (bf16[8,1152]{1,0:T(8,128)(2,1)S(1)}, bf16[8,1152]{1,0:T(8,128)(2,1)S(1)}, u32[]{:S(2)}, u32[]{:S(2)}) collective-permute-start(bf16[8,1152]{1,0:T(8,128)(2,1)S(1)} %shard_map.93.refs_0_), channel_id=1, source_target_pairs={{0,16},{4,20},{8,24},{12,28},{16,0},{20,4},{24,8},{28,12},{1,17},{... | collective-permute-start | bytes 55304 | tf_op jit(solution)/shard_map/ppermute | solution.py:395
  10.0 3.8 %collective-permute-start.1 = (bf16[8,1152]{1,0:T(8,128)(2,1)S(1)}, bf16[8,1152]{1,0:T(8,128)(2,1)S(1)}, u32[]{:S(2)}, u32[]{:S(2)}) collective-permute-start(bf16[8,1152]{1,0:T(8,128)(2,1)S(1)} %shard_map.93.refs_0_), channel_id=1, source_target_pairs={{0,4},{4,0},{8,12},{12,8},{16,20},{20,16},{24,28},{28,24},{1,5},{5... | collective-permute-start | bytes 55304 | tf_op jit(solution)/shard_map/ppermute | solution.py:395
  16.2 1.4 %collective-permute-start.4 = (bf16[128,768]{1,0:T(8,128)(2,1)S(1)}, bf16[128,768]{1,0:T(8,128)(2,1)S(1)}, u32[]{:S(2)}, u32[]{:S(2)}) collective-permute-start(bf16[128,768]{1,0:T(8,128)(2,1)S(1)} %get-tuple-element.25), channel_id=1, source_target_pairs={{0,1},{1,0},{2,3},{3,2},{4,5},{5,4},{6,7},{7,6},{8,9},{9,8},{10,11... | collective-permute-start | bytes 589832 | tf_op jit(solution)/shard_map/ppermute | solution.py:384
  17.7 8.1 %slice-start = ((s8[12582912]{0:T(1024)(128)(4,1)}), s8[4194304]{0:T(1024)(128)(4,1)S(1)}, s32[]{:S(2)}) async-start(s8[12582912]{0:T(1024)(128)(4,1)} %bitcast.3), calls=%async_computation | async-start | bytes 8388608
  17.7 8.1 %slice-start.1 = ((s8[12582912]{0:T(1024)(128)(4,1)}), s8[4194304]{0:T(1024)(128)(4,1)S(1)}, s32[]{:S(2)}) async-start(s8[12582912]{0:T(1024)(128)(4,1)} %bitcast.3), calls=%async_computation.1 | async-start | bytes 8388608
  18.5 7.3 %slice-start.2 = ((s8[12582912]{0:T(1024)(128)(4,1)}), s8[4194304]{0:T(1024)(128)(4,1)S(1)}, s32[]{:S(2)}) async-start(s8[12582912]{0:T(1024)(128)(4,1)} %bitcast.3), calls=%async_computation.2 | async-start | bytes 8388608
  18.5 7.1 %collective-permute-start.5 = (bf16[80,768]{1,0:T(8,128)(2,1)S(1)}, bf16[80,768]{1,0:T(8,128)(2,1)S(1)}, u32[]{:S(2)}, u32[]{:S(2)}) collective-permute-start(bf16[80,768]{1,0:T(8,128)(2,1)S(1)} %get-tuple-element.27.rest_0_), channel_id=1, source_target_pairs={{0,2},{1,3},{2,0},{3,1},{4,6},{5,7},{6,4},{7,5},{8,10},{9,11},{10,... | collective-permute-start | bytes 368648 | tf_op jit(solution)/shard_map/ppermute | solution.py:384
  20.1 5.6 %collective-permute-start.6 = (bf16[48,768]{1,0:T(8,128)(2,1)S(1)}, bf16[48,768]{1,0:T(8,128)(2,1)S(1)}, u32[]{:S(2)}, u32[]{:S(2)}) collective-permute-start(bf16[48,768]{1,0:T(8,128)(2,1)S(1)} %get-tuple-element.29), channel_id=1, source_target_pairs={{0,2},{1,3},{2,0},{3,1},{4,6},{5,7},{6,4},{7,5},{8,10},{9,11},{10,... | collective-permute-start | bytes 221192 | tf_op jit(solution)/shard_map/ppermute | solution.py:384
  25.7 1.5 %collective-permute-start.7 = (bf16[128,384]{1,0:T(8,128)(2,1)S(1)}, bf16[128,384]{1,0:T(8,128)(2,1)S(1)}, u32[]{:S(2)}, u32[]{:S(2)}) collective-permute-start(bf16[128,384]{1,0:T(8,128)(2,1)S(1)} %shard_map.100.h_ref), channel_id=1, source_target_pairs={{0,1},{1,0},{2,3},{3,2},{4,5},{5,4},{6,7},{7,6},{8,9},{9,8},{10,11... | collective-permute-start | bytes 294920 | tf_op jit(solution)/shard_map/ppermute | solution.py:384
  28.5 4.7 %collective-permute-start.8 = (bf16[8,1024]{1,0:T(8,128)(2,1)S(1)}, bf16[8,1024]{1,0:T(8,128)(2,1)S(1)}, u32[]{:S(2)}, u32[]{:S(2)}) collective-permute-start(bf16[8,1024]{1,0:T(8,128)(2,1)S(1)} %get-tuple-element.34), channel_id=1, source_target_pairs={{0,20},{4,16},{8,28},{12,24},{16,4},{20,0},{24,12},{28,8},{1,21},{... | collective-permute-start | bytes 49160 | tf_op jit(solution)/shard_map/ppermute | solution.py:395
  30.5 3.7 %collective-permute-start.9 = (bf16[8,1024]{1,0:T(8,128)(2,1)S(1)}, bf16[8,1024]{1,0:T(8,128)(2,1)S(1)}, u32[]{:S(2)}, u32[]{:S(2)}) collective-permute-start(bf16[8,1024]{1,0:T(8,128)(2,1)S(1)} %get-tuple-element.35), channel_id=1, source_target_pairs={{0,16},{4,20},{8,24},{12,28},{16,0},{20,4},{24,8},{28,12},{1,17},{... | collective-permute-start | bytes 49160 | tf_op jit(solution)/shard_map/ppermute | solution.py:395
  31.0 3.7 %collective-permute-start.10 = (bf16[8,1024]{1,0:T(8,128)(2,1)S(1)}, bf16[8,1024]{1,0:T(8,128)(2,1)S(1)}, u32[]{:S(2)}, u32[]{:S(2)}) collective-permute-start(bf16[8,1024]{1,0:T(8,128)(2,1)S(1)} %get-tuple-element.36), channel_id=1, source_target_pairs={{0,4},{4,0},{8,12},{12,8},{16,20},{20,16},{24,28},{28,24},{1,5},{5... | collective-permute-start | bytes 49160 | tf_op jit(solution)/shard_map/ppermute | solution.py:395
  34.8 4.6 %collective-permute-start.11 = (bf16[4,1024]{1,0:T(4,128)(2,1)S(1)}, bf16[4,1024]{1,0:T(4,128)(2,1)S(1)}, u32[]{:S(2)}, u32[]{:S(2)}) collective-permute-start(bf16[4,1024]{1,0:T(4,128)(2,1)S(1)} %get-tuple-element.38), channel_id=1, source_target_pairs={{0,8},{4,12},{8,0},{12,4},{16,24},{20,28},{24,16},{28,20},{1,9},{5... | collective-permute-start | bytes 24584 | tf_op jit(solution)/shard_map/ppermute | solution.py:395
